TPU v7x, 512 devices: a whole 4x8x8 slice. The times are simulated.
512 devices in a mesh: strike: 128 (over z, y, core), dip: 4 (over x).
Axes of the slice: x: 4, y: 8, z: 8, core: 2. Of those that a mesh axis runs over, the one named last changes fastest.
Arguments:
- slip: float32 [4096, 2048], P('strike', 'dip'), may hold values from 0 to 2
- rate: float32 [4096, 2048], P('strike', 'dip'), may hold values from 0 to 2
- prestress: float32 [4096, 2048], P('strike', 'dip'), may hold values from 0 to 1.5
- normal_stress: float32 [4096, 2048], P('strike', 'dip'), may hold values from 0.5 to 1.5
- history: float32 [8, 2, 4096, 2048], P(None, None, 'strike', 'dip'), may hold values from -6 to 6
- fric_flag: int32 [4096, 2048], P('strike', 'dip'), may hold values 0 or 1
- row_dest: int32 [4, 524288, 1], P('dip', 'strike'), may hold values from 0 to 127; in each aligned block of 4096 rows (0 to 4095, 4096 to 8191, ..., all dimensions but the last counted through in order) at most 64 rows name the same one
- row_node: int32 [4, 524288], P('dip', 'strike'), may hold values from 0 to 16383
- fe_traction: float32 [4, 524288], P('dip', 'strike'), may hold values from -8 to 8
- fe_count: int32 [4, 128], P('dip', 'strike'), may hold values from 1 to 4096, 393216 in all within a row
Outputs:
- new_rate: float32 [4096, 2048], P('strike', 'dip')
- stress: float32 [4096, 2048], P('strike', 'dip')
- fe_rate: float32 [4, 524288], P('dip', 'strike')
Inputs may be any that keep to these rules, and one draw needn't show every extreme that they name: `row_dest`: among the 4096 rows of one partition at most 64 name the same strike block, and some partition has exactly 64 rows naming one block. `fe_count`: the counts of one dip row sum to 3 * 4096 * P // 4 with P the number of strike devices; some partition is full.
All inputs are finite; a program needn't handle non-finite values. No bound on the sum of `fric_flag` on one device may be relied on, other than what follows from the above.
Results may differ from a plain program's by a relative error of at most 0.0003.
Values sent between devices are 32-bit elements; how exact they have to be, the bound alone decides.
No kernel may reach another device: no remote copies, remote signals or barrier semaphores. Data moves between devices by JAX's collectives and lax.ppermute only.
A program may use at most 64 MiB of HBM per device.

v0:
```python
import math

import jax
import jax.numpy as jnp
from jax import lax
from jax.sharding import PartitionSpec as P

full_turn = 2.0 * math.pi
highest = lax.Precision.HIGHEST
STEP_DT = 0.5
SHEAR_MOD = 1.0
DAMPING = 0.5
STATIC_FR = 0.6
DYNAMIC_FR = 0.4
KERNEL_DT = 0.5
KERNEL_DECAY = 0.15
KERNEL_FREQ = 0.9


def from_partner(x, axis, stride):
    return lax.ppermute(x, axis, [(i, i ^ 1 << stride) for i in range(lax.axis_size(axis))])


def reverse_bits(indices, levels):
    result = indices * 0
    for bit_index in range(levels):
        result = result + indices // 2**bit_index % 2 * 2 ** (levels - 1 - bit_index)
    return result


def wavenumber(freq_row, freq_col, length_row, length_col):
    signed_row = (
        jnp.where(freq_row >= length_row // 2, freq_row - length_row, freq_row).astype(jnp.float32)
        / length_row
    )
    signed_col = (
        jnp.where(freq_col >= length_col // 2, freq_col - length_col, freq_col).astype(jnp.float32)
        / length_col
    )
    return full_turn * jnp.sqrt(signed_row * signed_row + signed_col * signed_col)


def memory_sum(history, wavenum):
    real_part = jnp.zeros_like(wavenum)
    imag_part = jnp.zeros_like(wavenum)
    for lag_index in range(history.shape[0]):
        spacing = (lag_index + 1) * wavenum
        weight = KERNEL_DT * jnp.exp(-KERNEL_DECAY * spacing) * jnp.cos(KERNEL_FREQ * spacing)
        real_part = real_part + weight * history[lag_index, 0]
        imag_part = imag_part + weight * history[lag_index, 1]
    return (real_part, imag_part)


def twiddle_table(rows, cols, length, sign):
    product = (
        lax.broadcasted_iota(jnp.int32, (rows, cols), 0)
        * lax.broadcasted_iota(jnp.int32, (rows, cols), 1)
        % length
    )
    angle = product.astype(jnp.float32) * (full_turn / length)
    return (jnp.cos(angle), sign * jnp.sin(angle))


def mat_apply(real_part, imag_part, lookup, pattern):
    cos_part, sin_part = lookup

    def contract(left, right):
        return jnp.einsum(pattern, left, right, precision=highest)

    return (
        contract(real_part, cos_part) - contract(imag_part, sin_part),
        contract(real_part, sin_part) + contract(imag_part, cos_part),
    )


def spectral(real_part, imag_part, sign):
    length = real_part.shape[-1]
    if length <= 512:
        return mat_apply(
            real_part, imag_part, twiddle_table(length, length, length, sign), "...n,nk->...k"
        )
    inner_len = 2 ** ((length.bit_length() - 1) // 2)
    outer_len = length // inner_len
    new_shape = real_part.shape[:-1] + (outer_len, inner_len)
    real_part, imag_part = mat_apply(
        real_part.reshape(new_shape),
        imag_part.reshape(new_shape),
        twiddle_table(outer_len, outer_len, outer_len, sign),
        "...ab,ak->...bk",
    )
    cos_part, sin_part = twiddle_table(inner_len, outer_len, length, sign)
    real_part, imag_part = (
        real_part * cos_part - imag_part * sin_part,
        real_part * sin_part + imag_part * cos_part,
    )
    real_part, imag_part = mat_apply(
        real_part,
        imag_part,
        twiddle_table(inner_len, inner_len, inner_len, sign),
        "...bk,bl->...lk",
    )
    flat_shape = new_shape[:-2] + (length,)
    return (real_part.reshape(flat_shape), imag_part.reshape(flat_shape))


def rotate(stacked, cos_part, sin_part):
    return jnp.stack(
        [
            stacked[0] * cos_part - stacked[1] * sin_part,
            stacked[0] * sin_part + stacked[1] * cos_part,
        ]
    )


def rows_transform(stacked, sign):
    flipped = jnp.swapaxes(stacked, 1, 2)
    real_part, imag_part = spectral(flipped[0], flipped[1], sign)
    return jnp.swapaxes(jnp.stack([real_part, imag_part]), 1, 2)


def butterflies(stacked, strike_pos, levels, sign):
    order = list(range(levels - 1, -1, -1)) if sign < 0 else list(range(levels))
    for bit_index in order:
        half_span = 2**bit_index
        partner = from_partner(stacked, "strike", bit_index)
        is_upper = strike_pos // half_span % 2 == 1
        angle = (strike_pos % half_span).astype(jnp.float32) * (full_turn / (2 * half_span))
        cos_part = jnp.cos(angle)
        sin_part = sign * jnp.sin(angle)
        if sign < 0:
            low_out = stacked + partner
            high_out = rotate(partner - stacked, cos_part, sin_part)
        else:
            low_out = stacked + rotate(partner, cos_part, sin_part)
            high_out = partner - rotate(stacked, cos_part, sin_part)
        stacked = jnp.where(is_upper, high_out, low_out)
    return stacked


def dip_to_lines(stacked):
    return lax.all_to_all(stacked, "dip", split_axis=1, concat_axis=2, tiled=True)


def dip_to_blocks(stacked):
    return lax.all_to_all(stacked, "dip", split_axis=2, concat_axis=1, tiled=True)


def mode_twiddle(stacked, strike_pos, levels, total_strike, sign):
    rows_here = stacked.shape[1]
    product = (
        lax.broadcasted_iota(jnp.int32, (rows_here, 1), 0)
        * reverse_bits(strike_pos, levels)
        % total_strike
    )
    angle = product.astype(jnp.float32) * (full_turn / total_strike)
    return rotate(stacked, jnp.cos(angle), sign * jnp.sin(angle))


def strike_forward(stacked, strike_pos, levels, total_strike):
    result = butterflies(stacked, strike_pos, levels, -1.0)
    result = mode_twiddle(result, strike_pos, levels, total_strike, -1.0)
    result = rows_transform(result, -1.0)
    return result


def strike_inverse(stacked, strike_pos, levels, total_strike):
    result = rows_transform(stacked, 1.0)
    result = mode_twiddle(result, strike_pos, levels, total_strike, 1.0)
    result = butterflies(result, strike_pos, levels, 1.0)
    return result


def slot_ranks(target, blocks):
    count_rows = target.shape[0]
    block_len = math.gcd(count_rows, 512)
    onehot = (target[:, None] == lax.broadcasted_iota(jnp.int32, (1, blocks), 1)).astype(
        jnp.float32
    )
    onehot = onehot.reshape(count_rows // block_len, block_len, blocks)
    triangle = (
        lax.broadcasted_iota(jnp.int32, (block_len, block_len), 0)
        >= lax.broadcasted_iota(jnp.int32, (block_len, block_len), 1)
    ).astype(jnp.float32)

    def advance(running_count, row_block):
        running = jnp.dot(triangle, row_block, precision=highest) + running_count[None, :]
        return (
            running_count + jnp.sum(row_block, axis=0),
            jnp.sum(running * row_block, axis=1) - 1.0,
        )

    final_count, slot_rank = lax.scan(advance, jnp.zeros((blocks,), jnp.float32), onehot)
    return slot_rank.reshape(count_rows).astype(jnp.int32)


def body(
    slip,
    rate,
    prestress,
    normal_stress,
    history,
    fric_flag,
    row_dest,
    row_node,
    fe_traction,
    fe_count,
):
    blocks = lax.axis_size("strike")
    levels = blocks.bit_length() - 1
    strike_pos = lax.axis_index("strike")
    dip_pos = lax.axis_index("dip")
    rows_here = slip.shape[0]
    cols_here = slip.shape[1]
    total_strike = rows_here * blocks
    total_dip = cols_here * lax.axis_size("dip")
    scaling = 1.0 / math.sqrt(total_strike * total_dip)
    freq_row = reverse_bits(strike_pos, levels) + blocks * lax.broadcasted_iota(
        jnp.int32, (rows_here, cols_here), 0
    )
    freq_col = dip_pos * cols_here + lax.broadcasted_iota(jnp.int32, (rows_here, cols_here), 1)
    wavenum = wavenumber(freq_row, freq_col, total_strike, total_dip)
    memory_re, memory_im = memory_sum(history, wavenum)
    slip_new = slip + STEP_DT * rate
    gathered = dip_to_lines(slip_new[None])
    real_part, imag_part = spectral(gathered[0], jnp.zeros_like(gathered[0]), -1.0)
    stacked = dip_to_blocks(jnp.stack([real_part, imag_part]))
    spectrum = strike_forward(stacked, strike_pos, levels, total_strike) * scaling
    factor = -0.5 * SHEAR_MOD * wavenum
    func_spec = jnp.stack([factor * (spectrum[0] - memory_re), factor * (spectrum[1] - memory_im)])
    stacked = strike_inverse(func_spec, strike_pos, levels, total_strike)
    gathered = dip_to_lines(stacked)
    real_part, imag_part = spectral(gathered[0], gathered[1], 1.0)
    functional = dip_to_blocks(real_part[None])[0] * scaling
    target = row_dest[0, :, 0]
    node_ids = row_node[0]
    count_rows = target.shape[0]
    capacity = 2 * count_rows // blocks
    active = lax.broadcasted_iota(jnp.int32, (count_rows,), 0) < fe_count[0, 0]
    slot_ids = target * capacity + slot_ranks(target, blocks)
    payload = jnp.stack([jnp.where(active, fe_traction[0], 0.0), node_ids.astype(jnp.float32)])
    outbox = jnp.zeros((2, blocks * capacity), jnp.float32).at[:, slot_ids].set(payload)
    received = lax.all_to_all(
        outbox.reshape(2, blocks, capacity), "strike", split_axis=1, concat_axis=1, tiled=True
    )
    flat_nodes = received[1].reshape(-1).astype(jnp.int32)
    traction = (
        jnp.zeros((rows_here * cols_here,), jnp.float32).at[flat_nodes].add(received[0].reshape(-1))
    )
    traction = traction.reshape(rows_here, cols_here)
    stress = prestress + functional + traction
    strength = normal_stress * (STATIC_FR - (STATIC_FR - DYNAMIC_FR) * jnp.minimum(slip_new, 1.0))
    new_rate = jnp.where(fric_flag == 1, jnp.maximum(stress - strength, 0.0) / DAMPING, 0.0)
    sampled = new_rate.reshape(-1)[flat_nodes].reshape(blocks, capacity)
    returned = lax.all_to_all(sampled, "strike", split_axis=0, concat_axis=0, tiled=True)
    fe_rate = jnp.where(active, returned.reshape(-1)[slot_ids], 0.0)
    return (new_rate, stress, fe_rate[None])


def solution(mesh):
    in_specs = (
        P("strike", "dip"),
        P("strike", "dip"),
        P("strike", "dip"),
        P("strike", "dip"),
        P(None, None, "strike", "dip"),
        P("strike", "dip"),
        P("dip", "strike", None),
        P("dip", "strike"),
        P("dip", "strike"),
        P("dip", "strike"),
    )
    out_specs = (P("strike", "dip"), P("strike", "dip"), P("dip", "strike"))
    return jax.shard_map(body, mesh=mesh, in_specs=in_specs, out_specs=out_specs, check_vma=False)
```

profile of v0, /device:TPU:1, one launch (start us, length us, event | category | flops | bytes accessed | tf_op | source)
XLA Modules:
  0.0 384.9 jit_solution(9873735304663877453)
XLA Ops:
  2.2 4.8 %all-to-all-start = ((f32[1,32,512]{2,0,1:T(1,128)}), f32[1,32,512]{2,0,1:T(1,128)S(1)}, u32[]{:S(2)}, u32[]{:S(2)}) async-start(f32[1,32,512]{2,0,1:T(1,128)} %broadcast_in_dim.19), calls=%async_computation | async-start | bytes 131072 | tf_op jit(solution)/shard_map/all_to_all | solution.py:141
  9.2 8.8 %while.15 = (s32[]{:T(128)}, f32[128]{0:T(128)S(1)}, f32[8,512]{1,0:T(8,128)S(1)}, f32[8,512,128]{1,2,0:T(8,128)S(1)}, s32[]{:T(128)}, /*index=5*/s32[]{:T(128)}) while((s32[]{:T(128)}, f32[128]{0:T(128)S(1)}, f32[8,512]{1,0:T(8,128)S(1)}, f32[8,512,128]{1,2,0:T(8,128)S(1)}, s32[]{:T(128)}, /*index=5*/s32[]{:T(128)}) %tuple.66), condition=%wide.region_3.4_spmd.clone, body=%wide.region_0.3_spmd.clone.sunk | while | flops 403439744 | bytes 800863 | solution.py:192
  23.1 4.0 %reshape.1048 = f32[4,1,8192]{2,1,0:T(1,128)} reshape(f32[2048,2,8]{2,1,0:T(2,128)S(1)} %bitcast.240) | data formatting | bytes 262144
  27.0 4.2 %all-to-all-start.1 = ((f32[4,1,8192]{2,1,0:T(1,128)}), f32[4,1,8192]{2,1,0:T(1,128)S(1)}, u32[]{:S(2)}, u32[]{:S(2)}) async-start(f32[4,1,8192]{2,1,0:T(1,128)} %reshape.1048), calls=%async_computation.1 | async-start | bytes 262144 | tf_op jit(solution)/shard_map/all_to_all | solution.py:145
  32.0 4.1 %all-to-all-done.1 = f32[4,1,8192]{2,1,0:T(1,128)S(1)} async-done(((f32[4,1,8192]{2,1,0:T(1,128)}), f32[4,1,8192]{2,1,0:T(1,128)S(1)}, u32[]{:S(2)}, u32[]{:S(2)}) %all-to-all-start.1) | async-done | bytes 131104 | tf_op jit(solution)/shard_map/all_to_all | solution.py:145
  41.7 10.6 %collective-permute-start = (f32[2,32,512]{2,1,0:T(8,128)S(1)}, f32[2,32,512]{2,1,0:T(8,128)S(1)}, u32[]{:S(2)}, u32[]{:S(2)}) collective-permute-start(f32[2,32,512]{2,1,0:T(8,128)S(1)} %bitcast.244), channel_id=1, source_target_pairs={{0,256},{4,260},{8,264},{12,268},{16,272},{20,276},{24,280},{28,28... | collective-permute-start | bytes 393224 | tf_op jit(solution)/shard_map/ppermute | solution.py:21
  54.9 5.4 %collective-permute-start.1 = (f32[2,32,512]{2,1,0:T(8,128)S(1)}, f32[2,32,512]{2,1,0:T(8,128)S(1)}, u32[]{:S(2)}, u32[]{:S(2)}) collective-permute-start(f32[2,32,512]{2,1,0:T(8,128)S(1)} %maximum_select_fusion), channel_id=1, source_target_pairs={{0,128},{4,132},{8,136},{12,140},{16,144},{20,148},{24,152},{28,15... | collective-permute-start | bytes 393224 | tf_op jit(solution)/shard_map/ppermute | solution.py:21
  61.0 12.8 %scatter_custom_fusion = f32[2,8192]{0,1:T(8,128)} fusion(s32[4096]{0:T(1024)S(1)} %bitcast.256, f32[4096,2]{1,0:T(8,128)S(1)} %copy.54, f32[]{:T(128)} %constant.481.clone.1), kind=kCustom, calls=%fused_computation.18 | custom fusion | bytes 65540 | tf_op jit(solution)/shard_map/scatter | solution.py:241
  77.6 17.1 %all-to-all-start.4 = ((f32[128,1,128]{2,1,0:T(1,128)}), f32[128,1,128]{2,1,0:T(1,128)S(1)}, u32[]{:S(2)}, u32[]{:S(2)}) async-start(f32[128,1,128]{2,1,0:T(1,128)} %reshape.1046), calls=%async_computation.4 | async-start | bytes 131072 | tf_op jit(solution)/shard_map/all_to_all | solution.py:242
  98.6 3.7 collective-permute-done.2
  102.4 6.6 %collective-permute-start.3 = (f32[2,32,512]{2,1,0:T(8,128)S(1)}, f32[2,32,512]{2,1,0:T(8,128)S(1)}, u32[]{:S(2)}, u32[]{:S(2)}) collective-permute-start(f32[2,32,512]{2,1,0:T(8,128)S(1)} %maximum_select_fusion.2), channel_id=1, source_target_pairs={{0,32},{4,36},{8,40},{12,44},{16,48},{20,52},{24,56},{28,60},{32,0... | collective-permute-start | bytes 393224 | tf_op jit(solution)/shard_map/ppermute | solution.py:21
  112.2 7.9 %collective-permute-start.4 = (f32[2,32,512]{2,1,0:T(8,128)S(1)}, f32[2,32,512]{2,1,0:T(8,128)S(1)}, u32[]{:S(2)}, u32[]{:S(2)}) collective-permute-start(f32[2,32,512]{2,1,0:T(8,128)S(1)} %maximum_select_fusion.3), channel_id=1, source_target_pairs={{0,16},{4,20},{8,24},{12,28},{16,0},{20,4},{24,8},{28,12},{32,48},... | collective-permute-start | bytes 393224 | tf_op jit(solution)/shard_map/ppermute | solution.py:21
  129.1 4.6 %collective-permute-start.6 = (f32[2,32,512]{2,1,0:T(8,128)S(1)}, f32[2,32,512]{2,1,0:T(8,128)S(1)}, u32[]{:S(2)}, u32[]{:S(2)}) collective-permute-start(f32[2,32,512]{2,1,0:T(8,128)S(1)} %maximum_select_fusion.5), channel_id=1, source_target_pairs={{0,4},{4,0},{8,12},{12,8},{16,20},{20,16},{24,28},{28,24},{32,36},... | collective-permute-start | bytes 393224 | tf_op jit(solution)/shard_map/ppermute | solution.py:21
  144.6 3.6 collective-permute-start.8
  148.3 3.5 collective-permute-done.8
  151.9 5.0 %collective-permute-start.9 = (f32[2,32,512]{2,1,0:T(8,128)S(1)}, f32[2,32,512]{2,1,0:T(8,128)S(1)}, u32[]{:S(2)}, u32[]{:S(2)}) collective-permute-start(f32[2,32,512]{2,1,0:T(8,128)S(1)} %fusion.21), channel_id=1, source_target_pairs={{0,16},{4,20},{8,24},{12,28},{16,0},{20,4},{24,8},{28,12},{32,48},... | collective-permute-start | bytes 393224 | tf_op jit(solution)/shard_map/ppermute | solution.py:21
  156.9 5.8 %collective-permute-done.9 = f32[2,32,512]{2,1,0:T(8,128)S(1)} collective-permute-done((f32[2,32,512]{2,1,0:T(8,128)S(1)}, f32[2,32,512]{2,1,0:T(8,128)S(1)}, u32[]{:S(2)}, u32[]{:S(2)}) %collective-permute-start.9) | collective-permute-done | bytes 131104 | tf_op jit(solution)/shard_map/ppermute | solution.py:21
  162.8 7.2 %collective-permute-start.10 = (f32[2,32,512]{2,1,0:T(8,128)S(1)}, f32[2,32,512]{2,1,0:T(8,128)S(1)}, u32[]{:S(2)}, u32[]{:S(2)}) collective-permute-start(f32[2,32,512]{2,1,0:T(8,128)S(1)} %fusion.22), channel_id=1, source_target_pairs={{0,32},{4,36},{8,40},{12,44},{16,48},{20,52},{24,56},{28,60},{32,0... | collective-permute-start | bytes 393224 | tf_op jit(solution)/shard_map/ppermute | solution.py:21
  172.6 7.8 %collective-permute-start.11 = (f32[2,32,512]{2,1,0:T(8,128)S(1)}, f32[2,32,512]{2,1,0:T(8,128)S(1)}, u32[]{:S(2)}, u32[]{:S(2)}) collective-permute-start(f32[2,32,512]{2,1,0:T(8,128)S(1)} %fusion.23), channel_id=1, source_target_pairs={{0,64},{4,68},{8,72},{12,76},{16,80},{20,84},{24,88},{28,92},{32,9... | collective-permute-start | bytes 393224 | tf_op jit(solution)/shard_map/ppermute | solution.py:21
  182.7 4.9 %collective-permute-start.12 = (f32[2,32,512]{2,1,0:T(8,128)S(1)}, f32[2,32,512]{2,1,0:T(8,128)S(1)}, u32[]{:S(2)}, u32[]{:S(2)}) collective-permute-start(f32[2,32,512]{2,1,0:T(8,128)S(1)} %fusion.24), channel_id=1, source_target_pairs={{0,128},{4,132},{8,136},{12,140},{16,144},{20,148},{24,152},{28,15... | collective-permute-start | bytes 393224 | tf_op jit(solution)/shard_map/ppermute | solution.py:21
  187.6 4.3 %collective-permute-done.12 = f32[2,32,512]{2,1,0:T(8,128)S(1)} collective-permute-done((f32[2,32,512]{2,1,0:T(8,128)S(1)}, f32[2,32,512]{2,1,0:T(8,128)S(1)}, u32[]{:S(2)}, u32[]{:S(2)}) %collective-permute-start.12) | collective-permute-done | bytes 131104 | tf_op jit(solution)/shard_map/ppermute | solution.py:21
  192.0 6.0 %collective-permute-start.13 = (f32[2,32,512]{2,1,0:T(8,128)S(1)}, f32[2,32,512]{2,1,0:T(8,128)S(1)}, u32[]{:S(2)}, u32[]{:S(2)}) collective-permute-start(f32[2,32,512]{2,1,0:T(8,128)S(1)} %fusion.25), channel_id=1, source_target_pairs={{0,256},{4,260},{8,264},{12,268},{16,272},{20,276},{24,280},{28,28... | collective-permute-start | bytes 393224 | tf_op jit(solution)/shard_map/ppermute | solution.py:21
  198.0 5.0 %collective-permute-done.13 = f32[2,32,512]{2,1,0:T(8,128)S(1)} collective-permute-done((f32[2,32,512]{2,1,0:T(8,128)S(1)}, f32[2,32,512]{2,1,0:T(8,128)S(1)}, u32[]{:S(2)}, u32[]{:S(2)}) %collective-permute-start.13) | collective-permute-done | bytes 131104 | tf_op jit(solution)/shard_map/ppermute | solution.py:21
  203.9 3.5 all-to-all-start.2
  207.4 4.6 %all-to-all-done.2 = f32[2,32,512]{2,0,1:T(2,128)S(1)} async-done(((f32[2,32,512]{2,0,1:T(2,128)}), f32[2,32,512]{2,0,1:T(2,128)S(1)}, u32[]{:S(2)}, u32[]{:S(2)}) %all-to-all-start.2) | async-done | bytes 131104 | tf_op jit(solution)/shard_map/all_to_all | solution.py:141
  215.8 9.3 %reduce.19 = f32[2048,8]{1,0:T(8,128)S(1)} reduce(f32[2048,1,8]{2,1,0:T(1,128)S(1)} %bitcast.242, f32[]{:T(128)} %broadcast.1326), dimensions={1}, to_apply=%bitcast.218.reduce_sub_computation | reduce | bytes 131076
  226.3 3.3 all-to-all-start.3
  229.9 48.0 %scatter_custom_fusion.1 = f32[16384]{0:T(1024)S(1)} fusion(s32[8192]{0:T(1024)S(1)} %bitcast.255, f32[8192]{0:T(1024)S(1)} %reshape.1000, f32[]{:T(128)} %constant.481.clone.1), kind=kCustom, calls=%fused_computation.220 | custom fusion | flops 8192 | bytes 65540 | tf_op jit(solution)/shard_map/scatter-add | solution.py:247
  282.5 45.5 %gather_fusion = f32[8192]{0:T(1024)S(1)} fusion(f32[16384]{0:T(1024)S(1)} %bitcast.238, s32[8192]{0:T(1024)S(1)} %broadcast_clamp_fusion), kind=kCustom, calls=%fused_computation | custom fusion | bytes 98304 | tf_op jit(solution)/shard_map/gather | solution.py:253
  328.8 19.6 %all-to-all-start.5 = ((f32[128,1,64]{2,1,0:T(1,128)}), f32[128,1,64]{2,1,0:T(1,128)S(1)}, u32[]{:S(2)}, u32[]{:S(2)}) async-start(f32[128,1,64]{2,1,0:T(1,128)} %bitcast.55), calls=%async_computation.5 | async-start | bytes 131072 | tf_op jit(solution)/shard_map/all_to_all | solution.py:254
  348.4 11.4 %all-to-all-done.5 = f32[128,1,64]{2,1,0:T(1,128)S(1)} async-done(((f32[128,1,64]{2,1,0:T(1,128)}), f32[128,1,64]{2,1,0:T(1,128)S(1)}, u32[]{:S(2)}, u32[]{:S(2)}) %all-to-all-start.5) | async-done | bytes 32800 | tf_op jit(solution)/shard_map/all_to_all | solution.py:254
  361.3 23.0 %gather_fusion.1 = f32[4096]{0:T(1024)S(1)} fusion(f32[8192]{0:T(1024)S(1)} %reshape.971, s32[4096]{0:T(1024)S(1)} %broadcast_clamp_fusion.1), kind=kCustom, calls=%fused_computation.1 | custom fusion | bytes 49152 | tf_op jit(solution)/shard_map/gather | solution.py:255
  (207 shorter events, 73.7 us)
Async XLA Ops:
  2.2 16.0 %all-to-all-start = ((f32[1,32,512]{2,0,1:T(1,128)}), f32[1,32,512]{2,0,1:T(1,128)S(1)}, u32[]{:S(2)}, u32[]{:S(2)}) async-start(f32[1,32,512]{2,0,1:T(1,128)} %broadcast_in_dim.19), calls=%async_computation | async-start | bytes 131072 | tf_op jit(solution)/shard_map/all_to_all | solution.py:141
  22.0 9.3 %copy-start.2 = (s32[1,4096,1]{1,2,0:T(1,128)S(1)}, s32[1,4096,1]{1,2,0:T(1,128)}, u32[]{:S(2)}) copy-start(s32[1,4096,1]{1,2,0:T(1,128)} %param.18) | copy-start | bytes 49156
  27.0 9.1 %all-to-all-start.1 = ((f32[4,1,8192]{2,1,0:T(1,128)}), f32[4,1,8192]{2,1,0:T(1,128)S(1)}, u32[]{:S(2)}, u32[]{:S(2)}) async-start(f32[4,1,8192]{2,1,0:T(1,128)} %reshape.1048), calls=%async_computation.1 | async-start | bytes 262144 | tf_op jit(solution)/shard_map/all_to_all | solution.py:145
  37.6 14.7 %copy-start.6 = (f32[1,4096]{1,0:T(1,128)S(1)}, f32[1,4096]{1,0:T(1,128)}, u32[]{:S(2)}) copy-start(f32[1,4096]{1,0:T(1,128)} %param.20) | copy-start | bytes 49156
  37.6 15.0 %copy-start.7 = (s32[1,4096]{1,0:T(1,128)S(1)}, s32[1,4096]{1,0:T(1,128)}, u32[]{:S(2)}) copy-start(s32[1,4096]{1,0:T(1,128)} %param.19) | copy-start | bytes 49156
  41.7 13.1 %collective-permute-start = (f32[2,32,512]{2,1,0:T(8,128)S(1)}, f32[2,32,512]{2,1,0:T(8,128)S(1)}, u32[]{:S(2)}, u32[]{:S(2)}) collective-permute-start(f32[2,32,512]{2,1,0:T(8,128)S(1)} %bitcast.244), channel_id=1, source_target_pairs={{0,256},{4,260},{8,264},{12,268},{16,272},{20,276},{24,280},{28,28... | collective-permute-start | bytes 393224 | tf_op jit(solution)/shard_map/ppermute | solution.py:21
  54.9 40.1 %collective-permute-start.1 = (f32[2,32,512]{2,1,0:T(8,128)S(1)}, f32[2,32,512]{2,1,0:T(8,128)S(1)}, u32[]{:S(2)}, u32[]{:S(2)}) collective-permute-start(f32[2,32,512]{2,1,0:T(8,128)S(1)} %maximum_select_fusion), channel_id=1, source_target_pairs={{0,128},{4,132},{8,136},{12,140},{16,144},{20,148},{24,152},{28,15... | collective-permute-start | bytes 393224 | tf_op jit(solution)/shard_map/ppermute | solution.py:21
  77.6 47.8 %all-to-all-start.4 = ((f32[128,1,128]{2,1,0:T(1,128)}), f32[128,1,128]{2,1,0:T(1,128)S(1)}, u32[]{:S(2)}, u32[]{:S(2)}) async-start(f32[128,1,128]{2,1,0:T(1,128)} %reshape.1046), calls=%async_computation.4 | async-start | bytes 131072 | tf_op jit(solution)/shard_map/all_to_all | solution.py:242
  95.1 7.2 %collective-permute-start.2 = (f32[2,32,512]{2,1,0:T(8,128)S(1)}, f32[2,32,512]{2,1,0:T(8,128)S(1)}, u32[]{:S(2)}, u32[]{:S(2)}) collective-permute-start(f32[2,32,512]{2,1,0:T(8,128)S(1)} %maximum_select_fusion.1), channel_id=1, source_target_pairs={{0,64},{4,68},{8,72},{12,76},{16,80},{20,84},{24,88},{28,92},{32,9... | collective-permute-start | bytes 393224 | tf_op jit(solution)/shard_map/ppermute | solution.py:21
  102.4 9.7 %collective-permute-start.3 = (f32[2,32,512]{2,1,0:T(8,128)S(1)}, f32[2,32,512]{2,1,0:T(8,128)S(1)}, u32[]{:S(2)}, u32[]{:S(2)}) collective-permute-start(f32[2,32,512]{2,1,0:T(8,128)S(1)} %maximum_select_fusion.2), channel_id=1, source_target_pairs={{0,32},{4,36},{8,40},{12,44},{16,48},{20,52},{24,56},{28,60},{32,0... | collective-permute-start | bytes 393224 | tf_op jit(solution)/shard_map/ppermute | solution.py:21
  112.2 11.0 %collective-permute-start.4 = (f32[2,32,512]{2,1,0:T(8,128)S(1)}, f32[2,32,512]{2,1,0:T(8,128)S(1)}, u32[]{:S(2)}, u32[]{:S(2)}) collective-permute-start(f32[2,32,512]{2,1,0:T(8,128)S(1)} %maximum_select_fusion.3), channel_id=1, source_target_pairs={{0,16},{4,20},{8,24},{12,28},{16,0},{20,4},{24,8},{28,12},{32,48},... | collective-permute-start | bytes 393224 | tf_op jit(solution)/shard_map/ppermute | solution.py:21
  123.3 5.7 %collective-permute-start.5 = (f32[2,32,512]{2,1,0:T(8,128)S(1)}, f32[2,32,512]{2,1,0:T(8,128)S(1)}, u32[]{:S(2)}, u32[]{:S(2)}) collective-permute-start(f32[2,32,512]{2,1,0:T(8,128)S(1)} %maximum_select_fusion.4), channel_id=1, source_target_pairs={{0,8},{4,12},{8,0},{12,4},{16,24},{20,28},{24,16},{28,20},{32,40},... | collective-permute-start | bytes 393224 | tf_op jit(solution)/shard_map/ppermute | solution.py:21
  126.3 9.6 %copy-start = (f32[8,2,32,512]{3,2,1,0:T(8,128)S(1)}, f32[8,2,32,512]{3,2,1,0:T(8,128)}, u32[]{:S(2)}) copy-start(f32[8,2,32,512]{3,2,1,0:T(8,128)} %param.16) | copy-start | bytes 3145732
  129.1 5.6 %collective-permute-start.6 = (f32[2,32,512]{2,1,0:T(8,128)S(1)}, f32[2,32,512]{2,1,0:T(8,128)S(1)}, u32[]{:S(2)}, u32[]{:S(2)}) collective-permute-start(f32[2,32,512]{2,1,0:T(8,128)S(1)} %maximum_select_fusion.5), channel_id=1, source_target_pairs={{0,4},{4,0},{8,12},{12,8},{16,20},{20,16},{24,28},{28,24},{32,36},... | collective-permute-start | bytes 393224 | tf_op jit(solution)/shard_map/ppermute | solution.py:21
  141.3 3.2 collective-permute-start.7
  144.6 7.2 %collective-permute-start.8 = (f32[2,32,512]{2,1,0:T(8,128)S(1)}, f32[2,32,512]{2,1,0:T(8,128)S(1)}, u32[]{:S(2)}, u32[]{:S(2)}) collective-permute-start(f32[2,32,512]{2,1,0:T(8,128)S(1)} %fusion.20), channel_id=1, source_target_pairs={{0,8},{4,12},{8,0},{12,4},{16,24},{20,28},{24,16},{28,20},{32,40},... | collective-permute-start | bytes 393224 | tf_op jit(solution)/shard_map/ppermute | solution.py:21
  151.9 10.8 %collective-permute-start.9 = (f32[2,32,512]{2,1,0:T(8,128)S(1)}, f32[2,32,512]{2,1,0:T(8,128)S(1)}, u32[]{:S(2)}, u32[]{:S(2)}) collective-permute-start(f32[2,32,512]{2,1,0:T(8,128)S(1)} %fusion.21), channel_id=1, source_target_pairs={{0,16},{4,20},{8,24},{12,28},{16,0},{20,4},{24,8},{28,12},{32,48},... | collective-permute-start | bytes 393224 | tf_op jit(solution)/shard_map/ppermute | solution.py:21
  162.8 9.7 %collective-permute-start.10 = (f32[2,32,512]{2,1,0:T(8,128)S(1)}, f32[2,32,512]{2,1,0:T(8,128)S(1)}, u32[]{:S(2)}, u32[]{:S(2)}) collective-permute-start(f32[2,32,512]{2,1,0:T(8,128)S(1)} %fusion.22), channel_id=1, source_target_pairs={{0,32},{4,36},{8,40},{12,44},{16,48},{20,52},{24,56},{28,60},{32,0... | collective-permute-start | bytes 393224 | tf_op jit(solution)/shard_map/ppermute | solution.py:21
  172.6 10.1 %collective-permute-start.11 = (f32[2,32,512]{2,1,0:T(8,128)S(1)}, f32[2,32,512]{2,1,0:T(8,128)S(1)}, u32[]{:S(2)}, u32[]{:S(2)}) collective-permute-start(f32[2,32,512]{2,1,0:T(8,128)S(1)} %fusion.23), channel_id=1, source_target_pairs={{0,64},{4,68},{8,72},{12,76},{16,80},{20,84},{24,88},{28,92},{32,9... | collective-permute-start | bytes 393224 | tf_op jit(solution)/shard_map/ppermute | solution.py:21
  182.7 9.2 %collective-permute-start.12 = (f32[2,32,512]{2,1,0:T(8,128)S(1)}, f32[2,32,512]{2,1,0:T(8,128)S(1)}, u32[]{:S(2)}, u32[]{:S(2)}) collective-permute-start(f32[2,32,512]{2,1,0:T(8,128)S(1)} %fusion.24), channel_id=1, source_target_pairs={{0,128},{4,132},{8,136},{12,140},{16,144},{20,148},{24,152},{28,15... | collective-permute-start | bytes 393224 | tf_op jit(solution)/shard_map/ppermute | solution.py:21
  192.0 11.1 %collective-permute-start.13 = (f32[2,32,512]{2,1,0:T(8,128)S(1)}, f32[2,32,512]{2,1,0:T(8,128)S(1)}, u32[]{:S(2)}, u32[]{:S(2)}) collective-permute-start(f32[2,32,512]{2,1,0:T(8,128)S(1)} %fusion.25), channel_id=1, source_target_pairs={{0,256},{4,260},{8,264},{12,268},{16,272},{20,276},{24,280},{28,28... | collective-permute-start | bytes 393224 | tf_op jit(solution)/shard_map/ppermute | solution.py:21
  203.9 8.1 %all-to-all-start.2 = ((f32[2,32,512]{2,0,1:T(2,128)}), f32[2,32,512]{2,0,1:T(2,128)S(1)}, u32[]{:S(2)}, u32[]{:S(2)}) async-start(f32[2,32,512]{2,0,1:T(2,128)} %copy.46), calls=%async_computation.2 | async-start | bytes 262144 | tf_op jit(solution)/shard_map/all_to_all | solution.py:141
  226.3 51.6 %all-to-all-start.3 = ((f32[4,1,4096]{2,1,0:T(1,128)}), f32[4,1,4096]{2,1,0:T(1,128)S(1)}, u32[]{:S(2)}, u32[]{:S(2)}) async-start(f32[4,1,4096]{2,1,0:T(1,128)} %reshape.1050), calls=%async_computation.3 | async-start | bytes 131072 | tf_op jit(solution)/shard_map/all_to_all | solution.py:145
  278.7 3.1 copy-start.3
  278.7 3.1 copy-start.4
  278.7 3.1 copy-start.5
  282.5 45.6 %copy-start.1 = (f32[32,512]{1,0:T(8,128)}, f32[32,512]{1,0:T(8,128)S(1)}, u32[]{:S(2)}) copy-start(f32[32,512]{1,0:T(8,128)S(1)} %get-tuple-element.96) | copy-start | bytes 196612
  328.8 31.1 %all-to-all-start.5 = ((f32[128,1,64]{2,1,0:T(1,128)}), f32[128,1,64]{2,1,0:T(1,128)S(1)}, u32[]{:S(2)}, u32[]{:S(2)}) async-start(f32[128,1,64]{2,1,0:T(1,128)} %bitcast.55), calls=%async_computation.5 | async-start | bytes 131072 | tf_op jit(solution)/shard_map/all_to_all | solution.py:254
where the time goes:
time: 386 us; the launch traced here: 385 us
  starting transfers between devices  130 us (34%)
  local copies, waits for them, and re-layouts  104 us (27%)
  other arithmetic  72.7 us (19%)
  waiting for transfers between devices  59.2 us (15%)
  matrix products  15.6 us (4%)
    ppermute x14, starting transfers between devices, from_partner(): lax.ppermute(x, axis, [(i, i ^ 1 << stride) for i in range(lax.axis_size(...  77.1 us
    scatter-add x1, other arithmetic, body(): jnp.zeros((rows_here * cols_here,), jnp.float32).at[flat_nodes]  48 us
    gather x1, local copies, waits for them, and re-layouts, body(): sampled = new_rate.reshape(-1)[flat_nodes].reshape(blocks, capacity)  45.5 us
    ppermute x14, waiting for transfers between devices, from_partner(): lax.ppermute(x, axis, [(i, i ^ 1 << stride) for i in range(lax.axis_size(...  39 us
    gather x1, local copies, waits for them, and re-layouts, body(): fe_rate = jnp.where(active, returned.reshape(-1)[slot_ids], 0.0)  23 us
    all_to_all x1, starting transfers between devices, body(): lax.all_to_all(sampled, 'strike', split_axis=0, concat_axis=0, tiled=True)  19.6 us
    all_to_all x1, starting transfers between devices, body(): lax.all_to_all(outbox.reshape(2, blocks, capacity), 'strike', split_axis=...  17.1 us
    scatter x1, local copies, waits for them, and re-layouts, body(): jnp.zeros((2, blocks * capacity), jnp.float32).at[:, slot_ids].set(payload)  12.8 us
  transfers between devices with their start and end apart: 20, of which 16 were waited for; matrix products, arithmetic and copies ran while one was open for 20% of the time, Pallas kernels for 0%

commit v1 on v0

v1 whole, which is shorter than its diff:
```python
import math

import jax
import jax.numpy as jnp
import numpy as np
from jax import lax
from jax.experimental import pallas as pl
from jax.experimental.pallas import tpu as pltpu
from jax.sharding import Mesh
from jax.sharding import PartitionSpec as P

NS, ND = 4096, 2048
PS, QD = 128, 4
ROWS_DEV, COLS_DEV = NS // PS, ND // QD
GROUP = PS * QD
RATE_DT = 0.5
LEVELS = 7
CAP = 64
ROWS = 4096
CHUNK = 512
SCALE = 1.0 / math.sqrt(NS * ND)
bf16 = jnp.bfloat16
f32 = jnp.float32
NN = (((1,), (0,)), ((), ()))
NT = (((1,), (1,)), ((), ()))


def np_split(table):
    hi = table.astype(np.float32).astype(jnp.bfloat16)
    lo = (table - hi.astype(np.float64)).astype(np.float32).astype(jnp.bfloat16)
    return np.stack([hi, lo])


def np_rev(p):
    return sum(((p >> b) & 1) << (LEVELS - 1 - b) for b in range(LEVELS))


def dip_tables():
    i = np.arange(COLS_DEV)
    ang = 2 * np.pi * ((i[:, None] * i[None, :]) % ND) / ND
    return np.concatenate([np_split(np.cos(ang)), np_split(np.sin(ang))])


def strike_tables():
    p = np.arange(PS)
    k1 = np_rev(p)
    ang = 2 * np.pi * ((k1[:, None] * p[None, :]) % PS) / PS
    first = np.concatenate([np.cos(ang), -np.sin(ang)])
    r = np.arange(ROWS_DEV)
    tw = 2 * np.pi * (k1[:, None] * r[None, :]) / NS
    twiddle = np.stack([np.tile(np.cos(tw), (1, 4)), np.tile(np.sin(tw), (1, 4))]).astype(np.float32)
    small = 2 * np.pi * ((r[:, None] * r[None, :]) % ROWS_DEV) / ROWS_DEV
    cb = np.kron(np.eye(4), np.cos(small))
    sb = np.kron(np.eye(4), np.sin(small))
    second = np.block([[cb, -sb], [sb, cb]])
    second_inv = np.block([[cb, sb], [-sb, cb]])
    return np_split(first), np_split(first.T), twiddle, np_split(second), np_split(second_inv)


def memory_tables():
    out = np.zeros((2, 2 * PS, 2 * PS), np.float32)
    eye = np.eye(ROWS_DEV)
    for special in range(2):
        home = {0: 0, 1: 1, 2: 3, 3: 2} if special else {j: j for j in range(4)}
        partner = {0: 0, 3: 3, 1: 2, 2: 1} if special else {0: 3, 3: 0, 1: 2, 2: 1}
        for slot in range(4):
            own, other = home[slot], home[partner[slot]]
            for slab, part, w_re, w_im in ((own, 0, 0.5, 0.5), (own, 1, -0.5, 0.5), (other, 0, 0.5, -0.5), (other, 1, 0.5, 0.5)):
                rows = slice(64 * slab + 32 * part, 64 * slab + 32 * part + 32)
                out[special, rows, 32 * slot : 32 * slot + 32] += w_re * eye
                out[special, rows, PS + 32 * slot : PS + 32 * slot + 32] += w_im * eye
    return out.astype(jnp.bfloat16)


def dot(a, b, dims=NN):
    return lax.dot_general(a, b, dims, preferred_element_type=f32)


def split(x):
    hi = x.astype(bf16)
    return hi, (x - hi.astype(f32)).astype(bf16)


def dot_data_table(x, t_hi, t_lo):
    hi, lo = split(x)
    return dot(hi, t_hi) + (dot(lo, t_hi) + dot(hi, t_lo))


def dot_table_data(t_hi, t_lo, x):
    hi, lo = split(x)
    return dot(t_hi, hi) + (dot(t_hi, lo) + dot(t_lo, hi))


def iota(shape, dim):
    return lax.broadcasted_iota(jnp.int32, shape, dim)


def rev_bits(p):
    out = 0
    for b in range(LEVELS):
        out = out + (((p >> b) & 1) << (LEVELS - 1 - b))
    return out


def quarter(q):
    turn = (q * iota((1, COLS_DEV), 1)) & 3
    cm = jnp.where(turn == 0, 1.0, jnp.where(turn == 2, -1.0, 0.0))
    sm = jnp.where(turn == 1, 1.0, jnp.where(turn == 3, -1.0, 0.0))
    return cm, sm


def signed(freq, length):
    return jnp.where(freq >= length // 2, freq - length, freq).astype(f32) * (1.0 / length)


def slip_part(slip, rate, tables, q):
    x = slip + RATE_DT * rate
    phase = iota((ROWS_DEV, COLS_DEV), 1) & 3
    x4 = jnp.concatenate([jnp.where(phase == b, x, 0.0) for b in range(4)], axis=0)
    c = dot_data_table(x4, tables[0], tables[1])
    s = dot_data_table(x4, tables[2], tables[3])
    cm, sm = quarter(q)
    c, s = cm * c - sm * s, sm * c + cm * s
    cs = [c[32 * b : 32 * b + 32] for b in range(4)]
    ss = [s[32 * b : 32 * b + 32] for b in range(4)]
    c_even, c_odd = cs[0] + cs[2], cs[1] + cs[3]
    s_sum = (ss[0] + ss[2]) + (ss[1] + ss[3])
    h_a = (c_even + c_odd) + s_sum
    first = iota((ROWS_DEV, COLS_DEV), 1) == 0
    h_d = (c_even + jnp.where(first, -c_odd, c_odd)) - s_sum
    even = cs[0] - cs[2] + ss[3] - ss[1]
    odd = ss[0] - ss[2] + cs[1] - cs[3]
    return jnp.concatenate([h_a, even + odd, even - odd, h_d], axis=0).T


def memory_part(history, p, q):
    ks = rev_bits(p) + PS * iota((ROWS_DEV, COLS_DEV), 0)
    kd = q * COLS_DEV + iota((ROWS_DEV, COLS_DEV), 1)
    fs, fd = signed(ks, NS), signed(kd, ND)
    wave = (2.0 * math.pi) * jnp.sqrt(fs * fs + fd * fd)
    grow = jnp.exp(-0.15 * wave)
    ang = 0.9 * wave
    z_re, z_im = grow * jnp.cos(ang), grow * jnp.sin(ang)
    w_re, w_im = 0.5 * z_re, 0.5 * z_im
    m_re, m_im = w_re * history(0, 0), w_re * history(0, 1)
    for lag in range(1, 8):
        w_re, w_im = w_re * z_re - w_im * z_im, w_re * z_im + w_im * z_re
        m_re = m_re + w_re * history(lag, 0)
        m_im = m_im + w_re * history(lag, 1)
    both = jnp.concatenate([m_re, m_im], axis=0)
    odd = (q & 1) == 1
    both = jnp.concatenate([jnp.where(odd, 0.0, both), jnp.where(odd, both, 0.0)], axis=0)
    row = iota((COLS_DEV, COLS_DEV), 0)
    from_col = jnp.where(q < 2, row, (COLS_DEV - row) & (COLS_DEV - 1))
    perm = (iota((COLS_DEV, COLS_DEV), 1) == from_col).astype(f32).astype(bf16)
    hi, lo = split(both)
    return dot(perm, hi, NT) + dot(perm, lo, NT)


def send_kernel(idx, slip, rate, history, tables, out):
    p, q = idx[0], idx[1]
    out[pl.ds(0, GROUP, stride=2), :] = slip_part(slip[...], rate[...], [tables[i] for i in range(4)], q)
    out[pl.ds(1, GROUP, stride=2), :] = memory_part(lambda lag, part: history[lag, part], p, q)


def strike_part(slip_recv, mem_recv, first, first_t, twiddle, second, second_inv, mem_table, ell):
    n = PS
    u = (slip_recv[0:n] + slip_recv[n : 2 * n]) + (slip_recv[2 * n : 3 * n] + slip_recv[3 * n :])
    mem = jnp.concatenate([mem_recv[0:n] + mem_recv[n : 2 * n], mem_recv[2 * n : 3 * n] + mem_recv[3 * n :]], axis=1)
    m_hi, m_lo = split(mem)
    w = dot(m_hi, mem_table) + dot(m_lo, mem_table)
    a = dot_table_data(first[0], first[1], u)
    a_re, a_im = a[:n], a[n:]
    tc, ts = twiddle[0], twiddle[1]
    b = jnp.concatenate([a_re * tc + a_im * ts, a_im * tc - a_re * ts], axis=1)
    spec = dot_data_table(b, second[0], second[1])
    lane = iota((n, n), 1)
    fs = signed(rev_bits(iota((n, n), 0)) + PS * (lane & 31), NS)
    slot = lane >> 5
    kd = jnp.where((slot == 1) | (slot == 2), COLS_DEV + ell, ell)
    kd = jnp.where((slot == 3) & (ell == 0), 2 * COLS_DEV, kd)
    fd = kd.astype(f32) * (1.0 / ND)
    wave = (2.0 * math.pi) * jnp.sqrt(fs * fs + fd * fd)
    factor = (-0.5 * SCALE) * wave
    factor = jnp.concatenate([factor, factor], axis=1)
    g = factor * (SCALE * spec - w)
    b = dot_data_table(g, second_inv[0], second_inv[1])
    b_re, b_im = b[:, :n], b[:, n:]
    b = jnp.concatenate([b_re * tc - b_im * ts, b_re * ts + b_im * tc], axis=0)
    return dot_table_data(first_t[0], first_t[1], b)


def strike_kernel(idx, recv, outbox, first, first_t, twiddle, second, second_inv, mem_table, out):
    p, q = idx[0], idx[1]
    ell = PS * q + p
    special = jnp.where(ell == 0, 1, 0)
    t = strike_part(
        recv[pl.ds(0, GROUP, stride=2), :],
        recv[pl.ds(1, GROUP, stride=2), :],
        first,
        first_t,
        twiddle,
        second,
        second_inv,
        mem_table[special],
        ell,
    )
    box = outbox[...]
    for qd in range(QD):
        out[pl.ds(2 * PS * qd, PS, stride=2), :] = t
        out[pl.ds(2 * PS * qd + 1, PS, stride=2), :] = jnp.where(q == qd, box, 0.0)


def route_part(dest, node, value, count):
    dest = [dest[:, CHUNK * i : CHUNK * (i + 1)] for i in range(ROWS // CHUNK)]
    upto = (iota((CHUNK, CHUNK), 0) <= iota((CHUNK, CHUNK), 1)).astype(f32).astype(bf16)
    carry = jnp.zeros((PS, 1), f32)
    box = jnp.zeros((PS, 2 * CAP), f32)
    ranks = []
    for i in range(ROWS // CHUNK):
        cut = slice(CHUNK * i, CHUNK * (i + 1))
        named = iota((PS, CHUNK), 0) == dest[i]
        onehot = named.astype(f32).astype(bf16)
        upto_here = dot(onehot, upto) + carry
        rank = jnp.sum(jnp.where(named, upto_here, 0.0), axis=0, keepdims=True).astype(jnp.int32) - 1
        carry = upto_here[:, CHUNK - 1 : CHUNK]
        ranks.append(rank)
        live = (CHUNK * i + iota((1, CHUNK), 1)) < count
        v = jnp.where(live, value[:, cut], 0.0)
        v_hi = v.astype(bf16).astype(f32)
        v_lo = v - v_hi
        at = node[:, cut]
        n_hi = ((((at >> 7) & 3) << 5) + (at >> 9)) << 7
        n_lo = at & 127
        here = iota((CAP, CHUNK), 0) == rank
        part_1 = jnp.concatenate([jnp.where(here, v_hi, 0.0), jnp.where(here, n_hi.astype(f32), 0.0)], axis=0)
        part_2 = jnp.concatenate([jnp.where(here, v_lo, 0.0), jnp.where(here, n_lo.astype(f32), 0.0)], axis=0)
        box = box + (dot(onehot, part_1.astype(bf16), NT) + dot(onehot, part_2.astype(bf16), NT))
    return box, jnp.concatenate(ranks, axis=1)


def route_kernel(count, dest, node, value, out, rank):
    out[...], rank[...] = route_part(dest[...], node[...], value[...], count[0, 0])


def functional_part(recv, tables, q):
    t = recv.T
    a, b, c, d = [t[32 * j : 32 * j + 32] for j in range(4)]
    s1, d1, s2, d2 = a + d, a - d, b + c, b - c
    fix = jnp.where(iota((ROWS_DEV, COLS_DEV), 1) == 0, 2.0 * d, 0.0)
    even = jnp.concatenate([s1 + s2, s1 + d2 - fix, s1 - s2, s1 - d2 - fix], axis=0)
    odd = jnp.concatenate([d1 + d2, d1 - s2, d1 - d2, d1 + s2], axis=0)
    cm, sm = quarter(q)
    even, odd = cm * even + sm * odd, cm * odd - sm * even
    f = dot_data_table(even, tables[0], tables[1]) + dot_data_table(odd, tables[2], tables[3])
    phase = iota((ROWS_DEV, COLS_DEV), 1) & 3
    f = [jnp.where(phase == i, f[32 * i : 32 * i + 32], 0.0) for i in range(4)]
    return (f[0] + f[1]) + (f[2] + f[3])


def unpack_rows(fe, roll):
    top, bot = fe[0:CAP], fe[CAP:PS]
    left = iota((CAP, PS), 1) < CAP
    value = jnp.where(left, top, roll(bot))
    node = jnp.where(left, roll(top), bot).astype(jnp.int32)
    return value, node >> 7, node & 127


def lanes_of(x, group):
    return jnp.concatenate([x[4 * group + i : 4 * group + i + 1] for i in range(4)], axis=1)


def column_onehot(lo):
    return (iota((PS, CHUNK), 0) == lo).astype(f32).astype(bf16)


def traction_step(value, hi, onehot):
    named = iota((PS, CHUNK), 0) == hi
    v_hi = value.astype(bf16).astype(f32)
    rows = jnp.concatenate([jnp.where(named, v_hi, 0.0), jnp.where(named, value - v_hi, 0.0)], axis=0).astype(bf16)
    return dot(rows, onehot, NT)


def sample_step(rate_parts, hi, onehot):
    got = dot(rate_parts, jnp.concatenate([onehot, onehot], axis=0))
    return jnp.sum(jnp.where(iota((PS, CHUNK), 0) == hi, got, 0.0), axis=0, keepdims=True)


def owner_kernel(idx, recv, slip, rate, prestress, normal, flag, tables, new_rate, stress, sampled, onehots):
    q = idx[1]
    roll = lambda x: pltpu.roll(x, CAP, 1)
    fe = recv[pl.ds(1, GROUP, stride=2), :]
    fe = (fe[0:PS] + fe[PS : 2 * PS]) + (fe[2 * PS : 3 * PS] + fe[3 * PS :])
    value, hi, lo = unpack_rows(fe, roll)
    acc = jnp.zeros((2 * PS, PS), f32)
    groups = CAP // 4
    for g in range(groups):
        onehot = column_onehot(lanes_of(lo, g))
        onehots[g] = onehot
        acc = acc + traction_step(lanes_of(value, g), lanes_of(hi, g), onehot)
    acc = acc[:PS] + acc[PS:]
    traction = jnp.concatenate([acc[32 * i : 32 * i + 32] for i in range(4)], axis=1)
    f = functional_part(recv[pl.ds(0, GROUP, stride=2), :], [tables[i] for i in range(4)], q)
    slip_new = slip[...] + RATE_DT * rate[...]
    total = prestress[...] + f + traction
    strength = normal[...] * (0.6 - (0.6 - 0.4) * jnp.minimum(slip_new, 1.0))
    fresh = jnp.where(flag[...] == 1, jnp.maximum(total - strength, 0.0) * 2.0, 0.0)
    stress[...] = total
    new_rate[...] = fresh
    stacked = jnp.concatenate([fresh[:, PS * i : PS * (i + 1)] for i in range(4)], axis=0)
    parts = jnp.concatenate(split(stacked), axis=1)
    for g in range(groups):
        got = sample_step(parts, lanes_of(hi, g), onehots[g])
        for i in range(4):
            sampled[4 * g + i : 4 * g + i + 1, :] = got[:, PS * i : PS * (i + 1)]
    sampled[CAP:PS, :] = roll(sampled[0:CAP, :])


def return_part(got, dest, rank, count):
    parts = jnp.concatenate(split(got.T[:CAP]), axis=1)
    out = []
    for i in range(ROWS // CHUNK):
        cut = slice(CHUNK * i, CHUNK * (i + 1))
        onehot = (iota((PS, CHUNK), 0) == dest[:, cut]).astype(f32).astype(bf16)
        here = dot(parts, jnp.concatenate([onehot, onehot], axis=0))
        here = jnp.sum(jnp.where(iota((CAP, CHUNK), 0) == rank[:, cut], here, 0.0), axis=0, keepdims=True)
        live = (CHUNK * i + iota((1, CHUNK), 1)) < count
        out.append(jnp.where(live, here, 0.0))
    return jnp.concatenate(out, axis=1)


def return_kernel(count, got, dest, rank, out):
    out[...] = return_part(got[...], dest[...], rank[...], count[0, 0])


STRIKE = ("z", "y", "c")
ALL = ("dip", "z", "y", "c")


def call(kernel, out_shape, smem, vmem, scratch=(), name=None):
    specs = [pl.BlockSpec(memory_space=pltpu.SMEM)] * smem + [pl.BlockSpec(memory_space=pltpu.VMEM)] * vmem
    outs = jax.tree.map(lambda _: pl.BlockSpec(memory_space=pltpu.VMEM), out_shape)
    return pl.pallas_call(kernel, out_shape=out_shape, in_specs=specs, out_specs=outs, scratch_shapes=scratch, name=name)


def sds(shape, dtype=f32):
    return jax.ShapeDtypeStruct(shape, dtype)


def body(slip, rate, prestress, normal_stress, history, fric_flag, row_dest, row_node, fe_traction, fe_count):
    p = lax.axis_index(STRIKE).astype(jnp.int32)
    q = lax.axis_index("dip").astype(jnp.int32)
    idx = jnp.stack([p, q])
    tables = jnp.asarray(dip_tables())
    first, first_t, twiddle, second, second_inv = [jnp.asarray(t) for t in strike_tables()]
    mem_table = jnp.asarray(memory_tables())

    sent = call(send_kernel, sds((2 * GROUP, PS)), 1, 4, name="send")(idx, slip, rate, history, tables)
    recv = lax.all_to_all(sent.reshape(GROUP, 2, PS), ALL, 0, 0, tiled=True).reshape(2 * GROUP, PS)
    dest = row_dest.reshape(1, ROWS)
    box, rank = call(route_kernel, (sds((PS, PS)), sds((1, ROWS), jnp.int32)), 1, 3, name="route")(
        fe_count, dest, row_node, fe_traction
    )
    sent = call(strike_kernel, sds((2 * GROUP, PS)), 1, 8, name="strike")(
        idx, recv, box, first, first_t, twiddle, second, second_inv, mem_table
    )
    recv = lax.all_to_all(sent.reshape(GROUP, 2, PS), ALL, 0, 0, tiled=True).reshape(2 * GROUP, PS)
    new_rate, stress, sampled = call(
        owner_kernel,
        (sds((ROWS_DEV, COLS_DEV)), sds((ROWS_DEV, COLS_DEV)), sds((PS, PS))),
        1,
        7,
        scratch=[pltpu.VMEM((CAP // 4, PS, CHUNK), bf16)],
        name="owner",
    )(idx, recv, slip, rate, prestress, normal_stress, fric_flag, tables)
    got = lax.all_to_all(sampled.reshape(PS, 1, PS), STRIKE, 0, 0, tiled=True).reshape(PS, PS)
    fe_rate = call(return_kernel, sds((1, ROWS)), 1, 3, name="back")(fe_count, got, dest, rank)
    return new_rate, stress, fe_rate


def solution(mesh):
    fine = Mesh(mesh.devices.reshape(8, 8, 2, 4), ("z", "y", "c", "dip"))
    field = P(STRIKE, "dip")
    rows = P("dip", STRIKE)
    in_specs = (field, field, field, field, P(None, None, STRIKE, "dip"), field, P("dip", STRIKE, None), rows, rows, rows)
    return jax.shard_map(body, mesh=fine, in_specs=in_specs, out_specs=(field, field, rows), check_vma=False)
```

time: 386 us -> 113 us (0.29)
  starting transfers between devices: 130 us -> 22.1 us
  local copies, waits for them, and re-layouts: 104 us -> 0.8 us
  other arithmetic: 72.7 us -> 0.65 us
  blocking collectives: 0 us -> 51.8 us
  waiting for transfers between devices: 59.2 us -> 18.4 us
  Pallas kernels: 0 us -> 17.7 us
  matrix products: 15.6 us -> 0 us
    ppermute x14 -> x0, starting transfers between devices: 77.1 us -> none  [from_partner(): lax.ppermute(x, axis, [(i, i ^ 1 << stride) for i in range(lax.axis_size(...]
    gather x2 -> x0, local copies, waits for them, and re-layouts: 68.6 us -> none  [the longest x1 45.5 us: body(): sampled = new_rate.reshape(-1)[flat_nodes].reshape(blocks, capacity)]
    all_to_all x0 -> x2, blocking collectives: none -> 51.8 us  [the longest x1 33.1 us: body(): lax.all_to_all(sent.reshape(GROUP, 2, PS), ALL, 0, 0, tiled=True)]
    scatter-add x1 -> x0, other arithmetic: 48 us -> none  [body(): jnp.zeros((rows_here * cols_here,), jnp.float32).at[flat_nodes]]
    ppermute x14 -> x0, waiting for transfers between devices: 39 us -> none  [from_partner(): lax.ppermute(x, axis, [(i, i ^ 1 << stride) for i in range(lax.axis_size(...]
    all_to_all x6 -> x1, starting transfers between devices: 52.6 us -> 22.1 us  [body(): lax.all_to_all(sent.reshape(GROUP, 2, PS), ALL, 0, 0, tiled=True)]
    pallas_call x0 -> x5, Pallas kernels: none -> 17.7 us  [the longest x1 5.51 us: body(): call(owner_kernel, (sds((ROWS_DEV, COLS_DEV)), sds((ROWS_DEV, COLS_DEV)),...]
    dot_general x30 -> x0, matrix products: 15.6 us -> none  [the longest x22 8.64 us: contract(): return jnp.einsum(pattern, left, right, precision=highest)]
  transfers between devices with their start and end apart: 20 -> 1, of which waited for: 16 -> 1; matrix products, arithmetic and copies ran while one was open for 20% -> 0% of each run, Pallas kernels for 0% -> 3%
where the time goes in v1:
time: 113 us
  blocking collectives  51.8 us (46%)
  starting transfers between devices  22.1 us (20%)
  waiting for transfers between devices  18.4 us (16%)
  Pallas kernels  17.7 us (16%)
  between operations  1.3 us (1%)
    all_to_all x1, blocking collectives, body(): lax.all_to_all(sent.reshape(GROUP, 2, PS), ALL, 0, 0, tiled=True)  33.1 us
    all_to_all x1, starting transfers between devices, body(): lax.all_to_all(sent.reshape(GROUP, 2, PS), ALL, 0, 0, tiled=True)  22.1 us
    all_to_all x1, blocking collectives, body(): lax.all_to_all(sampled.reshape(PS, 1, PS), STRIKE, 0, 0, tiled=True)  18.7 us
    all_to_all x1, waiting for transfers between devices, body(): lax.all_to_all(sent.reshape(GROUP, 2, PS), ALL, 0, 0, tiled=True)  18.4 us
    pallas_call x1, Pallas kernels, body(): call(owner_kernel, (sds((ROWS_DEV, COLS_DEV)), sds((ROWS_DEV, COLS_DEV)),...  5.51 us
    pallas_call x1, Pallas kernels, body(): call(send_kernel, sds((2 * GROUP, PS)), 1, 4, name='send')  4.03 us
    pallas_call x1, Pallas kernels, body(): call(strike_kernel, sds((2 * GROUP, PS)), 1, 8, name='strike')  3.09 us
    pallas_call x1, Pallas kernels, body(): call(route_kernel, (sds((PS, PS)), sds((1, ROWS), jnp.int32)), 1, 3, name...  2.88 us
  transfers between devices with their start and end apart: 1, of which 1 were waited for; matrix products, arithmetic and copies ran while one was open for 0% of the time, Pallas kernels for 3%

profile of v1, /device:TPU:1, one launch (start us, length us, event | category | flops | bytes accessed | tf_op | source)
XLA Modules:
  0.0 112.7 jit_solution(2279711364775187939)
XLA Ops:
  0.6 0.6 pad_add_fusion.idx
  1.3 4.0 %send.1 = f32[1024,128]{1,0:T(8,128)} custom-call(s32[2]{0:T(128)} %pad_add_fusion.idx, f32[32,512]{1,0:T(8,128)} %slip.3, f32[32,512]{1,0:T(8,128)} %rate.3, f32[8,2,32,512]{3,2,1,0:T(8,128)} %history.1, bf16[4,512,512]{2,1,0:T(8,128)(2,1)} %constant.35.clone.tables), custom_call_target="tpu_custom_call" | custom-call | tf_op jit(solution)/shard_map/send/pallas_call | solution.py:358
  5.3 22.1 %all-to-all-start = ((f32[512,2,128]{2,1,0:T(2,128)}), f32[512,2,128]{2,1,0:T(2,128)S(1)}, u32[]{:S(2)}, u32[]{:S(2)}) async-start(f32[512,2,128]{2,1,0:T(2,128)} %bitcast.14), calls=%async_computation | async-start | bytes 1048576 | tf_op jit(solution)/shard_map/all_to_all | solution.py:359
  28.1 2.9 %route.1 = (f32[128,128]{1,0:T(8,128)}, s32[1,4096]{1,0:T(1,128)}) custom-call(s32[1,1]{1,0:T(1,128)S(6)} %copy.21.count, s32[1,4096]{1,0:T(1,128)} %bitcast.16, s32[1,4096]{1,0:T(1,128)} %node.1, f32[1,4096]{1,0:T(1,128)} %value.1), custom_call_target="tpu_custom_call" | custom-call | tf_op jit(solution)/shard_map/route/pallas_call | solution.py:361
  31.0 18.4 %all-to-all-done = f32[512,2,128]{2,1,0:T(2,128)S(1)} async-done(((f32[512,2,128]{2,1,0:T(2,128)}), f32[512,2,128]{2,1,0:T(2,128)S(1)}, u32[]{:S(2)}, u32[]{:S(2)}) %all-to-all-start) | async-done | bytes 524320 | tf_op jit(solution)/shard_map/all_to_all | solution.py:359
  49.4 0.0 copy-start
  49.4 0.8 copy-done
  50.2 3.1 %strike.1 = f32[1024,128]{1,0:T(8,128)} custom-call(s32[2]{0:T(128)} %pad_add_fusion.idx, f32[1024,128]{1,0:T(8,128)} %bitcast.11, f32[128,128]{1,0:T(8,128)} %get-tuple-element.8.outbox, bf16[2,256,128]{2,1,0:T(8,128)(2,1)} %constant.36.clone.first, bf16[2,128,256]{2,1,0:T(8,128)(2,1)} %constant.37.clone.first_t, f32[2,128,128]{2,1,0:T(8,128)} %constant.38.clone.twiddle, ...), custom_call_target="tpu_custom_call" | custom-call | tf_op jit(solution)/shard_map/strike/pallas_call | solution.py:364
  53.3 33.1 %all_to_all.15 = f32[512,2,128]{2,1,0:T(2,128)} all-to-all(f32[512,2,128]{2,1,0:T(2,128)} %bitcast.12), channel_id=1, replica_groups=mesh['z'=8,'y'=8,'c'=2,'dip'=4] {'dip','z','y','c'}, dimensions={0} | all-to-all | bytes 1048576 | tf_op jit(solution)/shard_map/all_to_all | solution.py:367
  86.4 5.5 %owner.1 = (f32[32,512]{1,0:T(8,128)}, f32[32,512]{1,0:T(8,128)}, f32[128,128]{1,0:T(8,128)}) custom-call(s32[2]{0:T(128)} %pad_add_fusion.idx, f32[1024,128]{1,0:T(8,128)} %bitcast.13, f32[32,512]{1,0:T(8,128)} %slip.3, f32[32,512]{1,0:T(8,128)} %rate.3, f32[32,512]{1,0:T(8,128)} %prestress.1, f32[32,512]{1,0:T(8,128)} %normal.1, s32[32,512]{1,0:T(8,128)} %flag.1, ...), custom_call_target="tpu_custom_call" | custom-call | tf_op jit(solution)/shard_map/owner/pallas_call | solution.py:368
  91.9 18.7 %all_to_all.16 = f32[128,1,128]{2,1,0:T(1,128)} all-to-all(f32[128,1,128]{2,1,0:T(1,128)} %bitcast.18), channel_id=1, replica_groups=mesh['z'=8,'y'=8,'c'=2,'dip'=4] {'z','y','c'}, dimensions={0} | all-to-all | bytes 131072 | tf_op jit(solution)/shard_map/all_to_all | solution.py:376
  110.6 2.2 %back.1 = f32[1,4096]{1,0:T(1,128)} custom-call(s32[1,1]{1,0:T(1,128)S(6)} %copy.21.count, f32[128,128]{1,0:T(8,128)} %bitcast.15, s32[1,4096]{1,0:T(1,128)} %bitcast.17, s32[1,4096]{1,0:T(1,128)} %get-tuple-element.12.rank), custom_call_target="tpu_custom_call" | custom-call | tf_op jit(solution)/shard_map/back/pallas_call | solution.py:377
Async XLA Ops:
  5.3 44.1 %all-to-all-start = ((f32[512,2,128]{2,1,0:T(2,128)}), f32[512,2,128]{2,1,0:T(2,128)S(1)}, u32[]{:S(2)}, u32[]{:S(2)}) async-start(f32[512,2,128]{2,1,0:T(2,128)} %bitcast.14), calls=%async_computation | async-start | bytes 1048576 | tf_op jit(solution)/shard_map/all_to_all | solution.py:359
  49.4 0.8 copy-start

commit v2 on v1

--- a/solution.py
+++ b/solution.py
@@ -12,12 +12,12 @@
 NS, ND = 4096, 2048
 PS, QD = 128, 4
 ROWS_DEV, COLS_DEV = NS // PS, ND // QD
-GROUP = PS * QD
 RATE_DT = 0.5
 LEVELS = 7
 CAP = 64
 ROWS = 4096
 CHUNK = 512
+SEND, BACK = 6, 5
 SCALE = 1.0 / math.sqrt(NS * ND)
 bf16 = jnp.bfloat16
 f32 = jnp.float32
@@ -58,17 +58,22 @@
 
 
 def memory_tables():
-    out = np.zeros((2, 2 * PS, 2 * PS), np.float32)
+    out = np.zeros((8, 64, 2 * PS), np.float32)
     eye = np.eye(ROWS_DEV)
     for special in range(2):
         home = {0: 0, 1: 1, 2: 3, 3: 2} if special else {j: j for j in range(4)}
         partner = {0: 0, 3: 3, 1: 2, 2: 1} if special else {0: 3, 3: 0, 1: 2, 2: 1}
-        for slot in range(4):
-            own, other = home[slot], home[partner[slot]]
-            for slab, part, w_re, w_im in ((own, 0, 0.5, 0.5), (own, 1, -0.5, 0.5), (other, 0, 0.5, -0.5), (other, 1, 0.5, 0.5)):
-                rows = slice(64 * slab + 32 * part, 64 * slab + 32 * part + 32)
-                out[special, rows, 32 * slot : 32 * slot + 32] += w_re * eye
-                out[special, rows, PS + 32 * slot : PS + 32 * slot + 32] += w_im * eye
+        for slab in range(4):
+            own = home[slab]
+            for slot, part, w_re, w_im in (
+                (own, 0, 0.5, 0.5),
+                (own, 1, -0.5, 0.5),
+                (partner[own], 0, 0.5, -0.5),
+                (partner[own], 1, 0.5, 0.5),
+            ):
+                rows = slice(32 * part, 32 * part + 32)
+                out[4 * special + slab, rows, 32 * slot : 32 * slot + 32] += w_re * eye
+                out[4 * special + slab, rows, PS + 32 * slot : PS + 32 * slot + 32] += w_im * eye
     return out.astype(jnp.bfloat16)
 
 
@@ -148,67 +153,84 @@
         m_re = m_re + w_re * history(lag, 0)
         m_im = m_im + w_re * history(lag, 1)
     both = jnp.concatenate([m_re, m_im], axis=0)
-    odd = (q & 1) == 1
-    both = jnp.concatenate([jnp.where(odd, 0.0, both), jnp.where(odd, both, 0.0)], axis=0)
+    zero = jnp.zeros_like(both)
+    lower, upper = split(jnp.concatenate([both, zero], axis=0)), split(jnp.concatenate([zero, both], axis=0))
     row = iota((COLS_DEV, COLS_DEV), 0)
     from_col = jnp.where(q < 2, row, (COLS_DEV - row) & (COLS_DEV - 1))
     perm = (iota((COLS_DEV, COLS_DEV), 1) == from_col).astype(f32).astype(bf16)
-    hi, lo = split(both)
-    return dot(perm, hi, NT) + dot(perm, lo, NT)
+    out = []
+    for h in range(2):
+        even, odd = perm[2 * h * PS : (2 * h + 1) * PS], perm[(2 * h + 1) * PS : (2 * h + 2) * PS]
+        out.append((dot(even, lower[0], NT) + dot(odd, upper[0], NT)) + (dot(even, lower[1], NT) + dot(odd, upper[1], NT)))
+    return out
 
 
 def send_kernel(idx, slip, rate, history, tables, out):
     p, q = idx[0], idx[1]
-    out[pl.ds(0, GROUP, stride=2), :] = slip_part(slip[...], rate[...], [tables[i] for i in range(4)], q)
-    out[pl.ds(1, GROUP, stride=2), :] = memory_part(lambda lag, part: history[lag, part], p, q)
-
-
-def strike_part(slip_recv, mem_recv, first, first_t, twiddle, second, second_inv, mem_table, ell):
+    lines = slip_part(slip[...], rate[...], [tables[i] for i in range(4)], q)
+    for i in range(4):
+        out[pl.ds(i, PS, stride=SEND), :] = lines[PS * i : PS * (i + 1)]
+    for h, part in enumerate(memory_part(lambda lag, part: history[lag, part], p, q)):
+        out[pl.ds(4 + h, PS, stride=SEND), :] = part
+
+
+def strike_part(lines, mems, first, first_t, twiddle, second, second_inv, mem_table, p, q):
     n = PS
-    u = (slip_recv[0:n] + slip_recv[n : 2 * n]) + (slip_recv[2 * n : 3 * n] + slip_recv[3 * n :])
-    mem = jnp.concatenate([mem_recv[0:n] + mem_recv[n : 2 * n], mem_recv[2 * n : 3 * n] + mem_recv[3 * n :]], axis=1)
-    m_hi, m_lo = split(mem)
-    w = dot(m_hi, mem_table) + dot(m_lo, mem_table)
-    a = dot_table_data(first[0], first[1], u)
-    a_re, a_im = a[:n], a[n:]
+    w = []
+    for h in range(2):
+        m_hi, m_lo = split(mems[h])
+        for parity in range(2):
+            special = jnp.where(p == 0, 4, 0) if h == 0 and parity == 0 else 0
+            table = mem_table(special + q)
+            zero = jnp.zeros_like(table)
+            table = jnp.concatenate([zero, table] if parity else [table, zero], axis=0)
+            w.append(dot(m_hi, table) + dot(m_lo, table))
+    w = jnp.concatenate(w, axis=0)
+    a = dot_table_data(first[0], first[1], jnp.concatenate(lines, axis=1))
     tc, ts = twiddle[0], twiddle[1]
-    b = jnp.concatenate([a_re * tc + a_im * ts, a_im * tc - a_re * ts], axis=1)
-    spec = dot_data_table(b, second[0], second[1])
+    b = []
+    for i in range(4):
+        a_re, a_im = a[:n, n * i : n * (i + 1)], a[n:, n * i : n * (i + 1)]
+        b.append(jnp.concatenate([a_re * tc + a_im * ts, a_im * tc - a_re * ts], axis=1))
+    spec = dot_data_table(jnp.concatenate(b, axis=0), second[0], second[1])
     lane = iota((n, n), 1)
     fs = signed(rev_bits(iota((n, n), 0)) + PS * (lane & 31), NS)
+    fs = fs * fs
     slot = lane >> 5
-    kd = jnp.where((slot == 1) | (slot == 2), COLS_DEV + ell, ell)
-    kd = jnp.where((slot == 3) & (ell == 0), 2 * COLS_DEV, kd)
-    fd = kd.astype(f32) * (1.0 / ND)
-    wave = (2.0 * math.pi) * jnp.sqrt(fs * fs + fd * fd)
-    factor = (-0.5 * SCALE) * wave
-    factor = jnp.concatenate([factor, factor], axis=1)
-    g = factor * (SCALE * spec - w)
+    factor = []
+    for i in range(4):
+        ell = p + PS * i
+        kd = jnp.where((slot == 1) | (slot == 2), COLS_DEV + ell, ell)
+        kd = jnp.where((slot == 3) & (ell == 0), 2 * COLS_DEV, kd)
+        fd = kd.astype(f32) * (1.0 / ND)
+        wave = (2.0 * math.pi) * jnp.sqrt(fs + fd * fd)
+        wave = (-0.5 * SCALE) * wave
+        factor.append(jnp.concatenate([wave, wave], axis=1))
+    g = jnp.concatenate(factor, axis=0) * (SCALE * spec - w)
     b = dot_data_table(g, second_inv[0], second_inv[1])
-    b_re, b_im = b[:, :n], b[:, n:]
-    b = jnp.concatenate([b_re * tc - b_im * ts, b_re * ts + b_im * tc], axis=0)
-    return dot_table_data(first_t[0], first_t[1], b)
+    turned = []
+    for i in range(4):
+        b_re, b_im = b[n * i : n * (i + 1), :n], b[n * i : n * (i + 1), n:]
+        turned.append(jnp.concatenate([b_re * tc - b_im * ts, b_re * ts + b_im * tc], axis=0))
+    return dot_table_data(first_t[0], first_t[1], jnp.concatenate(turned, axis=1))
 
 
 def strike_kernel(idx, recv, outbox, first, first_t, twiddle, second, second_inv, mem_table, out):
-    p, q = idx[0], idx[1]
-    ell = PS * q + p
-    special = jnp.where(ell == 0, 1, 0)
     t = strike_part(
-        recv[pl.ds(0, GROUP, stride=2), :],
-        recv[pl.ds(1, GROUP, stride=2), :],
+        [recv[pl.ds(i, PS, stride=SEND), :] for i in range(4)],
+        [recv[pl.ds(4 + h, PS, stride=SEND), :] for h in range(2)],
         first,
         first_t,
         twiddle,
         second,
         second_inv,
-        mem_table[special],
-        ell,
+        lambda i: mem_table[i],
+        idx[0],
+        idx[1],
     )
-    box = outbox[...]
-    for qd in range(QD):
-        out[pl.ds(2 * PS * qd, PS, stride=2), :] = t
-        out[pl.ds(2 * PS * qd + 1, PS, stride=2), :] = jnp.where(q == qd, box, 0.0)
+    for i in range(4):
+        out[pl.ds(i, PS, stride=BACK), :] = t[:, PS * i : PS * (i + 1)]
+    out[pl.ds(4, PS, stride=BACK), :] = outbox[...]
 
 
 def route_part(dest, node, value, count):
@@ -243,19 +265,29 @@
     out[...], rank[...] = route_part(dest[...], node[...], value[...], count[0, 0])
 
 
-def functional_part(recv, tables, q):
+def dip_inverse_part(recv, tables):
     t = recv.T
     a, b, c, d = [t[32 * j : 32 * j + 32] for j in range(4)]
     s1, d1, s2, d2 = a + d, a - d, b + c, b - c
     fix = jnp.where(iota((ROWS_DEV, COLS_DEV), 1) == 0, 2.0 * d, 0.0)
     even = jnp.concatenate([s1 + s2, s1 + d2 - fix, s1 - s2, s1 - d2 - fix], axis=0)
     odd = jnp.concatenate([d1 + d2, d1 - s2, d1 - d2, d1 + s2], axis=0)
-    cm, sm = quarter(q)
-    even, odd = cm * even + sm * odd, cm * odd - sm * even
-    f = dot_data_table(even, tables[0], tables[1]) + dot_data_table(odd, tables[2], tables[3])
+    turns = [quarter(qd) for qd in range(QD)]
+    evens = jnp.concatenate([cm * even + sm * odd for cm, sm in turns], axis=0)
+    odds = jnp.concatenate([cm * odd - sm * even for cm, sm in turns], axis=0)
+    f = dot_data_table(evens, tables[0], tables[1]) + dot_data_table(odds, tables[2], tables[3])
     phase = iota((ROWS_DEV, COLS_DEV), 1) & 3
-    f = [jnp.where(phase == i, f[32 * i : 32 * i + 32], 0.0) for i in range(4)]
-    return (f[0] + f[1]) + (f[2] + f[3])
+    out = []
+    for qd in range(QD):
+        g = [jnp.where(phase == i, f[PS * qd + 32 * i : PS * qd + 32 * i + 32], 0.0) for i in range(4)]
+        out.append((g[0] + g[1]) + (g[2] + g[3]))
+    return out
+
+
+def dip_kernel(recv, tables, out):
+    lines = jnp.concatenate([recv[pl.ds(i, PS, stride=BACK), :] for i in range(4)], axis=0)
+    for qd, share in enumerate(dip_inverse_part(lines, [tables[i] for i in range(4)])):
+        out[qd] = share
 
 
 def unpack_rows(fe, roll):
@@ -286,34 +318,38 @@
     return jnp.sum(jnp.where(iota((PS, CHUNK), 0) == hi, got, 0.0), axis=0, keepdims=True)
 
 
-def owner_kernel(idx, recv, slip, rate, prestress, normal, flag, tables, new_rate, stress, sampled, onehots):
-    q = idx[1]
-    roll = lambda x: pltpu.roll(x, CAP, 1)
-    fe = recv[pl.ds(1, GROUP, stride=2), :]
-    fe = (fe[0:PS] + fe[PS : 2 * PS]) + (fe[2 * PS : 3 * PS] + fe[3 * PS :])
-    value, hi, lo = unpack_rows(fe, roll)
+def roll_half(x):
+    return pltpu.roll(x, CAP, 1)
+
+
+def traction_kernel(recv, traction, onehots, spots):
+    value, hi, lo = unpack_rows(recv[pl.ds(4, PS, stride=BACK), :], roll_half)
+    spots[...] = hi
     acc = jnp.zeros((2 * PS, PS), f32)
-    groups = CAP // 4
-    for g in range(groups):
+    for g in range(CAP // 4):
         onehot = column_onehot(lanes_of(lo, g))
         onehots[g] = onehot
         acc = acc + traction_step(lanes_of(value, g), lanes_of(hi, g), onehot)
     acc = acc[:PS] + acc[PS:]
-    traction = jnp.concatenate([acc[32 * i : 32 * i + 32] for i in range(4)], axis=1)
-    f = functional_part(recv[pl.ds(0, GROUP, stride=2), :], [tables[i] for i in range(4)], q)
+    traction[...] = jnp.concatenate([acc[32 * i : 32 * i + 32] for i in range(4)], axis=1)
+
+
+def owner_kernel(shares, traction, onehots, spots, slip, rate, prestress, normal, flag, new_rate, stress, sampled):
+    f = (shares[0] + shares[1]) + (shares[2] + shares[3])
     slip_new = slip[...] + RATE_DT * rate[...]
-    total = prestress[...] + f + traction
+    total = prestress[...] + f + traction[...]
     strength = normal[...] * (0.6 - (0.6 - 0.4) * jnp.minimum(slip_new, 1.0))
     fresh = jnp.where(flag[...] == 1, jnp.maximum(total - strength, 0.0) * 2.0, 0.0)
     stress[...] = total
     new_rate[...] = fresh
     stacked = jnp.concatenate([fresh[:, PS * i : PS * (i + 1)] for i in range(4)], axis=0)
     parts = jnp.concatenate(split(stacked), axis=1)
-    for g in range(groups):
+    hi = spots[...]
+    for g in range(CAP // 4):
         got = sample_step(parts, lanes_of(hi, g), onehots[g])
         for i in range(4):
             sampled[4 * g + i : 4 * g + i + 1, :] = got[:, PS * i : PS * (i + 1)]
-    sampled[CAP:PS, :] = roll(sampled[0:CAP, :])
+    sampled[CAP:PS, :] = roll_half(sampled[0:CAP, :])
 
 
 def return_part(got, dest, rank, count):
@@ -334,17 +370,21 @@
 
 
 STRIKE = ("z", "y", "c")
-ALL = ("dip", "z", "y", "c")
-
-
-def call(kernel, out_shape, smem, vmem, scratch=(), name=None):
+
+
+def call(kernel, out_shape, smem, vmem, name):
     specs = [pl.BlockSpec(memory_space=pltpu.SMEM)] * smem + [pl.BlockSpec(memory_space=pltpu.VMEM)] * vmem
     outs = jax.tree.map(lambda _: pl.BlockSpec(memory_space=pltpu.VMEM), out_shape)
-    return pl.pallas_call(kernel, out_shape=out_shape, in_specs=specs, out_specs=outs, scratch_shapes=scratch, name=name)
+    return pl.pallas_call(kernel, out_shape=out_shape, in_specs=specs, out_specs=outs, name=name)
 
 
 def sds(shape, dtype=f32):
     return jax.ShapeDtypeStruct(shape, dtype)
+
+
+def over_strike(x, width):
+    unit = 2 if width % 2 == 0 else 1
+    return lax.all_to_all(x.reshape(PS * width // unit, unit, PS), STRIKE, 0, 0, tiled=True).reshape(PS * width, PS)
 
 
 def body(slip, rate, prestress, normal_stress, history, fric_flag, row_dest, row_node, fe_traction, fe_count):
@@ -352,29 +392,30 @@
     q = lax.axis_index("dip").astype(jnp.int32)
     idx = jnp.stack([p, q])
     tables = jnp.asarray(dip_tables())
-    first, first_t, twiddle, second, second_inv = [jnp.asarray(t) for t in strike_tables()]
-    mem_table = jnp.asarray(memory_tables())
-
-    sent = call(send_kernel, sds((2 * GROUP, PS)), 1, 4, name="send")(idx, slip, rate, history, tables)
-    recv = lax.all_to_all(sent.reshape(GROUP, 2, PS), ALL, 0, 0, tiled=True).reshape(2 * GROUP, PS)
+    strike = [jnp.asarray(t) for t in strike_tables()] + [jnp.asarray(memory_tables())]
+
+    sent = call(send_kernel, sds((PS * SEND, PS)), 1, 4, "send")(idx, slip, rate, history, tables)
+    recv = over_strike(sent, SEND)
     dest = row_dest.reshape(1, ROWS)
-    box, rank = call(route_kernel, (sds((PS, PS)), sds((1, ROWS), jnp.int32)), 1, 3, name="route")(
+    box, rank = call(route_kernel, (sds((PS, PS)), sds((1, ROWS), jnp.int32)), 1, 3, "route")(
         fe_count, dest, row_node, fe_traction
     )
-    sent = call(strike_kernel, sds((2 * GROUP, PS)), 1, 8, name="strike")(
-        idx, recv, box, first, first_t, twiddle, second, second_inv, mem_table
-    )
-    recv = lax.all_to_all(sent.reshape(GROUP, 2, PS), ALL, 0, 0, tiled=True).reshape(2 * GROUP, PS)
+    sent = call(strike_kernel, sds((PS * BACK, PS)), 1, 8, "strike")(idx, recv, box, *strike)
+    recv = over_strike(sent, BACK)
+    shares = call(dip_kernel, sds((QD, ROWS_DEV, COLS_DEV)), 0, 2, "dip")(recv, tables)
+    shares = lax.all_to_all(shares, "dip", 0, 0, tiled=True)
+    traction, onehots, spots = call(
+        traction_kernel,
+        (sds((ROWS_DEV, COLS_DEV)), sds((CAP // 4, PS, CHUNK), bf16), sds((CAP, PS), jnp.int32)),
+        0,
+        1,
+        "traction",
+    )(recv)
     new_rate, stress, sampled = call(
-        owner_kernel,
-        (sds((ROWS_DEV, COLS_DEV)), sds((ROWS_DEV, COLS_DEV)), sds((PS, PS))),
-        1,
-        7,
-        scratch=[pltpu.VMEM((CAP // 4, PS, CHUNK), bf16)],
-        name="owner",
-    )(idx, recv, slip, rate, prestress, normal_stress, fric_flag, tables)
-    got = lax.all_to_all(sampled.reshape(PS, 1, PS), STRIKE, 0, 0, tiled=True).reshape(PS, PS)
-    fe_rate = call(return_kernel, sds((1, ROWS)), 1, 3, name="back")(fe_count, got, dest, rank)
+        owner_kernel, (sds((ROWS_DEV, COLS_DEV)), sds((ROWS_DEV, COLS_DEV)), sds((PS, PS))), 0, 9, "owner"
+    )(shares, traction, onehots, spots, slip, rate, prestress, normal_stress, fric_flag)
+    got = over_strike(sampled, 1)
+    fe_rate = call(return_kernel, sds((1, ROWS)), 1, 3, "back")(fe_count, got, dest, rank)
     return new_rate, stress, fe_rate
 
 

time: 113 us -> 110 us (0.973)
  blocking collectives: 51.8 us -> 42.5 us
  Pallas kernels: 17.7 us -> 24.5 us
  waiting for transfers between devices: 18.4 us -> 16.1 us
    all_to_all x2, blocking collectives: 51.8 us -> 42.5 us  [over_strike(): lax.all_to_all(x.reshape(PS * width // unit, unit, PS), STRIKE, 0, 0, til...]
    pallas_call x4 -> x6, Pallas kernels: 12.2 us -> 21.2 us  [the longest x1 4.28 us: body(): call(dip_kernel, sds((QD, ROWS_DEV, COLS_DEV)), 0, 2, 'dip')(recv, tables)]
    all_to_all x1 -> x2, waiting for transfers between devices: 18.4 us -> 16.1 us  [the longest x1 14.3 us: over_strike(): lax.all_to_all(x.reshape(PS * width // unit, unit, PS), STRIKE, 0, 0, til...]
    pallas_call x1, Pallas kernels: 5.51 us -> 3.33 us  [body(): call(owner_kernel, (sds((ROWS_DEV, COLS_DEV)), sds((ROWS_DEV, COLS_DEV)),...]
    all_to_all x1 -> x2, starting transfers between devices: 22.1 us -> 22.4 us  [the longest x1 18.4 us: over_strike(): lax.all_to_all(x.reshape(PS * width // unit, unit, PS), STRIKE, 0, 0, til...]
  transfers between devices with their start and end apart: 1 -> 2, of which waited for: 1 -> 2; matrix products, arithmetic and copies ran while one was open for 0% -> 0% of each run, Pallas kernels for 3% -> 6%
where the time goes in v2:
time: 110 us; the launch traced here: 109 us
  blocking collectives  42.5 us (39%)
  Pallas kernels  24.5 us (22%)
  starting transfers between devices  22.4 us (20%)
  waiting for transfers between devices  16.1 us (15%)
  local copies, waits for them, and re-layouts  1.44 us (1%)
  between operations  1.3 us (1%)
    all_to_all x2, blocking collectives, over_strike(): lax.all_to_all(x.reshape(PS * width // unit, unit, PS), STRIKE, 0, 0, til...  42.5 us
    all_to_all x1, starting transfers between devices, over_strike(): lax.all_to_all(x.reshape(PS * width // unit, unit, PS), STRIKE, 0, 0, til...  18.4 us
    all_to_all x1, waiting for transfers between devices, over_strike(): lax.all_to_all(x.reshape(PS * width // unit, unit, PS), STRIKE, 0, 0, til...  14.3 us
    pallas_call x1, Pallas kernels, body(): call(dip_kernel, sds((QD, ROWS_DEV, COLS_DEV)), 0, 2, 'dip')(recv, tables)  4.28 us
    pallas_call x1, Pallas kernels, body(): call(send_kernel, sds((PS * SEND, PS)), 1, 4, 'send')  4.04 us
    pallas_call x1, Pallas kernels, body(): call(traction_kernel, (sds((ROWS_DEV, COLS_DEV)), sds((CAP // 4, PS, CHUN...  4.04 us
    all_to_all x1, starting transfers between devices, body(): shares = lax.all_to_all(shares, 'dip', 0, 0, tiled=True)  4.01 us
    pallas_call x1, Pallas kernels, body(): call(strike_kernel, sds((PS * BACK, PS)), 1, 8, 'strike')  3.79 us
  transfers between devices with their start and end apart: 2, of which 2 were waited for; matrix products, arithmetic and copies ran while one was open for 0% of the time, Pallas kernels for 6%

profile of v2, /device:TPU:1, one launch (start us, length us, event | category | flops | bytes accessed | tf_op | source)
XLA Modules:
  0.0 108.9 jit_solution(14642160540684716787)
XLA Ops:
  0.6 0.6 pad_add_fusion.idx
  1.2 4.0 %send.1 = f32[768,128]{1,0:T(8,128)} custom-call(s32[2]{0:T(128)} %pad_add_fusion.idx, f32[32,512]{1,0:T(8,128)} %slip.3, f32[32,512]{1,0:T(8,128)} %rate.3, f32[8,2,32,512]{3,2,1,0:T(8,128)} %history.1, bf16[4,512,512]{2,1,0:T(8,128)(2,1)} %constant.35.clone.tables), custom_call_target="tpu_custom_call" | custom-call | tf_op jit(solution)/shard_map/send/pallas_call | solution.py:397
  5.3 18.4 %all-to-all-start = ((f32[384,2,128]{2,1,0:T(2,128)}), f32[384,2,128]{2,1,0:T(2,128)S(1)}, u32[]{:S(2)}, u32[]{:S(2)}) async-start(f32[384,2,128]{2,1,0:T(2,128)} %bitcast.16), calls=%async_computation | async-start | bytes 786432 | tf_op jit(solution)/shard_map/all_to_all | solution.py:387
  24.3 2.9 %route.1 = (f32[128,128]{1,0:T(8,128)}, s32[1,4096]{1,0:T(1,128)}) custom-call(s32[1,1]{1,0:T(1,128)S(6)} %copy.22.count, s32[1,4096]{1,0:T(1,128)} %bitcast.19, s32[1,4096]{1,0:T(1,128)} %node.1, f32[1,4096]{1,0:T(1,128)} %value.1), custom_call_target="tpu_custom_call" | custom-call | tf_op jit(solution)/shard_map/route/pallas_call | solution.py:400
  27.2 14.3 %all-to-all-done = f32[384,2,128]{2,1,0:T(2,128)S(1)} async-done(((f32[384,2,128]{2,1,0:T(2,128)}), f32[384,2,128]{2,1,0:T(2,128)S(1)}, u32[]{:S(2)}, u32[]{:S(2)}) %all-to-all-start) | async-done | bytes 393248 | tf_op jit(solution)/shard_map/all_to_all | solution.py:387
  41.5 0.0 copy-start
  41.5 0.7 copy-done
  42.3 3.8 %strike.1 = f32[640,128]{1,0:T(8,128)} custom-call(s32[2]{0:T(128)} %pad_add_fusion.idx, f32[768,128]{1,0:T(8,128)} %bitcast.15, f32[128,128]{1,0:T(8,128)} %get-tuple-element.11.outbox, bf16[2,256,128]{2,1,0:T(8,128)(2,1)} %constant.36.clone.first, bf16[2,128,256]{2,1,0:T(8,128)(2,1)} %constant.37.clone.first_t, f32[2,128,128]{2,1,0:T(8,128)} %constant.38.clone.twiddle, ...), custom_call_target="tpu_custom_call" | custom-call | tf_op jit(solution)/shard_map/strike/pallas_call | solution.py:403
  46.1 23.0 %all_to_all.20 = f32[640,1,128]{2,1,0:T(1,128)} all-to-all(f32[640,1,128]{2,1,0:T(1,128)} %bitcast.17), channel_id=1, replica_groups=mesh['z'=8,'y'=8,'c'=2,'dip'=4] {'z','y','c'}, dimensions={0} | all-to-all | bytes 655360 | tf_op jit(solution)/shard_map/all_to_all | solution.py:387
  69.1 4.3 %dip.1 = f32[4,32,512]{2,1,0:T(8,128)} custom-call(f32[640,128]{1,0:T(8,128)} %bitcast.13, bf16[4,512,512]{2,1,0:T(8,128)(2,1)} %constant.35.clone.tables), custom_call_target="tpu_custom_call" | custom-call | tf_op jit(solution)/shard_map/dip/pallas_call | solution.py:405
  73.4 4.0 %all-to-all-start.2 = ((f32[4,32,512]{2,1,0:T(8,128)}), f32[4,32,512]{2,1,0:T(8,128)S(1)}, u32[]{:S(2)}, u32[]{:S(2)}) async-start(f32[4,32,512]{2,1,0:T(8,128)} %dip.1), calls=%async_computation.2 | async-start | bytes 524288 | tf_op jit(solution)/shard_map/all_to_all | solution.py:406
  77.4 4.0 %traction.1 = (f32[32,512]{1,0:T(8,128)}, bf16[16,128,512]{2,1,0:T(8,128)(2,1)}, s32[64,128]{1,0:T(8,128)}) custom-call(f32[640,128]{1,0:T(8,128)} %bitcast.14), custom_call_target="tpu_custom_call" | custom-call | tf_op jit(solution)/shard_map/traction/pallas_call | solution.py:407
  81.4 1.8 %all-to-all-done.2.shares = f32[4,32,512]{2,1,0:T(8,128)S(1)} async-done(((f32[4,32,512]{2,1,0:T(8,128)}), f32[4,32,512]{2,1,0:T(8,128)S(1)}, u32[]{:S(2)}, u32[]{:S(2)}) %all-to-all-start.2) | async-done | bytes 262176 | tf_op jit(solution)/shard_map/all_to_all | solution.py:406
  83.2 0.0 copy-start.1
  83.2 0.7 copy-done.1
  83.9 3.3 %owner.1 = (f32[32,512]{1,0:T(8,128)}, f32[32,512]{1,0:T(8,128)}, f32[128,128]{1,0:T(8,128)}) custom-call(f32[4,32,512]{2,1,0:T(8,128)} %copy-done.1, f32[32,512]{1,0:T(8,128)} %get-tuple-element.12.traction, bf16[16,128,512]{2,1,0:T(8,128)(2,1)} %get-tuple-element.13.onehots, s32[64,128]{1,0:T(8,128)} %get-tuple-element.14.spots, f32[32,512]{1,0:T(8,128)} %slip.3, ...), custom_call_target="tpu_custom_call" | custom-call | tf_op jit(solution)/shard_map/owner/pallas_call | solution.py:414
  87.3 19.5 %all_to_all.21 = f32[128,1,128]{2,1,0:T(1,128)} all-to-all(f32[128,1,128]{2,1,0:T(1,128)} %bitcast.21), channel_id=1, replica_groups=mesh['z'=8,'y'=8,'c'=2,'dip'=4] {'z','y','c'}, dimensions={0} | all-to-all | bytes 131072 | tf_op jit(solution)/shard_map/all_to_all | solution.py:387
  106.8 2.2 %back.1 = f32[1,4096]{1,0:T(1,128)} custom-call(s32[1,1]{1,0:T(1,128)S(6)} %copy.22.count, f32[128,128]{1,0:T(8,128)} %bitcast.18, s32[1,4096]{1,0:T(1,128)} %bitcast.20, s32[1,4096]{1,0:T(1,128)} %get-tuple-element.18.rank), custom_call_target="tpu_custom_call" | custom-call | tf_op jit(solution)/shard_map/back/pallas_call | solution.py:418
Async XLA Ops:
  5.3 36.3 %all-to-all-start = ((f32[384,2,128]{2,1,0:T(2,128)}), f32[384,2,128]{2,1,0:T(2,128)S(1)}, u32[]{:S(2)}, u32[]{:S(2)}) async-start(f32[384,2,128]{2,1,0:T(2,128)} %bitcast.16), calls=%async_computation | async-start | bytes 786432 | tf_op jit(solution)/shard_map/all_to_all | solution.py:387
  41.5 0.7 copy-start
  73.4 9.9 %all-to-all-start.2 = ((f32[4,32,512]{2,1,0:T(8,128)}), f32[4,32,512]{2,1,0:T(8,128)S(1)}, u32[]{:S(2)}, u32[]{:S(2)}) async-start(f32[4,32,512]{2,1,0:T(8,128)} %dip.1), calls=%async_computation.2 | async-start | bytes 524288 | tf_op jit(solution)/shard_map/all_to_all | solution.py:406
  83.2 0.7 copy-start.1

commit v3 on v2

--- a/solution.py
+++ b/solution.py
@@ -17,6 +17,8 @@
 CAP = 64
 ROWS = 4096
 CHUNK = 512
+VMEM_LIMIT = 24 << 20
+STRIKE = ("z", "y", "c")
 SEND, BACK = 6, 5
 SCALE = 1.0 / math.sqrt(NS * ND)
 bf16 = jnp.bfloat16
@@ -36,9 +38,13 @@
 
 
 def dip_tables():
-    i = np.arange(COLS_DEV)
-    ang = 2 * np.pi * ((i[:, None] * i[None, :]) % ND) / ND
-    return np.concatenate([np_split(np.cos(ang)), np_split(np.sin(ang))])
+    ell = np.arange(COLS_DEV)
+    ang = 2 * np.pi * ((np.arange(COLS_DEV // 4)[:, None] * ell[None, :]) % COLS_DEV) / COLS_DEV
+    b = np.tile(np.arange(4), QD)[:, None]
+    q = np.repeat(np.arange(QD), 4)[:, None]
+    turn = 2 * np.pi * ((ell * b + COLS_DEV * q * ell) % ND) / ND
+    tables = np.concatenate([np_split(np.cos(ang)), np_split(np.sin(ang))])
+    return tables, np.stack([np.cos(turn), np.sin(turn)]).astype(np.float32)
 
 
 def strike_tables():
@@ -100,6 +106,10 @@
     return lax.broadcasted_iota(jnp.int32, shape, dim)
 
 
+def position():
+    return lax.axis_index(STRIKE), lax.axis_index("dip")
+
+
 def rev_bits(p):
     out = 0
     for b in range(LEVELS):
@@ -107,27 +117,34 @@
     return out
 
 
-def quarter(q):
-    turn = (q * iota((1, COLS_DEV), 1)) & 3
-    cm = jnp.where(turn == 0, 1.0, jnp.where(turn == 2, -1.0, 0.0))
-    sm = jnp.where(turn == 1, 1.0, jnp.where(turn == 3, -1.0, 0.0))
-    return cm, sm
+def turn_rows(turns, q):
+    return [(turns(0, 4 * q + b), turns(1, 4 * q + b)) for b in range(4)]
+
+
+def interleave(dims):
+    pos = iota((COLS_DEV, COLS_DEV), dims)
+    return (iota((COLS_DEV, COLS_DEV), 1 - dims) == 4 * (pos & (PS - 1)) + (pos >> 7)).astype(f32).astype(bf16)
+
+
+def by_class(x):
+    return jnp.concatenate([x[:, PS * b : PS * (b + 1)] for b in range(4)], axis=0)
 
 
 def signed(freq, length):
     return jnp.where(freq >= length // 2, freq - length, freq).astype(f32) * (1.0 / length)
 
 
-def slip_part(slip, rate, tables, q):
+def slip_part(slip, rate, tables, turns, q):
     x = slip + RATE_DT * rate
-    phase = iota((ROWS_DEV, COLS_DEV), 1) & 3
-    x4 = jnp.concatenate([jnp.where(phase == b, x, 0.0) for b in range(4)], axis=0)
-    c = dot_data_table(x4, tables[0], tables[1])
-    s = dot_data_table(x4, tables[2], tables[3])
-    cm, sm = quarter(q)
-    c, s = cm * c - sm * s, sm * c + cm * s
-    cs = [c[32 * b : 32 * b + 32] for b in range(4)]
-    ss = [s[32 * b : 32 * b + 32] for b in range(4)]
+    parts = dot(jnp.concatenate(split(x), axis=0), interleave(1)).astype(bf16)
+    hi, lo = by_class(parts[:ROWS_DEV]), by_class(parts[ROWS_DEV:])
+    c = dot(hi, tables[0]) + (dot(lo, tables[0]) + dot(hi, tables[1]))
+    s = dot(hi, tables[2]) + (dot(lo, tables[2]) + dot(hi, tables[3]))
+    cs, ss = [], []
+    for b, (ct, st) in enumerate(turn_rows(turns, q)):
+        c_b, s_b = c[32 * b : 32 * b + 32], s[32 * b : 32 * b + 32]
+        cs.append(ct * c_b - st * s_b)
+        ss.append(st * c_b + ct * s_b)
     c_even, c_odd = cs[0] + cs[2], cs[1] + cs[3]
     s_sum = (ss[0] + ss[2]) + (ss[1] + ss[3])
     h_a = (c_even + c_odd) + s_sum
@@ -165,13 +182,27 @@
     return out
 
 
-def send_kernel(idx, slip, rate, history, tables, out):
-    p, q = idx[0], idx[1]
-    lines = slip_part(slip[...], rate[...], [tables[i] for i in range(4)], q)
+def send_kernel(slip_in, rate_in, history_in, tables_in, turns_in, out, slip, rate, history, tables, turns, sems):
+    p, q = position()
+    lags = history.shape[0]
+    lag_copies = [pltpu.make_async_copy(history_in.at[i], history.at[i], sems.at[i]) for i in range(lags)]
+    pairs = ((slip_in, slip), (rate_in, rate), (tables_in, tables), (turns_in, turns))
+    copies = [pltpu.make_async_copy(src, dst, sems.at[lags + i]) for i, (src, dst) in enumerate(pairs)]
+    for copy in lag_copies + copies:
+        copy.start()
+
+    def read(lag, part):
+        if part == 0:
+            lag_copies[lag].wait()
+        return history[lag, part]
+
+    for h, part in enumerate(memory_part(read, p, q)):
+        out[pl.ds(4 + h, PS, stride=SEND), :] = part
+    for copy in copies:
+        copy.wait()
+    lines = slip_part(slip[...], rate[...], tables, lambda i, row: turns[i, pl.ds(row, 1), :], q)
     for i in range(4):
         out[pl.ds(i, PS, stride=SEND), :] = lines[PS * i : PS * (i + 1)]
-    for h, part in enumerate(memory_part(lambda lag, part: history[lag, part], p, q)):
-        out[pl.ds(4 + h, PS, stride=SEND), :] = part
 
 
 def strike_part(lines, mems, first, first_t, twiddle, second, second_inv, mem_table, p, q):
@@ -215,7 +246,7 @@
     return dot_table_data(first_t[0], first_t[1], jnp.concatenate(turned, axis=1))
 
 
-def strike_kernel(idx, recv, outbox, first, first_t, twiddle, second, second_inv, mem_table, out):
+def strike_kernel(recv, outbox, first, first_t, twiddle, second, second_inv, mem_table, out):
     t = strike_part(
         [recv[pl.ds(i, PS, stride=SEND), :] for i in range(4)],
         [recv[pl.ds(4 + h, PS, stride=SEND), :] for h in range(2)],
@@ -225,8 +256,7 @@
         second,
         second_inv,
         lambda i: mem_table[i],
-        idx[0],
-        idx[1],
+        *position(),
     )
     for i in range(4):
         out[pl.ds(i, PS, stride=BACK), :] = t[:, PS * i : PS * (i + 1)]
@@ -265,28 +295,35 @@
     out[...], rank[...] = route_part(dest[...], node[...], value[...], count[0, 0])
 
 
-def dip_inverse_part(recv, tables):
+def dip_inverse_part(recv, tables, turns):
     t = recv.T
     a, b, c, d = [t[32 * j : 32 * j + 32] for j in range(4)]
     s1, d1, s2, d2 = a + d, a - d, b + c, b - c
     fix = jnp.where(iota((ROWS_DEV, COLS_DEV), 1) == 0, 2.0 * d, 0.0)
-    even = jnp.concatenate([s1 + s2, s1 + d2 - fix, s1 - s2, s1 - d2 - fix], axis=0)
-    odd = jnp.concatenate([d1 + d2, d1 - s2, d1 - d2, d1 + s2], axis=0)
-    turns = [quarter(qd) for qd in range(QD)]
-    evens = jnp.concatenate([cm * even + sm * odd for cm, sm in turns], axis=0)
-    odds = jnp.concatenate([cm * odd - sm * even for cm, sm in turns], axis=0)
-    f = dot_data_table(evens, tables[0], tables[1]) + dot_data_table(odds, tables[2], tables[3])
-    phase = iota((ROWS_DEV, COLS_DEV), 1) & 3
-    out = []
+    even = [s1 + s2, s1 + d2 - fix, s1 - s2, s1 - d2 - fix]
+    odd = [d1 + d2, d1 - s2, d1 - d2, d1 + s2]
+    evens, odds = [], []
     for qd in range(QD):
-        g = [jnp.where(phase == i, f[PS * qd + 32 * i : PS * qd + 32 * i + 32], 0.0) for i in range(4)]
-        out.append((g[0] + g[1]) + (g[2] + g[3]))
-    return out
-
-
-def dip_kernel(recv, tables, out):
+        for i, (ct, st) in enumerate(turn_rows(turns, qd)):
+            evens.append(ct * even[i] + st * odd[i])
+            odds.append(ct * odd[i] - st * even[i])
+    f = 0.0
+    for x, k in ((evens, 0), (odds, 2)):
+        hi, lo = split(jnp.concatenate(x, axis=0))
+        f = f + (dot(hi, tables[k], NT) + (dot(lo, tables[k], NT) + dot(hi, tables[k + 1], NT)))
+    rows = 32
+    f = [[f[rows * (4 * qd + i) : rows * (4 * qd + i + 1)] for i in range(4)] for qd in range(QD)]
+    f = jnp.concatenate([jnp.concatenate(x, axis=1) for x in f], axis=0)
+    hi, lo = split(f)
+    back = interleave(0)
+    f = dot(hi, back) + dot(lo, back)
+    return [f[rows * qd : rows * (qd + 1)] for qd in range(QD)]
+
+
+def dip_kernel(recv, tables, turns, out):
     lines = jnp.concatenate([recv[pl.ds(i, PS, stride=BACK), :] for i in range(4)], axis=0)
-    for qd, share in enumerate(dip_inverse_part(lines, [tables[i] for i in range(4)])):
+    shares = dip_inverse_part(lines, tables, lambda i, row: turns[i, row : row + 1, :])
+    for qd, share in enumerate(shares):
         out[qd] = share
 
 
@@ -322,19 +359,20 @@
     return pltpu.roll(x, CAP, 1)
 
 
-def traction_kernel(recv, traction, onehots, spots):
+def traction_kernel(recv, traction, spots):
     value, hi, lo = unpack_rows(recv[pl.ds(4, PS, stride=BACK), :], roll_half)
-    spots[...] = hi
+    spots[0], spots[1] = hi, lo
     acc = jnp.zeros((2 * PS, PS), f32)
     for g in range(CAP // 4):
         onehot = column_onehot(lanes_of(lo, g))
-        onehots[g] = onehot
         acc = acc + traction_step(lanes_of(value, g), lanes_of(hi, g), onehot)
     acc = acc[:PS] + acc[PS:]
     traction[...] = jnp.concatenate([acc[32 * i : 32 * i + 32] for i in range(4)], axis=1)
 
 
-def owner_kernel(shares, traction, onehots, spots, slip, rate, prestress, normal, flag, new_rate, stress, sampled):
+def owner_kernel(
+    shares, traction, spots, slip, rate, prestress, normal, flag, new_rate_out, stress_out, sampled, new_rate, stress, sems
+):
     f = (shares[0] + shares[1]) + (shares[2] + shares[3])
     slip_new = slip[...] + RATE_DT * rate[...]
     total = prestress[...] + f + traction[...]
@@ -342,14 +380,22 @@
     fresh = jnp.where(flag[...] == 1, jnp.maximum(total - strength, 0.0) * 2.0, 0.0)
     stress[...] = total
     new_rate[...] = fresh
+    copies = [
+        pltpu.make_async_copy(new_rate, new_rate_out, sems.at[0]),
+        pltpu.make_async_copy(stress, stress_out, sems.at[1]),
+    ]
+    for copy in copies:
+        copy.start()
     stacked = jnp.concatenate([fresh[:, PS * i : PS * (i + 1)] for i in range(4)], axis=0)
     parts = jnp.concatenate(split(stacked), axis=1)
-    hi = spots[...]
+    hi, lo = spots[0], spots[1]
     for g in range(CAP // 4):
-        got = sample_step(parts, lanes_of(hi, g), onehots[g])
+        got = sample_step(parts, lanes_of(hi, g), column_onehot(lanes_of(lo, g)))
         for i in range(4):
             sampled[4 * g + i : 4 * g + i + 1, :] = got[:, PS * i : PS * (i + 1)]
     sampled[CAP:PS, :] = roll_half(sampled[0:CAP, :])
+    for copy in copies:
+        copy.wait()
 
 
 def return_part(got, dest, rank, count):
@@ -365,21 +411,30 @@
     return jnp.concatenate(out, axis=1)
 
 
-def return_kernel(count, got, dest, rank, out):
+def return_kernel(count, got, rank, dest, out):
     out[...] = return_part(got[...], dest[...], rank[...], count[0, 0])
 
 
-STRIKE = ("z", "y", "c")
-
-
-def call(kernel, out_shape, smem, vmem, name):
-    specs = [pl.BlockSpec(memory_space=pltpu.SMEM)] * smem + [pl.BlockSpec(memory_space=pltpu.VMEM)] * vmem
-    outs = jax.tree.map(lambda _: pl.BlockSpec(memory_space=pltpu.VMEM), out_shape)
-    return pl.pallas_call(kernel, out_shape=out_shape, in_specs=specs, out_specs=outs, name=name)
+def call(kernel, out_shape, operands, name, scalars=(), args=(), far=(), far_outs=0, scratch=()):
+    spec = pl.BlockSpec(memory_space=pltpu.VMEM)
+    hbm = pl.BlockSpec(memory_space=pltpu.HBM)
+    in_specs = [pl.BlockSpec(memory_space=pltpu.SMEM)] * len(scalars) + [hbm] * len(far) + [spec] * (len(operands) + len(args))
+    outs = tuple(hbm if i < far_outs else spec for i in range(len(out_shape))) if isinstance(out_shape, tuple) else spec
+    far = [pltpu.with_memory_space_constraint(x, pltpu.HBM) for x in far]
+    operands = [pltpu.with_memory_space_constraint(x, pltpu.VMEM) for x in operands]
+    return pl.pallas_call(
+        kernel,
+        out_shape=out_shape,
+        in_specs=in_specs,
+        out_specs=outs,
+        name=name,
+        scratch_shapes=scratch,
+        compiler_params=pltpu.CompilerParams(vmem_limit_bytes=VMEM_LIMIT),
+    )(*scalars, *far, *operands, *args)
 
 
 def sds(shape, dtype=f32):
-    return jax.ShapeDtypeStruct(shape, dtype)
+    return pltpu.VMEM(shape, dtype)
 
 
 def over_strike(x, width):
@@ -388,34 +443,38 @@
 
 
 def body(slip, rate, prestress, normal_stress, history, fric_flag, row_dest, row_node, fe_traction, fe_count):
-    p = lax.axis_index(STRIKE).astype(jnp.int32)
-    q = lax.axis_index("dip").astype(jnp.int32)
-    idx = jnp.stack([p, q])
-    tables = jnp.asarray(dip_tables())
+    tables, turns = [jnp.asarray(t) for t in dip_tables()]
     strike = [jnp.asarray(t) for t in strike_tables()] + [jnp.asarray(memory_tables())]
-
-    sent = call(send_kernel, sds((PS * SEND, PS)), 1, 4, "send")(idx, slip, rate, history, tables)
+    dest = row_dest.reshape(1, ROWS)
+
+    inputs = (slip, rate, history, tables, turns)
+    scratch = [pltpu.VMEM(x.shape, x.dtype) for x in inputs] + [pltpu.SemaphoreType.DMA((history.shape[0] + 4,))]
+    sent = call(send_kernel, sds((PS * SEND, PS)), (), "send", far=inputs, scratch=scratch)
     recv = over_strike(sent, SEND)
-    dest = row_dest.reshape(1, ROWS)
-    box, rank = call(route_kernel, (sds((PS, PS)), sds((1, ROWS), jnp.int32)), 1, 3, "route")(
-        fe_count, dest, row_node, fe_traction
+    box, rank = call(
+        route_kernel, (sds((PS, PS)), sds((1, ROWS), jnp.int32)), (), "route", (fe_count,), (dest, row_node, fe_traction)
     )
-    sent = call(strike_kernel, sds((PS * BACK, PS)), 1, 8, "strike")(idx, recv, box, *strike)
+    sent = call(strike_kernel, sds((PS * BACK, PS)), (recv, box), "strike", args=strike)
     recv = over_strike(sent, BACK)
-    shares = call(dip_kernel, sds((QD, ROWS_DEV, COLS_DEV)), 0, 2, "dip")(recv, tables)
+    shares = call(dip_kernel, sds((QD, ROWS_DEV, COLS_DEV)), (recv,), "dip", args=(tables, turns))
     shares = lax.all_to_all(shares, "dip", 0, 0, tiled=True)
-    traction, onehots, spots = call(
+    traction, spots = call(
         traction_kernel,
-        (sds((ROWS_DEV, COLS_DEV)), sds((CAP // 4, PS, CHUNK), bf16), sds((CAP, PS), jnp.int32)),
-        0,
-        1,
+        (sds((ROWS_DEV, COLS_DEV)), sds((2, CAP, PS), jnp.int32)),
+        (recv,),
         "traction",
-    )(recv)
+    )
     new_rate, stress, sampled = call(
-        owner_kernel, (sds((ROWS_DEV, COLS_DEV)), sds((ROWS_DEV, COLS_DEV)), sds((PS, PS))), 0, 9, "owner"
-    )(shares, traction, onehots, spots, slip, rate, prestress, normal_stress, fric_flag)
+        owner_kernel,
+        (jax.ShapeDtypeStruct(slip.shape, f32), jax.ShapeDtypeStruct(slip.shape, f32), sds((PS, PS))),
+        (shares, traction, spots),
+        "owner",
+        args=(slip, rate, prestress, normal_stress, fric_flag),
+        far_outs=2,
+        scratch=[sds(slip.shape), sds(slip.shape), pltpu.SemaphoreType.DMA((2,))],
+    )
     got = over_strike(sampled, 1)
-    fe_rate = call(return_kernel, sds((1, ROWS)), 1, 3, "back")(fe_count, got, dest, rank)
+    fe_rate = call(return_kernel, jax.ShapeDtypeStruct((1, ROWS), f32), (got, rank), "back", (fe_count,), (dest,))
     return new_rate, stress, fe_rate
 
 

time: 110 us -> 97.4 us (0.89)
  Pallas kernels: 24.5 us -> 13.1 us
  waiting for transfers between devices: 16.1 us -> 20.1 us
  blocking collectives: 42.5 us -> 39.7 us
  local copies, waits for them, and re-layouts: 1.44 us -> 0.09 us
    pallas_call x7, Pallas kernels: 24.5 us -> 13.1 us  [call(): pl.pallas_call(kernel, out_shape=out_shape, in_specs=in_specs, out_specs=...]
    all_to_all x2, blocking collectives: 42.5 us -> 39.7 us  [over_strike(): lax.all_to_all(x.reshape(PS * width // unit, unit, PS), STRIKE, 0, 0, til...]
    all_to_all x1, waiting for transfers between devices: 1.8 us -> 4.37 us  [body(): shares = lax.all_to_all(shares, 'dip', 0, 0, tiled=True)]
    all_to_all x1, waiting for transfers between devices: 14.3 us -> 15.7 us  [over_strike(): lax.all_to_all(x.reshape(PS * width // unit, unit, PS), STRIKE, 0, 0, til...]
    unnamed x4 -> x32, local copies, waits for them, and re-layouts: 1.44 us -> 0.09 us
  transfers between devices with their start and end apart: 2 -> 2, of which waited for: 2 -> 2; matrix products, arithmetic and copies ran while one was open for 0% -> 0% of each run, Pallas kernels for 6% -> 3%
where the time goes in v3:
time: 97.4 us; the launch traced here: 97.1 us
  blocking collectives  39.7 us (41%)
  starting transfers between devices  22.6 us (23%)
  waiting for transfers between devices  20.1 us (21%)
  Pallas kernels  13.1 us (13%)
  between operations  1.51 us (2%)
    all_to_all x2, blocking collectives, over_strike(): lax.all_to_all(x.reshape(PS * width // unit, unit, PS), STRIKE, 0, 0, til...  39.7 us
    all_to_all x1, starting transfers between devices, over_strike(): lax.all_to_all(x.reshape(PS * width // unit, unit, PS), STRIKE, 0, 0, til...  18.6 us
    all_to_all x1, waiting for transfers between devices, over_strike(): lax.all_to_all(x.reshape(PS * width // unit, unit, PS), STRIKE, 0, 0, til...  15.7 us
    pallas_call x7, Pallas kernels, call(): pl.pallas_call(kernel, out_shape=out_shape, in_specs=in_specs, out_specs=...  13.1 us
    all_to_all x1, waiting for transfers between devices, body(): shares = lax.all_to_all(shares, 'dip', 0, 0, tiled=True)  4.37 us
    all_to_all x1, starting transfers between devices, body(): shares = lax.all_to_all(shares, 'dip', 0, 0, tiled=True)  4.02 us
  transfers between devices with their start and end apart: 2, of which 2 were waited for; matrix products, arithmetic and copies ran while one was open for 0% of the time, Pallas kernels for 3%

profile of v3, /device:TPU:1, one launch (start us, length us, event | category | flops | bytes accessed | tf_op | source)
XLA Modules:
  0.0 97.1 jit_solution(11608267186880686008)
XLA Ops:
  0.6 0.0 copy-start.10
  0.6 0.0 copy-start.14
  0.7 0.0 copy-start.15
  0.7 0.0 copy-start.7
  0.7 0.0 copy-start.8
  0.7 0.0 copy-start.9
  0.7 3.4 %send.1 = f32[768,128]{1,0:T(8,128)} custom-call(f32[32,512]{1,0:T(8,128)} %slip.1, f32[32,512]{1,0:T(8,128)} %rate.1, f32[8,2,32,512]{3,2,1,0:T(8,128)} %history_in.1, bf16[4,128,512]{2,1,0:T(8,128)(2,1)} %constant.16.clone.tables_in.tables, f32[2,16,512]{2,1,0:T(8,128)} %constant.17.clone.turns_in.turns), custom_call_target="tpu_custom_call" | custom-call | tf_op jit(solution)/shard_map/send/pallas_call | solution.py:425
  4.1 0.0 copy-start.1
  4.1 0.0 copy-start.2
  4.2 0.0 copy-start.3
  4.2 18.6 %all-to-all-start = ((f32[384,2,128]{2,1,0:T(2,128)}), f32[384,2,128]{2,1,0:T(2,128)S(1)}, u32[]{:S(2)}, u32[]{:S(2)}) async-start(f32[384,2,128]{2,1,0:T(2,128)} %bitcast), calls=%async_computation | async-start | bytes 786432 | tf_op jit(solution)/shard_map/all_to_all | solution.py:442
  23.4 0.0 copy-done.10
  23.4 0.0 copy-done.14
  23.4 0.0 copy-done.15
  23.4 1.5 %route.1 = (f32[128,128]{1,0:T(8,128)S(1)}, s32[1,4096]{1,0:T(1,128)S(1)}) custom-call(s32[1,1]{1,0:T(1,128)S(6)} %copy.23.count, s32[1,4096]{1,0:T(1,128)S(1)} %bitcast.16, s32[1,4096]{1,0:T(1,128)S(1)} %copy-done.14, f32[1,4096]{1,0:T(1,128)S(1)} %copy-done.15), custom_call_target="tpu_custom_call" | custom-call | tf_op jit(solution)/shard_map/route/pallas_call | solution.py:425
  24.9 15.7 %all-to-all-done = f32[384,2,128]{2,1,0:T(2,128)S(1)} async-done(((f32[384,2,128]{2,1,0:T(2,128)}), f32[384,2,128]{2,1,0:T(2,128)S(1)}, u32[]{:S(2)}, u32[]{:S(2)}) %all-to-all-start) | async-done | bytes 393248 | tf_op jit(solution)/shard_map/all_to_all | solution.py:442
  40.6 0.0 copy-done.9
  40.6 1.7 %strike.1 = f32[640,128]{1,0:T(8,128)S(1)} custom-call(f32[768,128]{1,0:T(8,128)S(1)} %bitcast.13, f32[128,128]{1,0:T(8,128)S(1)} %get-tuple-element.10.outbox, bf16[2,256,128]{2,1,0:T(8,128)(2,1)S(1)} %copy-done.9, bf16[2,128,256]{2,1,0:T(8,128)(2,1)S(1)} %copy-done.8, f32[2,128,128]{2,1,0:T(8,128)S(1)} %copy-done.7, bf16[2,256,256]{2,1,0:T(8,128)(2,1)S(1)} %copy-done.3, ...), custom_call_target="tpu_custom_call" | custom-call | tf_op jit(solution)/shard_map/strike/pallas_call | solution.py:425
  42.3 0.0 copy-start
  42.3 0.0 copy-start.4
  42.3 21.8 %all_to_all.20 = f32[640,1,128]{2,1,0:T(1,128)S(1)} all-to-all(f32[640,1,128]{2,1,0:T(1,128)S(1)} %bitcast.14), channel_id=1, replica_groups=mesh['z'=8,'y'=8,'c'=2,'dip'=4] {'z','y','c'}, dimensions={0} | all-to-all | bytes 655360 | tf_op jit(solution)/shard_map/all_to_all | solution.py:442
  64.1 0.0 copy-done
  64.1 2.2 %dip.1 = f32[4,32,512]{2,1,0:T(8,128)} custom-call(f32[640,128]{1,0:T(8,128)S(1)} %bitcast.11, bf16[4,128,512]{2,1,0:T(8,128)(2,1)S(1)} %copy-done, f32[2,16,512]{2,1,0:T(8,128)S(1)} %copy-done.4), custom_call_target="tpu_custom_call" | custom-call | tf_op jit(solution)/shard_map/dip/pallas_call | solution.py:425
  66.3 4.0 %all-to-all-start.2 = ((f32[4,32,512]{2,1,0:T(8,128)}), f32[4,32,512]{2,1,0:T(8,128)S(1)}, u32[]{:S(2)}, u32[]{:S(2)}) async-start(f32[4,32,512]{2,1,0:T(8,128)} %dip.1), calls=%async_computation.2 | async-start | bytes 524288 | tf_op jit(solution)/shard_map/all_to_all | solution.py:460
  70.4 0.0 copy-start.12
  70.4 0.0 copy-start.13
  70.4 1.4 %traction.1 = (f32[32,512]{1,0:T(8,128)S(1)}, s32[2,64,128]{2,1,0:T(8,128)S(1)}) custom-call(f32[640,128]{1,0:T(8,128)S(1)} %bitcast.12), custom_call_target="tpu_custom_call" | custom-call | tf_op jit(solution)/shard_map/traction/pallas_call | solution.py:425
  71.8 4.4 %all-to-all-done.2.shares = f32[4,32,512]{2,1,0:T(8,128)S(1)} async-done(((f32[4,32,512]{2,1,0:T(8,128)}), f32[4,32,512]{2,1,0:T(8,128)S(1)}, u32[]{:S(2)}, u32[]{:S(2)}) %all-to-all-start.2) | async-done | bytes 262176 | tf_op jit(solution)/shard_map/all_to_all | solution.py:460
  76.2 0.0 copy-done.6
  76.2 1.6 %owner.1 = (f32[32,512]{1,0:T(8,128)}, f32[32,512]{1,0:T(8,128)}, f32[128,128]{1,0:T(8,128)S(1)}) custom-call(f32[4,32,512]{2,1,0:T(8,128)S(1)} %all-to-all-done.2.shares, f32[32,512]{1,0:T(8,128)S(1)} %get-tuple-element.11.traction, s32[2,64,128]{2,1,0:T(8,128)S(1)} %get-tuple-element.12.spots, f32[32,512]{1,0:T(8,128)S(1)} %copy-done.5, ...), custom_call_target="tpu_custom_call" | custom-call | tf_op jit(solution)/shard_map/owner/pallas_call | solution.py:425
  77.8 17.9 %all_to_all.21 = f32[128,1,128]{2,1,0:T(1,128)S(1)} all-to-all(f32[128,1,128]{2,1,0:T(1,128)S(1)} %bitcast.18), channel_id=1, replica_groups=mesh['z'=8,'y'=8,'c'=2,'dip'=4] {'z','y','c'}, dimensions={0} | all-to-all | bytes 131072 | tf_op jit(solution)/shard_map/all_to_all | solution.py:442
  95.7 1.3 %back.1 = f32[1,4096]{1,0:T(1,128)} custom-call(s32[1,1]{1,0:T(1,128)S(6)} %copy.23.count, f32[128,128]{1,0:T(8,128)S(1)} %bitcast.15, s32[1,4096]{1,0:T(1,128)S(1)} %get-tuple-element.16.rank, s32[1,4096]{1,0:T(1,128)S(1)} %bitcast.17), custom_call_target="tpu_custom_call" | custom-call | tf_op jit(solution)/shard_map/back/pallas_call | solution.py:425
  (13 shorter events, 0.0 us)
Async XLA Ops:
  0.6 22.7 %copy-start.10 = (s32[1,4096,1]{1,2,0:T(1,128)S(1)}, s32[1,4096,1]{1,2,0:T(1,128)}, u32[]{:S(2)}) copy-start(s32[1,4096,1]{1,2,0:T(1,128)} %param.24) | copy-start | bytes 49156
  0.6 22.7 %copy-start.14 = (s32[1,4096]{1,0:T(1,128)S(1)}, s32[1,4096]{1,0:T(1,128)}, u32[]{:S(2)}) copy-start(s32[1,4096]{1,0:T(1,128)} %node.1) | copy-start | bytes 49156
  0.7 22.7 %copy-start.15 = (f32[1,4096]{1,0:T(1,128)S(1)}, f32[1,4096]{1,0:T(1,128)}, u32[]{:S(2)}) copy-start(f32[1,4096]{1,0:T(1,128)} %value.1) | copy-start | bytes 49156
  0.7 39.9 %copy-start.7 = (f32[2,128,128]{2,1,0:T(8,128)S(1)}, f32[2,128,128]{2,1,0:T(8,128)}, u32[]{:S(2)}) copy-start(f32[2,128,128]{2,1,0:T(8,128)} %constant.20.clone.twiddle) | copy-start | bytes 393220
  0.7 39.9 %copy-start.8 = (bf16[2,128,256]{2,1,0:T(8,128)(2,1)S(1)}, bf16[2,128,256]{2,1,0:T(8,128)(2,1)}, u32[]{:S(2)}) copy-start(bf16[2,128,256]{2,1,0:T(8,128)(2,1)} %constant.19.clone.first_t) | copy-start | bytes 393220
  0.7 39.9 %copy-start.9 = (bf16[2,256,128]{2,1,0:T(8,128)(2,1)S(1)}, bf16[2,256,128]{2,1,0:T(8,128)(2,1)}, u32[]{:S(2)}) copy-start(bf16[2,256,128]{2,1,0:T(8,128)(2,1)} %constant.18.clone.first) | copy-start | bytes 393220
  4.1 36.5 %copy-start.1 = (bf16[8,64,256]{2,1,0:T(8,128)(2,1)S(1)}, bf16[8,64,256]{2,1,0:T(8,128)(2,1)}, u32[]{:S(2)}) copy-start(bf16[8,64,256]{2,1,0:T(8,128)(2,1)} %constant.23.clone.mem_table) | copy-start | bytes 786436
  4.1 36.5 %copy-start.2 = (bf16[2,256,256]{2,1,0:T(8,128)(2,1)S(1)}, bf16[2,256,256]{2,1,0:T(8,128)(2,1)}, u32[]{:S(2)}) copy-start(bf16[2,256,256]{2,1,0:T(8,128)(2,1)} %constant.22.clone.second_inv) | copy-start | bytes 786436
  4.2 36.5 %copy-start.3 = (bf16[2,256,256]{2,1,0:T(8,128)(2,1)S(1)}, bf16[2,256,256]{2,1,0:T(8,128)(2,1)}, u32[]{:S(2)}) copy-start(bf16[2,256,256]{2,1,0:T(8,128)(2,1)} %constant.21.clone.second) | copy-start | bytes 786436
  4.2 36.4 %all-to-all-start = ((f32[384,2,128]{2,1,0:T(2,128)}), f32[384,2,128]{2,1,0:T(2,128)S(1)}, u32[]{:S(2)}, u32[]{:S(2)}) async-start(f32[384,2,128]{2,1,0:T(2,128)} %bitcast), calls=%async_computation | async-start | bytes 786432 | tf_op jit(solution)/shard_map/all_to_all | solution.py:442
  42.3 21.8 %copy-start = (bf16[4,128,512]{2,1,0:T(8,128)(2,1)S(1)}, bf16[4,128,512]{2,1,0:T(8,128)(2,1)}, u32[]{:S(2)}) copy-start(bf16[4,128,512]{2,1,0:T(8,128)(2,1)} %constant.16.clone.tables_in.tables) | copy-start | bytes 1572868
  42.3 21.8 %copy-start.4 = (f32[2,16,512]{2,1,0:T(8,128)S(1)}, f32[2,16,512]{2,1,0:T(8,128)}, u32[]{:S(2)}) copy-start(f32[2,16,512]{2,1,0:T(8,128)} %constant.17.clone.turns_in.turns) | copy-start | bytes 196612
  66.3 9.9 %all-to-all-start.2 = ((f32[4,32,512]{2,1,0:T(8,128)}), f32[4,32,512]{2,1,0:T(8,128)S(1)}, u32[]{:S(2)}, u32[]{:S(2)}) async-start(f32[4,32,512]{2,1,0:T(8,128)} %dip.1), calls=%async_computation.2 | async-start | bytes 524288 | tf_op jit(solution)/shard_map/all_to_all | solution.py:460
  70.4 5.8 %copy-start.5 = (f32[32,512]{1,0:T(8,128)S(1)}, f32[32,512]{1,0:T(8,128)}, u32[]{:S(2)}) copy-start(f32[32,512]{1,0:T(8,128)} %slip.1) | copy-start | bytes 196612
  70.4 5.8 %copy-start.6 = (f32[32,512]{1,0:T(8,128)S(1)}, f32[32,512]{1,0:T(8,128)}, u32[]{:S(2)}) copy-start(f32[32,512]{1,0:T(8,128)} %rate.1) | copy-start | bytes 196612
  70.4 5.8 %copy-start.11 = (f32[32,512]{1,0:T(8,128)S(1)}, f32[32,512]{1,0:T(8,128)}, u32[]{:S(2)}) copy-start(f32[32,512]{1,0:T(8,128)} %prestress.1) | copy-start | bytes 196612
  70.4 5.8 %copy-start.12 = (f32[32,512]{1,0:T(8,128)S(1)}, f32[32,512]{1,0:T(8,128)}, u32[]{:S(2)}) copy-start(f32[32,512]{1,0:T(8,128)} %normal.1) | copy-start | bytes 196612
  70.4 5.8 %copy-start.13 = (s32[32,512]{1,0:T(8,128)S(1)}, s32[32,512]{1,0:T(8,128)}, u32[]{:S(2)}) copy-start(s32[32,512]{1,0:T(8,128)} %flag.1) | copy-start | bytes 196612

commit v4 on v3

--- a/solution.py
+++ b/solution.py
@@ -19,7 +19,7 @@
 CHUNK = 512
 VMEM_LIMIT = 24 << 20
 STRIKE = ("z", "y", "c")
-SEND, BACK = 6, 5
+SEND, BACK = 4, 3
 SCALE = 1.0 / math.sqrt(NS * ND)
 bf16 = jnp.bfloat16
 f32 = jnp.float32
@@ -64,23 +64,16 @@
 
 
 def memory_tables():
-    out = np.zeros((8, 64, 2 * PS), np.float32)
+    out = np.zeros((4, 2, 2, 32, 2, 2, 2, 32), np.float32)
     eye = np.eye(ROWS_DEV)
-    for special in range(2):
-        home = {0: 0, 1: 1, 2: 3, 3: 2} if special else {j: j for j in range(4)}
-        partner = {0: 0, 3: 3, 1: 2, 2: 1} if special else {0: 3, 3: 0, 1: 2, 2: 1}
-        for slab in range(4):
-            own = home[slab]
-            for slot, part, w_re, w_im in (
-                (own, 0, 0.5, 0.5),
-                (own, 1, -0.5, 0.5),
-                (partner[own], 0, 0.5, -0.5),
-                (partner[own], 1, 0.5, 0.5),
-            ):
-                rows = slice(32 * part, 32 * part + 32)
-                out[4 * special + slab, rows, 32 * slot : 32 * slot + 32] += w_re * eye
-                out[4 * special + slab, rows, PS + 32 * slot : PS + 32 * slot + 32] += w_im * eye
-    return out.astype(jnp.bfloat16)
+    for case in range(4):
+        own = case & 1
+        for parity in range(2):
+            other = own if case >= 2 and parity == 0 else 1 - own
+            for slot, part, w_re, w_im in ((own, 0, 0.5, 0.5), (own, 1, -0.5, 0.5), (other, 0, 0.5, -0.5), (other, 1, 0.5, 0.5)):
+                out[case, parity, part, :, 0, parity, slot, :] += w_re * eye
+                out[case, parity, part, :, 1, parity, slot, :] += w_im * eye
+    return out.reshape(4, PS, 2 * PS).astype(jnp.bfloat16)
 
 
 def dot(a, b, dims=NN):
@@ -134,25 +127,34 @@
     return jnp.where(freq >= length // 2, freq - length, freq).astype(f32) * (1.0 / length)
 
 
-def slip_part(slip, rate, tables, turns, q):
-    x = slip + RATE_DT * rate
-    parts = dot(jnp.concatenate(split(x), axis=0), interleave(1)).astype(bf16)
-    hi, lo = by_class(parts[:ROWS_DEV]), by_class(parts[ROWS_DEV:])
+def outer_modes(ell, q):
+    return jnp.where(ell == 0, 1 - (q & 1), 1 - ((q ^ (q >> 1)) & 1)) == 1
+
+
+def slip_part(own, other, tables, turns, q):
+    parts = jnp.concatenate(split(own) + split(other), axis=0)
+    parts = dot(parts, interleave(1)).astype(bf16)
+    own_hi, own_lo, other_hi, other_lo = [by_class(parts[ROWS_DEV * i : ROWS_DEV * (i + 1)]) for i in range(4)]
+    hi, lo = jnp.concatenate([own_hi, other_hi], axis=0), jnp.concatenate([own_lo, other_lo], axis=0)
     c = dot(hi, tables[0]) + (dot(lo, tables[0]) + dot(hi, tables[1]))
     s = dot(hi, tables[2]) + (dot(lo, tables[2]) + dot(hi, tables[3]))
-    cs, ss = [], []
-    for b, (ct, st) in enumerate(turn_rows(turns, q)):
-        c_b, s_b = c[32 * b : 32 * b + 32], s[32 * b : 32 * b + 32]
-        cs.append(ct * c_b - st * s_b)
-        ss.append(st * c_b + ct * s_b)
+    cs, ss = [0.0] * 4, [0.0] * 4
+    for block, block_q in enumerate((q, q ^ 1)):
+        for b, (ct, st) in enumerate(turn_rows(turns, block_q)):
+            rows = slice(PS * block + 32 * b, PS * block + 32 * b + 32)
+            cs[b] = cs[b] + (ct * c[rows] - st * s[rows])
+            ss[b] = ss[b] + (st * c[rows] + ct * s[rows])
     c_even, c_odd = cs[0] + cs[2], cs[1] + cs[3]
     s_sum = (ss[0] + ss[2]) + (ss[1] + ss[3])
+    ell = iota((ROWS_DEV, COLS_DEV), 1)
     h_a = (c_even + c_odd) + s_sum
-    first = iota((ROWS_DEV, COLS_DEV), 1) == 0
-    h_d = (c_even + jnp.where(first, -c_odd, c_odd)) - s_sum
+    h_d = (c_even + jnp.where(ell == 0, -c_odd, c_odd)) - s_sum
     even = cs[0] - cs[2] + ss[3] - ss[1]
     odd = ss[0] - ss[2] + cs[1] - cs[3]
-    return jnp.concatenate([h_a, even + odd, even - odd, h_d], axis=0).T
+    outer = outer_modes(ell, q)
+    both = jnp.concatenate([jnp.where(outer, h_a, even + odd), jnp.where(outer, h_d, even - odd)], axis=0)
+    both = [both[:, PS * i : PS * (i + 1)] for i in range(4)]
+    return [jnp.concatenate(both[2 * h : 2 * h + 2], axis=0).T for h in range(2)]
 
 
 def memory_part(history, p, q):
@@ -182,27 +184,27 @@
     return out
 
 
-def send_kernel(slip_in, rate_in, history_in, tables_in, turns_in, out, slip, rate, history, tables, turns, sems):
+def memory_kernel(history_in, out, history, sems):
     p, q = position()
-    lags = history.shape[0]
-    lag_copies = [pltpu.make_async_copy(history_in.at[i], history.at[i], sems.at[i]) for i in range(lags)]
-    pairs = ((slip_in, slip), (rate_in, rate), (tables_in, tables), (turns_in, turns))
-    copies = [pltpu.make_async_copy(src, dst, sems.at[lags + i]) for i, (src, dst) in enumerate(pairs)]
-    for copy in lag_copies + copies:
+    copies = [pltpu.make_async_copy(history_in.at[i], history.at[i], sems.at[i]) for i in range(history.shape[0])]
+    for copy in copies:
         copy.start()
 
     def read(lag, part):
         if part == 0:
-            lag_copies[lag].wait()
+            copies[lag].wait()
         return history[lag, part]
 
     for h, part in enumerate(memory_part(read, p, q)):
-        out[pl.ds(4 + h, PS, stride=SEND), :] = part
-    for copy in copies:
-        copy.wait()
-    lines = slip_part(slip[...], rate[...], tables, lambda i, row: turns[i, pl.ds(row, 1), :], q)
-    for i in range(4):
-        out[pl.ds(i, PS, stride=SEND), :] = lines[PS * i : PS * (i + 1)]
+        out[PS * h : PS * (h + 1), :] = part
+
+
+def send_kernel(own, other, mem, tables, turns, out):
+    q = position()[1]
+    lines = slip_part(own[...], other[...], tables, lambda i, row: turns[i, pl.ds(row, 1), :], q)
+    for h in range(2):
+        out[pl.ds(h, PS, stride=SEND), :] = lines[h]
+        out[pl.ds(2 + h, PS, stride=SEND), :] = mem[PS * h : PS * (h + 1), :]
 
 
 def strike_part(lines, mems, first, first_t, twiddle, second, second_inv, mem_table, p, q):
@@ -210,29 +212,25 @@
     w = []
     for h in range(2):
         m_hi, m_lo = split(mems[h])
-        for parity in range(2):
-            special = jnp.where(p == 0, 4, 0) if h == 0 and parity == 0 else 0
-            table = mem_table(special + q)
-            zero = jnp.zeros_like(table)
-            table = jnp.concatenate([zero, table] if parity else [table, zero], axis=0)
-            w.append(dot(m_hi, table) + dot(m_lo, table))
+        alone = jnp.where((p == 0) & ((q & 1) == 0), 2, 0) if h == 0 else 0
+        table = mem_table(alone + (q >> 1))
+        w.append(dot(m_hi, table) + dot(m_lo, table))
     w = jnp.concatenate(w, axis=0)
     a = dot_table_data(first[0], first[1], jnp.concatenate(lines, axis=1))
     tc, ts = twiddle[0], twiddle[1]
     b = []
-    for i in range(4):
-        a_re, a_im = a[:n, n * i : n * (i + 1)], a[n:, n * i : n * (i + 1)]
+    for h in range(2):
+        a_re, a_im = a[:n, n * h : n * (h + 1)], a[n:, n * h : n * (h + 1)]
         b.append(jnp.concatenate([a_re * tc + a_im * ts, a_im * tc - a_re * ts], axis=1))
     spec = dot_data_table(jnp.concatenate(b, axis=0), second[0], second[1])
     lane = iota((n, n), 1)
     fs = signed(rev_bits(iota((n, n), 0)) + PS * (lane & 31), NS)
     fs = fs * fs
-    slot = lane >> 5
+    parity, slot = lane >> 6, (lane >> 5) & 1
     factor = []
-    for i in range(4):
-        ell = p + PS * i
-        kd = jnp.where((slot == 1) | (slot == 2), COLS_DEV + ell, ell)
-        kd = jnp.where((slot == 3) & (ell == 0), 2 * COLS_DEV, kd)
+    for h in range(2):
+        ell = p + PS * (2 * h + parity)
+        kd = jnp.where(outer_modes(ell, q), jnp.where((ell == 0) & (slot == 1), 2 * COLS_DEV, ell), COLS_DEV + ell)
         fd = kd.astype(f32) * (1.0 / ND)
         wave = (2.0 * math.pi) * jnp.sqrt(fs + fd * fd)
         wave = (-0.5 * SCALE) * wave
@@ -240,16 +238,16 @@
     g = jnp.concatenate(factor, axis=0) * (SCALE * spec - w)
     b = dot_data_table(g, second_inv[0], second_inv[1])
     turned = []
-    for i in range(4):
-        b_re, b_im = b[n * i : n * (i + 1), :n], b[n * i : n * (i + 1), n:]
+    for h in range(2):
+        b_re, b_im = b[n * h : n * (h + 1), :n], b[n * h : n * (h + 1), n:]
         turned.append(jnp.concatenate([b_re * tc - b_im * ts, b_re * ts + b_im * tc], axis=0))
     return dot_table_data(first_t[0], first_t[1], jnp.concatenate(turned, axis=1))
 
 
 def strike_kernel(recv, outbox, first, first_t, twiddle, second, second_inv, mem_table, out):
     t = strike_part(
-        [recv[pl.ds(i, PS, stride=SEND), :] for i in range(4)],
-        [recv[pl.ds(4 + h, PS, stride=SEND), :] for h in range(2)],
+        [recv[pl.ds(h, PS, stride=SEND), :] for h in range(2)],
+        [recv[pl.ds(2 + h, PS, stride=SEND), :] for h in range(2)],
         first,
         first_t,
         twiddle,
@@ -258,9 +256,9 @@
         lambda i: mem_table[i],
         *position(),
     )
-    for i in range(4):
-        out[pl.ds(i, PS, stride=BACK), :] = t[:, PS * i : PS * (i + 1)]
-    out[pl.ds(4, PS, stride=BACK), :] = outbox[...]
+    for h in range(2):
+        out[pl.ds(h, PS, stride=BACK), :] = t[:, PS * h : PS * (h + 1)]
+    out[pl.ds(2, PS, stride=BACK), :] = outbox[...]
 
 
 def route_part(dest, node, value, count):
@@ -295,11 +293,18 @@
     out[...], rank[...] = route_part(dest[...], node[...], value[...], count[0, 0])
 
 
-def dip_inverse_part(recv, tables, turns):
-    t = recv.T
-    a, b, c, d = [t[32 * j : 32 * j + 32] for j in range(4)]
-    s1, d1, s2, d2 = a + d, a - d, b + c, b - c
-    fix = jnp.where(iota((ROWS_DEV, COLS_DEV), 1) == 0, 2.0 * d, 0.0)
+def dip_inverse_part(lines, tables, turns, q):
+    lines = [x.T for x in lines]
+    t0, t1 = [
+        jnp.concatenate([lines[i >> 1][64 * (i & 1) + 32 * slot : 64 * (i & 1) + 32 * slot + 32] for i in range(4)], axis=1)
+        for slot in range(2)
+    ]
+    ell = iota((ROWS_DEV, COLS_DEV), 1)
+    outer = outer_modes(ell, q)
+    total, diff = t0 + t1, t0 - t1
+    s1, d1 = jnp.where(outer, total, 0.0), jnp.where(outer, diff, 0.0)
+    s2, d2 = total - s1, diff - d1
+    fix = jnp.where(outer & (ell == 0), 2.0 * t1, 0.0)
     even = [s1 + s2, s1 + d2 - fix, s1 - s2, s1 - d2 - fix]
     odd = [d1 + d2, d1 - s2, d1 - d2, d1 + s2]
     evens, odds = [], []
@@ -321,8 +326,8 @@
 
 
 def dip_kernel(recv, tables, turns, out):
-    lines = jnp.concatenate([recv[pl.ds(i, PS, stride=BACK), :] for i in range(4)], axis=0)
-    shares = dip_inverse_part(lines, tables, lambda i, row: turns[i, row : row + 1, :])
+    lines = [recv[pl.ds(h, PS, stride=BACK), :] for h in range(2)]
+    shares = dip_inverse_part(lines, tables, lambda i, row: turns[i, row : row + 1, :], position()[1])
     for qd, share in enumerate(shares):
         out[qd] = share
 
@@ -360,7 +365,7 @@
 
 
 def traction_kernel(recv, traction, spots):
-    value, hi, lo = unpack_rows(recv[pl.ds(4, PS, stride=BACK), :], roll_half)
+    value, hi, lo = unpack_rows(recv[pl.ds(2, PS, stride=BACK), :], roll_half)
     spots[0], spots[1] = hi, lo
     acc = jnp.zeros((2 * PS, PS), f32)
     for g in range(CAP // 4):
@@ -438,7 +443,7 @@
 
 
 def over_strike(x, width):
-    unit = 2 if width % 2 == 0 else 1
+    unit = width if width in (1, 2, 4) else 1
     return lax.all_to_all(x.reshape(PS * width // unit, unit, PS), STRIKE, 0, 0, tiled=True).reshape(PS * width, PS)
 
 
@@ -447,9 +452,17 @@
     strike = [jnp.asarray(t) for t in strike_tables()] + [jnp.asarray(memory_tables())]
     dest = row_dest.reshape(1, ROWS)
 
-    inputs = (slip, rate, history, tables, turns)
-    scratch = [pltpu.VMEM(x.shape, x.dtype) for x in inputs] + [pltpu.SemaphoreType.DMA((history.shape[0] + 4,))]
-    sent = call(send_kernel, sds((PS * SEND, PS)), (), "send", far=inputs, scratch=scratch)
+    slip_new = slip + RATE_DT * rate
+    other = lax.ppermute(slip_new, "dip", [(i, i ^ 1) for i in range(QD)])
+    mem = call(
+        memory_kernel,
+        sds((2 * PS, PS)),
+        (),
+        "memory",
+        far=(history,),
+        scratch=[sds(history.shape), pltpu.SemaphoreType.DMA((history.shape[0],))],
+    )
+    sent = call(send_kernel, sds((PS * SEND, PS)), (slip_new, other, mem), "send", args=(tables, turns))
     recv = over_strike(sent, SEND)
     box, rank = call(
         route_kernel, (sds((PS, PS)), sds((1, ROWS), jnp.int32)), (), "route", (fe_count,), (dest, row_node, fe_traction)

time: 97.4 us -> 97.3 us (level)
  starting transfers between devices: 22.6 us -> 27.1 us
  waiting for transfers between devices: 20.1 us -> 17.4 us
  blocking collectives: 39.7 us -> 37.1 us
    ppermute x0 -> x1, starting transfers between devices: none -> 4.07 us  [body(): other = lax.ppermute(slip_new, 'dip', [(i, i ^ 1) for i in range(QD)])]
    all_to_all x2, blocking collectives: 39.7 us -> 37.1 us  [over_strike(): lax.all_to_all(x.reshape(PS * width // unit, unit, PS), STRIKE, 0, 0, til...]
    all_to_all x1, waiting for transfers between devices: 15.7 us -> 13.1 us  [over_strike(): lax.all_to_all(x.reshape(PS * width // unit, unit, PS), STRIKE, 0, 0, til...]
    pallas_call x7 -> x8, Pallas kernels: 13.1 us -> 12.8 us  [call(): pl.pallas_call(kernel, out_shape=out_shape, in_specs=in_specs, out_specs=...]
  transfers between devices with their start and end apart: 2 -> 3, of which waited for: 2 -> 2; matrix products, arithmetic and copies ran while one was open for 0% -> 0% of each run, Pallas kernels for 3% -> 5%
where the time goes in v4:
time: 97.3 us; the launch traced here: 96.8 us
  blocking collectives  37.1 us (38%)
  starting transfers between devices  27.1 us (28%)
  waiting for transfers between devices  17.4 us (18%)
  Pallas kernels  12.8 us (13%)
  between operations  1.51 us (2%)
    all_to_all x2, blocking collectives, over_strike(): lax.all_to_all(x.reshape(PS * width // unit, unit, PS), STRIKE, 0, 0, til...  37.1 us
    all_to_all x1, starting transfers between devices, over_strike(): lax.all_to_all(x.reshape(PS * width // unit, unit, PS), STRIKE, 0, 0, til...  18.8 us
    all_to_all x1, waiting for transfers between devices, over_strike(): lax.all_to_all(x.reshape(PS * width // unit, unit, PS), STRIKE, 0, 0, til...  13.1 us
    pallas_call x8, Pallas kernels, call(): pl.pallas_call(kernel, out_shape=out_shape, in_specs=in_specs, out_specs=...  12.8 us
    all_to_all x1, waiting for transfers between devices, body(): shares = lax.all_to_all(shares, 'dip', 0, 0, tiled=True)  4.36 us
    all_to_all x1, starting transfers between devices, body(): shares = lax.all_to_all(shares, 'dip', 0, 0, tiled=True)  4.15 us
    ppermute x1, starting transfers between devices, body(): other = lax.ppermute(slip_new, 'dip', [(i, i ^ 1) for i in range(QD)])  4.07 us
  transfers between devices with their start and end apart: 3, of which 2 were waited for; matrix products, arithmetic and copies ran while one was open for 0% of the time, Pallas kernels for 5%

profile of v4, /device:TPU:1, one launch (start us, length us, event | category | flops | bytes accessed | tf_op | source)
XLA Modules:
  0.0 96.8 jit_solution(8343326109927921024)
XLA Ops:
  0.6 0.9 multiply_add_fusion.own
  1.5 0.0 copy-start
  1.5 0.0 copy-start.1
  1.5 4.1 %collective-permute-start = (f32[32,512]{1,0:T(8,128)S(1)}, f32[32,512]{1,0:T(8,128)S(1)}, u32[]{:S(2)}, u32[]{:S(2)}) collective-permute-start(f32[32,512]{1,0:T(8,128)S(1)} %multiply_add_fusion.own), channel_id=1, source_target_pairs={{0,1},{1,0},{2,3},{3,2},{4,5},{5,4},{6,7},{7,6},{8,9},{9,8},{10,11... | collective-permute-start | bytes 196616 | tf_op jit(solution)/shard_map/ppermute | solution.py:456
  5.6 1.9 %memory.1.mem = f32[256,128]{1,0:T(8,128)S(1)} custom-call(f32[8,2,32,512]{3,2,1,0:T(8,128)} %history_in.1), custom_call_target="tpu_custom_call" | custom-call | tf_op jit(solution)/shard_map/memory/pallas_call | solution.py:430
  7.5 0.0 collective-permute-done.other
  7.5 0.0 copy-start.10
  7.5 0.0 copy-start.14
  7.5 0.0 copy-start.15
  7.6 0.0 copy-start.4
  7.6 0.0 copy-start.7
  7.6 0.0 copy-start.8
  7.6 0.0 copy-start.9
  7.6 1.6 %send.1 = f32[512,128]{1,0:T(8,128)} custom-call(f32[32,512]{1,0:T(8,128)S(1)} %multiply_add_fusion.own, f32[32,512]{1,0:T(8,128)S(1)} %collective-permute-done.other, f32[256,128]{1,0:T(8,128)S(1)} %memory.1.mem, bf16[4,128,512]{2,1,0:T(8,128)(2,1)S(1)} %copy-done, f32[2,16,512]{2,1,0:T(8,128)S(1)} %copy-done.1), custom_call_target="tpu_custom_call" | custom-call | tf_op jit(solution)/shard_map/send/pallas_call | solution.py:430
  9.2 18.8 %all-to-all-start = ((f32[128,4,128]{2,1,0:T(4,128)}), f32[128,4,128]{2,1,0:T(4,128)S(1)}, u32[]{:S(2)}, u32[]{:S(2)}) async-start(f32[128,4,128]{2,1,0:T(4,128)} %bitcast), calls=%async_computation | async-start | bytes 524288 | tf_op jit(solution)/shard_map/all_to_all | solution.py:447
  28.7 0.0 copy-done.10
  28.7 0.0 copy-done.14
  28.7 0.0 copy-done.15
  28.8 1.5 %route.1 = (f32[128,128]{1,0:T(8,128)S(1)}, s32[1,4096]{1,0:T(1,128)S(1)}) custom-call(s32[1,1]{1,0:T(1,128)S(6)} %copy.23.count, s32[1,4096]{1,0:T(1,128)S(1)} %bitcast.16, s32[1,4096]{1,0:T(1,128)S(1)} %copy-done.14, f32[1,4096]{1,0:T(1,128)S(1)} %copy-done.15), custom_call_target="tpu_custom_call" | custom-call | tf_op jit(solution)/shard_map/route/pallas_call | solution.py:430
  30.2 13.1 %all-to-all-done = f32[128,4,128]{2,1,0:T(4,128)S(1)} async-done(((f32[128,4,128]{2,1,0:T(4,128)}), f32[128,4,128]{2,1,0:T(4,128)S(1)}, u32[]{:S(2)}, u32[]{:S(2)}) %all-to-all-start) | async-done | bytes 262176 | tf_op jit(solution)/shard_map/all_to_all | solution.py:447
  43.3 0.0 copy-done.7
  43.4 1.2 %strike.1 = f32[384,128]{1,0:T(8,128)S(1)} custom-call(f32[512,128]{1,0:T(8,128)S(1)} %bitcast.13, f32[128,128]{1,0:T(8,128)S(1)} %get-tuple-element.10.outbox, bf16[2,256,128]{2,1,0:T(8,128)(2,1)S(1)} %copy-done.9, bf16[2,128,256]{2,1,0:T(8,128)(2,1)S(1)} %copy-done.8, f32[2,128,128]{2,1,0:T(8,128)S(1)} %copy-done.7, bf16[2,256,256]{2,1,0:T(8,128)(2,1)S(1)} %copy-done.4, ...), custom_call_target="tpu_custom_call" | custom-call | tf_op jit(solution)/shard_map/strike/pallas_call | solution.py:430
  44.6 19.0 %all_to_all.20 = f32[384,1,128]{2,1,0:T(1,128)S(1)} all-to-all(f32[384,1,128]{2,1,0:T(1,128)S(1)} %bitcast.14), channel_id=1, replica_groups=mesh['z'=8,'y'=8,'c'=2,'dip'=4] {'z','y','c'}, dimensions={0} | all-to-all | bytes 393216 | tf_op jit(solution)/shard_map/all_to_all | solution.py:447
  63.5 2.3 %dip.1 = f32[4,32,512]{2,1,0:T(8,128)} custom-call(f32[384,128]{1,0:T(8,128)S(1)} %bitcast.11, bf16[4,128,512]{2,1,0:T(8,128)(2,1)S(1)} %copy-done, f32[2,16,512]{2,1,0:T(8,128)S(1)} %copy-done.1), custom_call_target="tpu_custom_call" | custom-call | tf_op jit(solution)/shard_map/dip/pallas_call | solution.py:430
  65.8 4.2 %all-to-all-start.2 = ((f32[4,32,512]{2,1,0:T(8,128)}), f32[4,32,512]{2,1,0:T(8,128)S(1)}, u32[]{:S(2)}, u32[]{:S(2)}) async-start(f32[4,32,512]{2,1,0:T(8,128)} %dip.1), calls=%async_computation.2 | async-start | bytes 524288 | tf_op jit(solution)/shard_map/all_to_all | solution.py:473
  69.9 1.4 %traction.1 = (f32[32,512]{1,0:T(8,128)S(1)}, s32[2,64,128]{2,1,0:T(8,128)S(1)}) custom-call(f32[384,128]{1,0:T(8,128)S(1)} %bitcast.12), custom_call_target="tpu_custom_call" | custom-call | tf_op jit(solution)/shard_map/traction/pallas_call | solution.py:430
  71.4 4.4 %all-to-all-done.2.shares = f32[4,32,512]{2,1,0:T(8,128)S(1)} async-done(((f32[4,32,512]{2,1,0:T(8,128)}), f32[4,32,512]{2,1,0:T(8,128)S(1)}, u32[]{:S(2)}, u32[]{:S(2)}) %all-to-all-start.2) | async-done | bytes 262176 | tf_op jit(solution)/shard_map/all_to_all | solution.py:473
  75.7 0.0 copy-done.6
  75.7 0.0 copy-done.11
  75.8 1.6 %owner.1 = (f32[32,512]{1,0:T(8,128)}, f32[32,512]{1,0:T(8,128)}, f32[128,128]{1,0:T(8,128)S(1)}) custom-call(f32[4,32,512]{2,1,0:T(8,128)S(1)} %all-to-all-done.2.shares, f32[32,512]{1,0:T(8,128)S(1)} %get-tuple-element.11.traction, s32[2,64,128]{2,1,0:T(8,128)S(1)} %get-tuple-element.12.spots, f32[32,512]{1,0:T(8,128)S(1)} %copy-done.5, ...), custom_call_target="tpu_custom_call" | custom-call | tf_op jit(solution)/shard_map/owner/pallas_call | solution.py:430
  77.4 18.1 %all_to_all.21 = f32[128,1,128]{2,1,0:T(1,128)S(1)} all-to-all(f32[128,1,128]{2,1,0:T(1,128)S(1)} %bitcast.18), channel_id=1, replica_groups=mesh['z'=8,'y'=8,'c'=2,'dip'=4] {'z','y','c'}, dimensions={0} | all-to-all | bytes 131072 | tf_op jit(solution)/shard_map/all_to_all | solution.py:447
  95.5 1.3 %back.1 = f32[1,4096]{1,0:T(1,128)} custom-call(s32[1,1]{1,0:T(1,128)S(6)} %copy.23.count, f32[128,128]{1,0:T(8,128)S(1)} %bitcast.15, s32[1,4096]{1,0:T(1,128)S(1)} %get-tuple-element.16.rank, s32[1,4096]{1,0:T(1,128)S(1)} %bitcast.17), custom_call_target="tpu_custom_call" | custom-call | tf_op jit(solution)/shard_map/back/pallas_call | solution.py:430
  (17 shorter events, 0.0 us)
Async XLA Ops:
  1.5 6.0 %copy-start = (bf16[4,128,512]{2,1,0:T(8,128)(2,1)S(1)}, bf16[4,128,512]{2,1,0:T(8,128)(2,1)}, u32[]{:S(2)}) copy-start(bf16[4,128,512]{2,1,0:T(8,128)(2,1)} %constant.18.clone.tables) | copy-start | bytes 1572868
  1.5 6.0 %copy-start.1 = (f32[2,16,512]{2,1,0:T(8,128)S(1)}, f32[2,16,512]{2,1,0:T(8,128)}, u32[]{:S(2)}) copy-start(f32[2,16,512]{2,1,0:T(8,128)} %constant.19.clone.turns) | copy-start | bytes 196612
  1.5 6.0 %collective-permute-start = (f32[32,512]{1,0:T(8,128)S(1)}, f32[32,512]{1,0:T(8,128)S(1)}, u32[]{:S(2)}, u32[]{:S(2)}) collective-permute-start(f32[32,512]{1,0:T(8,128)S(1)} %multiply_add_fusion.own), channel_id=1, source_target_pairs={{0,1},{1,0},{2,3},{3,2},{4,5},{5,4},{6,7},{7,6},{8,9},{9,8},{10,11... | collective-permute-start | bytes 196616 | tf_op jit(solution)/shard_map/ppermute | solution.py:456
  7.5 21.2 %copy-start.10 = (s32[1,4096,1]{1,2,0:T(1,128)S(1)}, s32[1,4096,1]{1,2,0:T(1,128)}, u32[]{:S(2)}) copy-start(s32[1,4096,1]{1,2,0:T(1,128)} %param.24) | copy-start | bytes 49156
  7.5 21.2 %copy-start.14 = (s32[1,4096]{1,0:T(1,128)S(1)}, s32[1,4096]{1,0:T(1,128)}, u32[]{:S(2)}) copy-start(s32[1,4096]{1,0:T(1,128)} %node.1) | copy-start | bytes 49156
  7.5 21.2 %copy-start.15 = (f32[1,4096]{1,0:T(1,128)S(1)}, f32[1,4096]{1,0:T(1,128)}, u32[]{:S(2)}) copy-start(f32[1,4096]{1,0:T(1,128)} %value.1) | copy-start | bytes 49156
  7.6 35.8 %copy-start.4 = (bf16[2,256,256]{2,1,0:T(8,128)(2,1)S(1)}, bf16[2,256,256]{2,1,0:T(8,128)(2,1)}, u32[]{:S(2)}) copy-start(bf16[2,256,256]{2,1,0:T(8,128)(2,1)} %constant.23.clone.second) | copy-start | bytes 786436
  7.6 35.7 %copy-start.7 = (f32[2,128,128]{2,1,0:T(8,128)S(1)}, f32[2,128,128]{2,1,0:T(8,128)}, u32[]{:S(2)}) copy-start(f32[2,128,128]{2,1,0:T(8,128)} %constant.22.clone.twiddle) | copy-start | bytes 393220
  7.6 35.7 %copy-start.8 = (bf16[2,128,256]{2,1,0:T(8,128)(2,1)S(1)}, bf16[2,128,256]{2,1,0:T(8,128)(2,1)}, u32[]{:S(2)}) copy-start(bf16[2,128,256]{2,1,0:T(8,128)(2,1)} %constant.21.clone.first_t) | copy-start | bytes 393220
  7.6 35.7 %copy-start.9 = (bf16[2,256,128]{2,1,0:T(8,128)(2,1)S(1)}, bf16[2,256,128]{2,1,0:T(8,128)(2,1)}, u32[]{:S(2)}) copy-start(bf16[2,256,128]{2,1,0:T(8,128)(2,1)} %constant.20.clone.first) | copy-start | bytes 393220
  9.2 34.1 %copy-start.2 = (bf16[4,128,256]{2,1,0:T(8,128)(2,1)S(1)}, bf16[4,128,256]{2,1,0:T(8,128)(2,1)}, u32[]{:S(2)}) copy-start(bf16[4,128,256]{2,1,0:T(8,128)(2,1)} %constant.25.clone.mem_table) | copy-start | bytes 786436
  9.2 34.1 %copy-start.3 = (bf16[2,256,256]{2,1,0:T(8,128)(2,1)S(1)}, bf16[2,256,256]{2,1,0:T(8,128)(2,1)}, u32[]{:S(2)}) copy-start(bf16[2,256,256]{2,1,0:T(8,128)(2,1)} %constant.24.clone.second_inv) | copy-start | bytes 786436
  9.2 34.1 %all-to-all-start = ((f32[128,4,128]{2,1,0:T(4,128)}), f32[128,4,128]{2,1,0:T(4,128)S(1)}, u32[]{:S(2)}, u32[]{:S(2)}) async-start(f32[128,4,128]{2,1,0:T(4,128)} %bitcast), calls=%async_computation | async-start | bytes 524288 | tf_op jit(solution)/shard_map/all_to_all | solution.py:447
  65.8 10.0 %copy-start.12 = (f32[32,512]{1,0:T(8,128)S(1)}, f32[32,512]{1,0:T(8,128)}, u32[]{:S(2)}) copy-start(f32[32,512]{1,0:T(8,128)} %normal.1) | copy-start | bytes 196612
  65.8 10.0 %copy-start.13 = (s32[32,512]{1,0:T(8,128)S(1)}, s32[32,512]{1,0:T(8,128)}, u32[]{:S(2)}) copy-start(s32[32,512]{1,0:T(8,128)} %flag.1) | copy-start | bytes 196612
  65.8 10.0 %all-to-all-start.2 = ((f32[4,32,512]{2,1,0:T(8,128)}), f32[4,32,512]{2,1,0:T(8,128)S(1)}, u32[]{:S(2)}, u32[]{:S(2)}) async-start(f32[4,32,512]{2,1,0:T(8,128)} %dip.1), calls=%async_computation.2 | async-start | bytes 524288 | tf_op jit(solution)/shard_map/all_to_all | solution.py:473
  69.9 5.8 %copy-start.5 = (f32[32,512]{1,0:T(8,128)S(1)}, f32[32,512]{1,0:T(8,128)}, u32[]{:S(2)}) copy-start(f32[32,512]{1,0:T(8,128)} %slip.1) | copy-start | bytes 196612
  69.9 5.8 %copy-start.6 = (f32[32,512]{1,0:T(8,128)S(1)}, f32[32,512]{1,0:T(8,128)}, u32[]{:S(2)}) copy-start(f32[32,512]{1,0:T(8,128)} %rate.1) | copy-start | bytes 196612
  69.9 5.8 %copy-start.11 = (f32[32,512]{1,0:T(8,128)S(1)}, f32[32,512]{1,0:T(8,128)}, u32[]{:S(2)}) copy-start(f32[32,512]{1,0:T(8,128)} %prestress.1) | copy-start | bytes 196612

commit v5 on v3

--- a/solution.py
+++ b/solution.py
@@ -155,14 +155,17 @@
     return jnp.concatenate([h_a, even + odd, even - odd, h_d], axis=0).T
 
 
-def memory_part(history, p, q):
+def memory_weights(p, q):
     ks = rev_bits(p) + PS * iota((ROWS_DEV, COLS_DEV), 0)
     kd = q * COLS_DEV + iota((ROWS_DEV, COLS_DEV), 1)
     fs, fd = signed(ks, NS), signed(kd, ND)
     wave = (2.0 * math.pi) * jnp.sqrt(fs * fs + fd * fd)
     grow = jnp.exp(-0.15 * wave)
     ang = 0.9 * wave
-    z_re, z_im = grow * jnp.cos(ang), grow * jnp.sin(ang)
+    return grow * jnp.cos(ang), grow * jnp.sin(ang)
+
+
+def memory_part(z_re, z_im, history, q):
     w_re, w_im = 0.5 * z_re, 0.5 * z_im
     m_re, m_im = w_re * history(0, 0), w_re * history(0, 1)
     for lag in range(1, 8):
@@ -170,39 +173,41 @@
         m_re = m_re + w_re * history(lag, 0)
         m_im = m_im + w_re * history(lag, 1)
     both = jnp.concatenate([m_re, m_im], axis=0)
-    zero = jnp.zeros_like(both)
-    lower, upper = split(jnp.concatenate([both, zero], axis=0)), split(jnp.concatenate([zero, both], axis=0))
-    row = iota((COLS_DEV, COLS_DEV), 0)
-    from_col = jnp.where(q < 2, row, (COLS_DEV - row) & (COLS_DEV - 1))
-    perm = (iota((COLS_DEV, COLS_DEV), 1) == from_col).astype(f32).astype(bf16)
+    shifted = pltpu.roll(both, COLS_DEV - 1, 1)
+    near = [both[:, PS * i : PS * (i + 1)] for i in range(4)]
+    far = [shifted[:, PS * i : PS * (i + 1)] for i in range(4)]
+    blocks = [jnp.where(q < 2, near[i], far[3 - i]) for i in range(4)]
+    row = iota((PS, PS), 0)
+    perm = (iota((PS, PS), 1) == jnp.where(q < 2, row, PS - 1 - row)).astype(f32).astype(bf16)
     out = []
     for h in range(2):
-        even, odd = perm[2 * h * PS : (2 * h + 1) * PS], perm[(2 * h + 1) * PS : (2 * h + 2) * PS]
-        out.append((dot(even, lower[0], NT) + dot(odd, upper[0], NT)) + (dot(even, lower[1], NT) + dot(odd, upper[1], NT)))
+        hi, lo = split(jnp.concatenate(blocks[2 * h : 2 * h + 2], axis=0))
+        out.append(dot(perm, hi, NT) + dot(perm, lo, NT))
     return out
 
 
 def send_kernel(slip_in, rate_in, history_in, tables_in, turns_in, out, slip, rate, history, tables, turns, sems):
     p, q = position()
     lags = history.shape[0]
-    lag_copies = [pltpu.make_async_copy(history_in.at[i], history.at[i], sems.at[i]) for i in range(lags)]
     pairs = ((slip_in, slip), (rate_in, rate), (tables_in, tables), (turns_in, turns))
     copies = [pltpu.make_async_copy(src, dst, sems.at[lags + i]) for i, (src, dst) in enumerate(pairs)]
-    for copy in lag_copies + copies:
+    lag_copies = [pltpu.make_async_copy(history_in.at[i], history.at[i], sems.at[i]) for i in range(lags)]
+    for copy in copies + lag_copies:
         copy.start()
-
-    def read(lag, part):
-        if part == 0:
-            lag_copies[lag].wait()
-        return history[lag, part]
-
-    for h, part in enumerate(memory_part(read, p, q)):
-        out[pl.ds(4 + h, PS, stride=SEND), :] = part
+    z_re, z_im = memory_weights(p, q)
     for copy in copies:
         copy.wait()
     lines = slip_part(slip[...], rate[...], tables, lambda i, row: turns[i, pl.ds(row, 1), :], q)
     for i in range(4):
         out[pl.ds(i, PS, stride=SEND), :] = lines[PS * i : PS * (i + 1)]
+
+    def read(lag, part):
+        if part == 0:
+            lag_copies[lag].wait()
+        return history[lag, part]
+
+    for h, part in enumerate(memory_part(z_re, z_im, read, q)):
+        out[pl.ds(4 + h, PS, stride=SEND), :] = part
 
 
 def strike_part(lines, mems, first, first_t, twiddle, second, second_inv, mem_table, p, q):
@@ -303,17 +308,25 @@
     even = [s1 + s2, s1 + d2 - fix, s1 - s2, s1 - d2 - fix]
     odd = [d1 + d2, d1 - s2, d1 - d2, d1 + s2]
     evens, odds = [], []
-    for qd in range(QD):
-        for i, (ct, st) in enumerate(turn_rows(turns, qd)):
-            evens.append(ct * even[i] + st * odd[i])
-            odds.append(ct * odd[i] - st * even[i])
+    for i, (ct, st) in enumerate(turn_rows(turns, 0)):
+        evens.append(ct * even[i] + st * odd[i])
+        odds.append(ct * odd[i] - st * even[i])
+    evens, odds = split(jnp.concatenate(evens, axis=0)), split(jnp.concatenate(odds, axis=0))
+    turn = iota((1, COLS_DEV), 1) & 3
+    keep_even = jnp.where((turn & 1) == 0, 1.0, 0.0).astype(bf16)
+    keep_odd = jnp.where((turn & 1) == 1, 1.0, 0.0).astype(bf16)
+    flip_even = jnp.where(turn == 0, 1.0, jnp.where(turn == 2, -1.0, 0.0)).astype(bf16)
+    flip_odd = jnp.where(turn == 1, 1.0, jnp.where(turn == 3, -1.0, 0.0)).astype(bf16)
     f = 0.0
-    for x, k in ((evens, 0), (odds, 2)):
-        hi, lo = split(jnp.concatenate(x, axis=0))
+    for k, x, y, sign in ((0, evens, odds, flip_odd), (2, odds, evens, -flip_odd)):
+        hi, lo = [
+            jnp.concatenate([x[i] * keep_even, x[i] * keep_odd, x[i] * flip_even, y[i] * sign], axis=0) for i in range(2)
+        ]
         f = f + (dot(hi, tables[k], NT) + (dot(lo, tables[k], NT) + dot(hi, tables[k + 1], NT)))
+    f = [f[PS * i : PS * (i + 1)] for i in range(4)]
+    f = [f[0] + f[1], f[2] + f[3], f[0] - f[1], f[2] - f[3]]
     rows = 32
-    f = [[f[rows * (4 * qd + i) : rows * (4 * qd + i + 1)] for i in range(4)] for qd in range(QD)]
-    f = jnp.concatenate([jnp.concatenate(x, axis=1) for x in f], axis=0)
+    f = jnp.concatenate([jnp.concatenate([x[rows * i : rows * (i + 1)] for i in range(4)], axis=1) for x in f], axis=0)
     hi, lo = split(f)
     back = interleave(0)
     f = dot(hi, back) + dot(lo, back)
@@ -359,19 +372,20 @@
     return pltpu.roll(x, CAP, 1)
 
 
-def traction_kernel(recv, traction, spots):
+def traction_kernel(recv, traction, onehots, spots):
     value, hi, lo = unpack_rows(recv[pl.ds(4, PS, stride=BACK), :], roll_half)
-    spots[0], spots[1] = hi, lo
+    spots[...] = hi
     acc = jnp.zeros((2 * PS, PS), f32)
     for g in range(CAP // 4):
         onehot = column_onehot(lanes_of(lo, g))
+        onehots[g] = onehot
         acc = acc + traction_step(lanes_of(value, g), lanes_of(hi, g), onehot)
     acc = acc[:PS] + acc[PS:]
     traction[...] = jnp.concatenate([acc[32 * i : 32 * i + 32] for i in range(4)], axis=1)
 
 
 def owner_kernel(
-    shares, traction, spots, slip, rate, prestress, normal, flag, new_rate_out, stress_out, sampled, new_rate, stress, sems
+    shares, traction, onehots, spots, slip, rate, prestress, normal, flag, new_rate_out, stress_out, sampled, new_rate, stress, sems
 ):
     f = (shares[0] + shares[1]) + (shares[2] + shares[3])
     slip_new = slip[...] + RATE_DT * rate[...]
@@ -388,9 +402,9 @@
         copy.start()
     stacked = jnp.concatenate([fresh[:, PS * i : PS * (i + 1)] for i in range(4)], axis=0)
     parts = jnp.concatenate(split(stacked), axis=1)
-    hi, lo = spots[0], spots[1]
+    hi = spots[...]
     for g in range(CAP // 4):
-        got = sample_step(parts, lanes_of(hi, g), column_onehot(lanes_of(lo, g)))
+        got = sample_step(parts, lanes_of(hi, g), onehots[g])
         for i in range(4):
             sampled[4 * g + i : 4 * g + i + 1, :] = got[:, PS * i : PS * (i + 1)]
     sampled[CAP:PS, :] = roll_half(sampled[0:CAP, :])
@@ -458,16 +472,16 @@
     recv = over_strike(sent, BACK)
     shares = call(dip_kernel, sds((QD, ROWS_DEV, COLS_DEV)), (recv,), "dip", args=(tables, turns))
     shares = lax.all_to_all(shares, "dip", 0, 0, tiled=True)
-    traction, spots = call(
+    traction, onehots, spots = call(
         traction_kernel,
-        (sds((ROWS_DEV, COLS_DEV)), sds((2, CAP, PS), jnp.int32)),
+        (sds(slip.shape), sds((CAP // 4, PS, CHUNK), bf16), sds((CAP, PS), jnp.int32)),
         (recv,),
         "traction",
     )
     new_rate, stress, sampled = call(
         owner_kernel,
         (jax.ShapeDtypeStruct(slip.shape, f32), jax.ShapeDtypeStruct(slip.shape, f32), sds((PS, PS))),
-        (shares, traction, spots),
+        (shares, traction, onehots, spots),
         "owner",
         args=(slip, rate, prestress, normal_stress, fric_flag),
         far_outs=2,

time: 97.4 us -> 96.8 us (level)
  transfers between devices with their start and end apart: 2 -> 2, of which waited for: 2 -> 2; matrix products, arithmetic and copies ran while one was open for 0% -> 0% of each run, Pallas kernels for 3% -> 4%
where the time goes in v5:
time: 96.8 us; the launch traced here: 96.4 us
  blocking collectives  39.7 us (41%)
  starting transfers between devices  22.6 us (23%)
  waiting for transfers between devices  19.5 us (20%)
  Pallas kernels  13 us (13%)
  between operations  1.53 us (2%)
    all_to_all x2, blocking collectives, over_strike(): lax.all_to_all(x.reshape(PS * width // unit, unit, PS), STRIKE, 0, 0, til...  39.7 us
    all_to_all x1, starting transfers between devices, over_strike(): lax.all_to_all(x.reshape(PS * width // unit, unit, PS), STRIKE, 0, 0, til...  18.6 us
    all_to_all x1, waiting for transfers between devices, over_strike(): lax.all_to_all(x.reshape(PS * width // unit, unit, PS), STRIKE, 0, 0, til...  15.7 us
    pallas_call x7, Pallas kernels, call(): pl.pallas_call(kernel, out_shape=out_shape, in_specs=in_specs, out_specs=...  13 us
    all_to_all x1, starting transfers between devices, body(): shares = lax.all_to_all(shares, 'dip', 0, 0, tiled=True)  4.02 us
    all_to_all x1, waiting for transfers between devices, body(): shares = lax.all_to_all(shares, 'dip', 0, 0, tiled=True)  3.81 us
  transfers between devices with their start and end apart: 2, of which 2 were waited for; matrix products, arithmetic and copies ran while one was open for 0% of the time, Pallas kernels for 4%

profile of v5, /device:TPU:1, one launch (start us, length us, event | category | flops | bytes accessed | tf_op | source)
XLA Modules:
  0.0 96.4 jit_solution(10006274230752412532)
XLA Ops:
  0.6 0.0 copy-start.1
  0.6 0.0 copy-start.2
  0.7 0.0 copy-start.3
  0.7 0.0 copy-start.7
  0.7 0.0 copy-start.8
  0.7 0.0 copy-start.9
  0.7 0.0 copy-start.15
  0.7 0.0 copy-start.14
  0.7 0.0 copy-start.13
  0.7 3.3 %send.1 = f32[768,128]{1,0:T(8,128)} custom-call(f32[32,512]{1,0:T(8,128)} %slip.1, f32[32,512]{1,0:T(8,128)} %rate.1, f32[8,2,32,512]{3,2,1,0:T(8,128)} %history_in.1, bf16[4,128,512]{2,1,0:T(8,128)(2,1)} %constant.16.clone.tables_in.tables, f32[2,16,512]{2,1,0:T(8,128)} %constant.17.clone.turns_in.turns), custom_call_target="tpu_custom_call" | custom-call | tf_op jit(solution)/shard_map/send/pallas_call | solution.py:439
  4.0 0.0 copy-start
  4.0 0.0 copy-start.6
  4.0 18.6 %all-to-all-start = ((f32[384,2,128]{2,1,0:T(2,128)}), f32[384,2,128]{2,1,0:T(2,128)S(1)}, u32[]{:S(2)}, u32[]{:S(2)}) async-start(f32[384,2,128]{2,1,0:T(2,128)} %bitcast), calls=%async_computation | async-start | bytes 786432 | tf_op jit(solution)/shard_map/all_to_all | solution.py:456
  23.3 0.0 copy-done.15
  23.3 0.0 copy-done.14
  23.3 1.5 %route.1 = (f32[128,128]{1,0:T(8,128)S(1)}, s32[1,4096]{1,0:T(1,128)S(1)}) custom-call(s32[1,1]{1,0:T(1,128)S(6)} %copy.23.count, s32[1,4096]{1,0:T(1,128)S(1)} %bitcast.16, s32[1,4096]{1,0:T(1,128)S(1)} %copy-done.14, f32[1,4096]{1,0:T(1,128)S(1)} %copy-done.15), custom_call_target="tpu_custom_call" | custom-call | tf_op jit(solution)/shard_map/route/pallas_call | solution.py:439
  24.8 15.7 %all-to-all-done = f32[384,2,128]{2,1,0:T(2,128)S(1)} async-done(((f32[384,2,128]{2,1,0:T(2,128)}), f32[384,2,128]{2,1,0:T(2,128)S(1)}, u32[]{:S(2)}, u32[]{:S(2)}) %all-to-all-start) | async-done | bytes 393248 | tf_op jit(solution)/shard_map/all_to_all | solution.py:456
  40.5 0.0 copy-done.2
  40.5 0.0 copy-start.4
  40.5 0.0 copy-start.5
  40.5 0.0 copy-start.10
  40.5 0.0 copy-start.11
  40.6 0.0 copy-start.12
  40.6 1.7 %strike.1 = f32[640,128]{1,0:T(8,128)S(1)} custom-call(f32[768,128]{1,0:T(8,128)S(1)} %bitcast.13, f32[128,128]{1,0:T(8,128)S(1)} %get-tuple-element.11.outbox, bf16[2,256,128]{2,1,0:T(8,128)(2,1)S(1)} %copy-done.9, bf16[2,128,256]{2,1,0:T(8,128)(2,1)S(1)} %copy-done.8, f32[2,128,128]{2,1,0:T(8,128)S(1)} %copy-done.7, bf16[2,256,256]{2,1,0:T(8,128)(2,1)S(1)} %copy-done.3, ...), custom_call_target="tpu_custom_call" | custom-call | tf_op jit(solution)/shard_map/strike/pallas_call | solution.py:439
  42.2 21.7 %all_to_all.20 = f32[640,1,128]{2,1,0:T(1,128)S(1)} all-to-all(f32[640,1,128]{2,1,0:T(1,128)S(1)} %bitcast.14), channel_id=1, replica_groups=mesh['z'=8,'y'=8,'c'=2,'dip'=4] {'z','y','c'}, dimensions={0} | all-to-all | bytes 655360 | tf_op jit(solution)/shard_map/all_to_all | solution.py:456
  63.9 2.3 %dip.1 = f32[4,32,512]{2,1,0:T(8,128)} custom-call(f32[640,128]{1,0:T(8,128)S(1)} %bitcast.11, bf16[4,128,512]{2,1,0:T(8,128)(2,1)S(1)} %copy-done, f32[2,16,512]{2,1,0:T(8,128)S(1)} %copy-done.6), custom_call_target="tpu_custom_call" | custom-call | tf_op jit(solution)/shard_map/dip/pallas_call | solution.py:439
  66.2 4.0 %all-to-all-start.2 = ((f32[4,32,512]{2,1,0:T(8,128)}), f32[4,32,512]{2,1,0:T(8,128)S(1)}, u32[]{:S(2)}, u32[]{:S(2)}) async-start(f32[4,32,512]{2,1,0:T(8,128)} %dip.1), calls=%async_computation.2 | async-start | bytes 524288 | tf_op jit(solution)/shard_map/all_to_all | solution.py:474
  70.2 2.0 %traction.1 = (f32[32,512]{1,0:T(8,128)S(1)}, bf16[16,128,512]{2,1,0:T(8,128)(2,1)S(1)}, s32[64,128]{1,0:T(8,128)S(1)}) custom-call(f32[640,128]{1,0:T(8,128)S(1)} %bitcast.12), custom_call_target="tpu_custom_call" | custom-call | tf_op jit(solution)/shard_map/traction/pallas_call | solution.py:439
  72.2 3.8 %all-to-all-done.2.shares = f32[4,32,512]{2,1,0:T(8,128)S(1)} async-done(((f32[4,32,512]{2,1,0:T(8,128)}), f32[4,32,512]{2,1,0:T(8,128)S(1)}, u32[]{:S(2)}, u32[]{:S(2)}) %all-to-all-start.2) | async-done | bytes 262176 | tf_op jit(solution)/shard_map/all_to_all | solution.py:474
  76.1 0.9 owner.1
  77.0 18.1 %all_to_all.21 = f32[128,1,128]{2,1,0:T(1,128)S(1)} all-to-all(f32[128,1,128]{2,1,0:T(1,128)S(1)} %bitcast.18), channel_id=1, replica_groups=mesh['z'=8,'y'=8,'c'=2,'dip'=4] {'z','y','c'}, dimensions={0} | all-to-all | bytes 131072 | tf_op jit(solution)/shard_map/all_to_all | solution.py:456
  95.1 1.3 %back.1 = f32[1,4096]{1,0:T(1,128)} custom-call(s32[1,1]{1,0:T(1,128)S(6)} %copy.23.count, f32[128,128]{1,0:T(8,128)S(1)} %bitcast.15, s32[1,4096]{1,0:T(1,128)S(1)} %get-tuple-element.18.rank, s32[1,4096]{1,0:T(1,128)S(1)} %bitcast.17), custom_call_target="tpu_custom_call" | custom-call | tf_op jit(solution)/shard_map/back/pallas_call | solution.py:439
  (13 shorter events, 0.0 us)
Async XLA Ops:
  0.6 39.8 %copy-start.1 = (bf16[8,64,256]{2,1,0:T(8,128)(2,1)S(1)}, bf16[8,64,256]{2,1,0:T(8,128)(2,1)}, u32[]{:S(2)}) copy-start(bf16[8,64,256]{2,1,0:T(8,128)(2,1)} %constant.23.clone.mem_table) | copy-start | bytes 786436
  0.6 39.8 %copy-start.2 = (bf16[2,256,256]{2,1,0:T(8,128)(2,1)S(1)}, bf16[2,256,256]{2,1,0:T(8,128)(2,1)}, u32[]{:S(2)}) copy-start(bf16[2,256,256]{2,1,0:T(8,128)(2,1)} %constant.22.clone.second_inv) | copy-start | bytes 786436
  0.7 39.8 %copy-start.3 = (bf16[2,256,256]{2,1,0:T(8,128)(2,1)S(1)}, bf16[2,256,256]{2,1,0:T(8,128)(2,1)}, u32[]{:S(2)}) copy-start(bf16[2,256,256]{2,1,0:T(8,128)(2,1)} %constant.21.clone.second) | copy-start | bytes 786436
  0.7 39.8 %copy-start.7 = (f32[2,128,128]{2,1,0:T(8,128)S(1)}, f32[2,128,128]{2,1,0:T(8,128)}, u32[]{:S(2)}) copy-start(f32[2,128,128]{2,1,0:T(8,128)} %constant.20.clone.twiddle) | copy-start | bytes 393220
  0.7 39.8 %copy-start.8 = (bf16[2,128,256]{2,1,0:T(8,128)(2,1)S(1)}, bf16[2,128,256]{2,1,0:T(8,128)(2,1)}, u32[]{:S(2)}) copy-start(bf16[2,128,256]{2,1,0:T(8,128)(2,1)} %constant.19.clone.first_t) | copy-start | bytes 393220
  0.7 39.8 %copy-start.9 = (bf16[2,256,128]{2,1,0:T(8,128)(2,1)S(1)}, bf16[2,256,128]{2,1,0:T(8,128)(2,1)}, u32[]{:S(2)}) copy-start(bf16[2,256,128]{2,1,0:T(8,128)(2,1)} %constant.18.clone.first) | copy-start | bytes 393220
  0.7 22.6 %copy-start.15 = (f32[1,4096]{1,0:T(1,128)S(1)}, f32[1,4096]{1,0:T(1,128)}, u32[]{:S(2)}) copy-start(f32[1,4096]{1,0:T(1,128)} %value.1) | copy-start | bytes 49156
  0.7 22.6 %copy-start.14 = (s32[1,4096]{1,0:T(1,128)S(1)}, s32[1,4096]{1,0:T(1,128)}, u32[]{:S(2)}) copy-start(s32[1,4096]{1,0:T(1,128)} %node.1) | copy-start | bytes 49156
  0.7 22.6 %copy-start.13 = (s32[1,4096,1]{1,2,0:T(1,128)S(1)}, s32[1,4096,1]{1,2,0:T(1,128)}, u32[]{:S(2)}) copy-start(s32[1,4096,1]{1,2,0:T(1,128)} %param.24) | copy-start | bytes 49156
  4.0 59.9 %copy-start = (bf16[4,128,512]{2,1,0:T(8,128)(2,1)S(1)}, bf16[4,128,512]{2,1,0:T(8,128)(2,1)}, u32[]{:S(2)}) copy-start(bf16[4,128,512]{2,1,0:T(8,128)(2,1)} %constant.16.clone.tables_in.tables) | copy-start | bytes 1572868
  4.0 59.9 %copy-start.6 = (f32[2,16,512]{2,1,0:T(8,128)S(1)}, f32[2,16,512]{2,1,0:T(8,128)}, u32[]{:S(2)}) copy-start(f32[2,16,512]{2,1,0:T(8,128)} %constant.17.clone.turns_in.turns) | copy-start | bytes 196612
  4.0 36.4 %all-to-all-start = ((f32[384,2,128]{2,1,0:T(2,128)}), f32[384,2,128]{2,1,0:T(2,128)S(1)}, u32[]{:S(2)}, u32[]{:S(2)}) async-start(f32[384,2,128]{2,1,0:T(2,128)} %bitcast), calls=%async_computation | async-start | bytes 786432 | tf_op jit(solution)/shard_map/all_to_all | solution.py:456
  40.5 35.5 %copy-start.4 = (f32[32,512]{1,0:T(8,128)S(1)}, f32[32,512]{1,0:T(8,128)}, u32[]{:S(2)}) copy-start(f32[32,512]{1,0:T(8,128)} %slip.1) | copy-start | bytes 196612
  40.5 35.5 %copy-start.5 = (f32[32,512]{1,0:T(8,128)S(1)}, f32[32,512]{1,0:T(8,128)}, u32[]{:S(2)}) copy-start(f32[32,512]{1,0:T(8,128)} %rate.1) | copy-start | bytes 196612
  40.5 35.5 %copy-start.10 = (f32[32,512]{1,0:T(8,128)S(1)}, f32[32,512]{1,0:T(8,128)}, u32[]{:S(2)}) copy-start(f32[32,512]{1,0:T(8,128)} %prestress.1) | copy-start | bytes 196612
  40.5 35.5 %copy-start.11 = (f32[32,512]{1,0:T(8,128)S(1)}, f32[32,512]{1,0:T(8,128)}, u32[]{:S(2)}) copy-start(f32[32,512]{1,0:T(8,128)} %normal.1) | copy-start | bytes 196612
  40.6 35.5 %copy-start.12 = (s32[32,512]{1,0:T(8,128)S(1)}, s32[32,512]{1,0:T(8,128)}, u32[]{:S(2)}) copy-start(s32[32,512]{1,0:T(8,128)} %flag.1) | copy-start | bytes 196612
  66.2 9.9 %all-to-all-start.2 = ((f32[4,32,512]{2,1,0:T(8,128)}), f32[4,32,512]{2,1,0:T(8,128)S(1)}, u32[]{:S(2)}, u32[]{:S(2)}) async-start(f32[4,32,512]{2,1,0:T(8,128)} %dip.1), calls=%async_computation.2 | async-start | bytes 524288 | tf_op jit(solution)/shard_map/all_to_all | solution.py:474

commit v6 on v4

--- a/solution.py
+++ b/solution.py
@@ -114,9 +114,9 @@
     return [(turns(0, 4 * q + b), turns(1, 4 * q + b)) for b in range(4)]
 
 
-def interleave(dims):
-    pos = iota((COLS_DEV, COLS_DEV), dims)
-    return (iota((COLS_DEV, COLS_DEV), 1 - dims) == 4 * (pos & (PS - 1)) + (pos >> 7)).astype(f32).astype(bf16)
+def interleave():
+    pos = iota((COLS_DEV, COLS_DEV), 1)
+    return (iota((COLS_DEV, COLS_DEV), 0) == 4 * (pos & (PS - 1)) + (pos >> 7)).astype(f32).astype(bf16)
 
 
 def by_class(x):
@@ -131,19 +131,22 @@
     return jnp.where(ell == 0, 1 - (q & 1), 1 - ((q ^ (q >> 1)) & 1)) == 1
 
 
-def slip_part(own, other, tables, turns, q):
-    parts = jnp.concatenate(split(own) + split(other), axis=0)
-    parts = dot(parts, interleave(1)).astype(bf16)
-    own_hi, own_lo, other_hi, other_lo = [by_class(parts[ROWS_DEV * i : ROWS_DEV * (i + 1)]) for i in range(4)]
-    hi, lo = jnp.concatenate([own_hi, other_hi], axis=0), jnp.concatenate([own_lo, other_lo], axis=0)
+def dip_forward_part(x, perm, tables, turns, q):
+    parts = dot(jnp.concatenate(split(x), axis=0), perm).astype(bf16)
+    hi, lo = by_class(parts[:ROWS_DEV]), by_class(parts[ROWS_DEV:])
     c = dot(hi, tables[0]) + (dot(lo, tables[0]) + dot(hi, tables[1]))
     s = dot(hi, tables[2]) + (dot(lo, tables[2]) + dot(hi, tables[3]))
-    cs, ss = [0.0] * 4, [0.0] * 4
-    for block, block_q in enumerate((q, q ^ 1)):
-        for b, (ct, st) in enumerate(turn_rows(turns, block_q)):
-            rows = slice(PS * block + 32 * b, PS * block + 32 * b + 32)
-            cs[b] = cs[b] + (ct * c[rows] - st * s[rows])
-            ss[b] = ss[b] + (st * c[rows] + ct * s[rows])
+    cs, ss = [], []
+    for b, (ct, st) in enumerate(turn_rows(turns, q)):
+        c_b, s_b = c[32 * b : 32 * b + 32], s[32 * b : 32 * b + 32]
+        cs.append(ct * c_b - st * s_b)
+        ss.append(st * c_b + ct * s_b)
+    return jnp.concatenate(cs + ss, axis=0)
+
+
+def slip_part(sums, q):
+    sums = [sums[32 * i : 32 * i + 32] for i in range(8)]
+    cs, ss = sums[:4], sums[4:]
     c_even, c_odd = cs[0] + cs[2], cs[1] + cs[3]
     s_sum = (ss[0] + ss[2]) + (ss[1] + ss[3])
     ell = iota((ROWS_DEV, COLS_DEV), 1)
@@ -157,14 +160,17 @@
     return [jnp.concatenate(both[2 * h : 2 * h + 2], axis=0).T for h in range(2)]
 
 
-def memory_part(history, p, q):
+def memory_weights(p, q):
     ks = rev_bits(p) + PS * iota((ROWS_DEV, COLS_DEV), 0)
     kd = q * COLS_DEV + iota((ROWS_DEV, COLS_DEV), 1)
     fs, fd = signed(ks, NS), signed(kd, ND)
     wave = (2.0 * math.pi) * jnp.sqrt(fs * fs + fd * fd)
     grow = jnp.exp(-0.15 * wave)
     ang = 0.9 * wave
-    z_re, z_im = grow * jnp.cos(ang), grow * jnp.sin(ang)
+    return grow * jnp.cos(ang), grow * jnp.sin(ang)
+
+
+def memory_part(z_re, z_im, history, q):
     w_re, w_im = 0.5 * z_re, 0.5 * z_im
     m_re, m_im = w_re * history(0, 0), w_re * history(0, 1)
     for lag in range(1, 8):
@@ -172,36 +178,48 @@
         m_re = m_re + w_re * history(lag, 0)
         m_im = m_im + w_re * history(lag, 1)
     both = jnp.concatenate([m_re, m_im], axis=0)
-    zero = jnp.zeros_like(both)
-    lower, upper = split(jnp.concatenate([both, zero], axis=0)), split(jnp.concatenate([zero, both], axis=0))
-    row = iota((COLS_DEV, COLS_DEV), 0)
-    from_col = jnp.where(q < 2, row, (COLS_DEV - row) & (COLS_DEV - 1))
-    perm = (iota((COLS_DEV, COLS_DEV), 1) == from_col).astype(f32).astype(bf16)
+    shifted = pltpu.roll(both, COLS_DEV - 1, 1)
+    near = [both[:, PS * i : PS * (i + 1)] for i in range(4)]
+    far = [shifted[:, PS * i : PS * (i + 1)] for i in range(4)]
+    blocks = [jnp.where(q < 2, near[i], far[3 - i]) for i in range(4)]
+    row = iota((PS, PS), 0)
+    perm = (iota((PS, PS), 1) == jnp.where(q < 2, row, PS - 1 - row)).astype(f32).astype(bf16)
     out = []
     for h in range(2):
-        even, odd = perm[2 * h * PS : (2 * h + 1) * PS], perm[(2 * h + 1) * PS : (2 * h + 2) * PS]
-        out.append((dot(even, lower[0], NT) + dot(odd, upper[0], NT)) + (dot(even, lower[1], NT) + dot(odd, upper[1], NT)))
+        hi, lo = split(jnp.concatenate(blocks[2 * h : 2 * h + 2], axis=0))
+        out.append(dot(perm, hi, NT) + dot(perm, lo, NT))
     return out
 
 
-def memory_kernel(history_in, out, history, sems):
+def near_kernel(history_in, tables_in, turns_in, own, mem, sums, perm, tables, turns, history, sems):
     p, q = position()
-    copies = [pltpu.make_async_copy(history_in.at[i], history.at[i], sems.at[i]) for i in range(history.shape[0])]
-    for copy in copies:
+    lags = history.shape[0]
+    far_tables = [
+        pltpu.make_async_copy(tables_in, tables, sems.at[lags]),
+        pltpu.make_async_copy(turns_in, turns, sems.at[lags + 1]),
+    ]
+    copies = [pltpu.make_async_copy(history_in.at[i], history.at[i], sems.at[i]) for i in range(lags)]
+    for copy in far_tables + copies:
         copy.start()
+    z_re, z_im = memory_weights(p, q)
+    perm[...] = interleave()
+    for copy in far_tables:
+        copy.wait()
+    sums[...] = dip_forward_part(own[...], perm[...], tables, lambda i, row: turns[i, pl.ds(row, 1), :], q)
 
     def read(lag, part):
         if part == 0:
             copies[lag].wait()
         return history[lag, part]
 
-    for h, part in enumerate(memory_part(read, p, q)):
-        out[PS * h : PS * (h + 1), :] = part
-
-
-def send_kernel(own, other, mem, tables, turns, out):
+    for h, part in enumerate(memory_part(z_re, z_im, read, q)):
+        mem[PS * h : PS * (h + 1), :] = part
+
+
+def send_kernel(other, mem, sums, perm, tables, turns, out):
     q = position()[1]
-    lines = slip_part(own[...], other[...], tables, lambda i, row: turns[i, pl.ds(row, 1), :], q)
+    far = dip_forward_part(other[...], perm[...], tables, lambda i, row: turns[i, pl.ds(row, 1), :], q ^ 1)
+    lines = slip_part(sums[...] + far, q)
     for h in range(2):
         out[pl.ds(h, PS, stride=SEND), :] = lines[h]
         out[pl.ds(2 + h, PS, stride=SEND), :] = mem[PS * h : PS * (h + 1), :]
@@ -293,7 +311,7 @@
     out[...], rank[...] = route_part(dest[...], node[...], value[...], count[0, 0])
 
 
-def dip_inverse_part(lines, tables, turns, q):
+def dip_inverse_part(lines, tables, turns, perm, q):
     lines = [x.T for x in lines]
     t0, t1 = [
         jnp.concatenate([lines[i >> 1][64 * (i & 1) + 32 * slot : 64 * (i & 1) + 32 * slot + 32] for i in range(4)], axis=1)
@@ -308,26 +326,33 @@
     even = [s1 + s2, s1 + d2 - fix, s1 - s2, s1 - d2 - fix]
     odd = [d1 + d2, d1 - s2, d1 - d2, d1 + s2]
     evens, odds = [], []
-    for qd in range(QD):
-        for i, (ct, st) in enumerate(turn_rows(turns, qd)):
-            evens.append(ct * even[i] + st * odd[i])
-            odds.append(ct * odd[i] - st * even[i])
+    for i, (ct, st) in enumerate(turn_rows(turns, 0)):
+        evens.append(ct * even[i] + st * odd[i])
+        odds.append(ct * odd[i] - st * even[i])
+    evens, odds = split(jnp.concatenate(evens, axis=0)), split(jnp.concatenate(odds, axis=0))
+    turn = iota((1, COLS_DEV), 1) & 3
+    keep_even = jnp.where((turn & 1) == 0, 1.0, 0.0).astype(bf16)
+    keep_odd = jnp.where((turn & 1) == 1, 1.0, 0.0).astype(bf16)
+    flip_even = jnp.where(turn == 0, 1.0, jnp.where(turn == 2, -1.0, 0.0)).astype(bf16)
+    flip_odd = jnp.where(turn == 1, 1.0, jnp.where(turn == 3, -1.0, 0.0)).astype(bf16)
     f = 0.0
-    for x, k in ((evens, 0), (odds, 2)):
-        hi, lo = split(jnp.concatenate(x, axis=0))
+    for k, x, y, sign in ((0, evens, odds, flip_odd), (2, odds, evens, -flip_odd)):
+        hi, lo = [
+            jnp.concatenate([x[i] * keep_even, x[i] * keep_odd, x[i] * flip_even, y[i] * sign], axis=0) for i in range(2)
+        ]
         f = f + (dot(hi, tables[k], NT) + (dot(lo, tables[k], NT) + dot(hi, tables[k + 1], NT)))
+    f = [f[PS * i : PS * (i + 1)] for i in range(4)]
+    f = [f[0] + f[1], f[2] + f[3], f[0] - f[1], f[2] - f[3]]
     rows = 32
-    f = [[f[rows * (4 * qd + i) : rows * (4 * qd + i + 1)] for i in range(4)] for qd in range(QD)]
-    f = jnp.concatenate([jnp.concatenate(x, axis=1) for x in f], axis=0)
+    f = jnp.concatenate([jnp.concatenate([x[rows * i : rows * (i + 1)] for i in range(4)], axis=1) for x in f], axis=0)
     hi, lo = split(f)
-    back = interleave(0)
-    f = dot(hi, back) + dot(lo, back)
+    f = dot(hi, perm, NT) + dot(lo, perm, NT)
     return [f[rows * qd : rows * (qd + 1)] for qd in range(QD)]
 
 
-def dip_kernel(recv, tables, turns, out):
+def dip_kernel(recv, perm, tables, turns, out):
     lines = [recv[pl.ds(h, PS, stride=BACK), :] for h in range(2)]
-    shares = dip_inverse_part(lines, tables, lambda i, row: turns[i, row : row + 1, :], position()[1])
+    shares = dip_inverse_part(lines, tables, lambda i, row: turns[i, row : row + 1, :], perm[...], position()[1])
     for qd, share in enumerate(shares):
         out[qd] = share
 
@@ -364,19 +389,20 @@
     return pltpu.roll(x, CAP, 1)
 
 
-def traction_kernel(recv, traction, spots):
+def traction_kernel(recv, traction, onehots, spots):
     value, hi, lo = unpack_rows(recv[pl.ds(2, PS, stride=BACK), :], roll_half)
-    spots[0], spots[1] = hi, lo
+    spots[...] = hi
     acc = jnp.zeros((2 * PS, PS), f32)
     for g in range(CAP // 4):
         onehot = column_onehot(lanes_of(lo, g))
+        onehots[g] = onehot
         acc = acc + traction_step(lanes_of(value, g), lanes_of(hi, g), onehot)
     acc = acc[:PS] + acc[PS:]
     traction[...] = jnp.concatenate([acc[32 * i : 32 * i + 32] for i in range(4)], axis=1)
 
 
 def owner_kernel(
-    shares, traction, spots, slip, rate, prestress, normal, flag, new_rate_out, stress_out, sampled, new_rate, stress, sems
+    shares, traction, onehots, spots, slip, rate, prestress, normal, flag, new_rate_out, stress_out, sampled, new_rate, stress, sems
 ):
     f = (shares[0] + shares[1]) + (shares[2] + shares[3])
     slip_new = slip[...] + RATE_DT * rate[...]
@@ -393,9 +419,9 @@
         copy.start()
     stacked = jnp.concatenate([fresh[:, PS * i : PS * (i + 1)] for i in range(4)], axis=0)
     parts = jnp.concatenate(split(stacked), axis=1)
-    hi, lo = spots[0], spots[1]
+    hi = spots[...]
     for g in range(CAP // 4):
-        got = sample_step(parts, lanes_of(hi, g), column_onehot(lanes_of(lo, g)))
+        got = sample_step(parts, lanes_of(hi, g), onehots[g])
         for i in range(4):
             sampled[4 * g + i : 4 * g + i + 1, :] = got[:, PS * i : PS * (i + 1)]
     sampled[CAP:PS, :] = roll_half(sampled[0:CAP, :])
@@ -454,33 +480,39 @@
 
     slip_new = slip + RATE_DT * rate
     other = lax.ppermute(slip_new, "dip", [(i, i ^ 1) for i in range(QD)])
-    mem = call(
-        memory_kernel,
-        sds((2 * PS, PS)),
-        (),
-        "memory",
-        far=(history,),
-        scratch=[sds(history.shape), pltpu.SemaphoreType.DMA((history.shape[0],))],
+    mem, sums, perm, tables, turns = call(
+        near_kernel,
+        (
+            sds((2 * PS, PS)),
+            sds((8 * ROWS_DEV, COLS_DEV)),
+            sds((COLS_DEV, COLS_DEV), bf16),
+            sds(tables.shape, bf16),
+            sds(turns.shape),
+        ),
+        (slip_new,),
+        "near",
+        far=(history, tables, turns),
+        scratch=[sds(history.shape), pltpu.SemaphoreType.DMA((history.shape[0] + 2,))],
     )
-    sent = call(send_kernel, sds((PS * SEND, PS)), (slip_new, other, mem), "send", args=(tables, turns))
+    sent = call(send_kernel, sds((PS * SEND, PS)), (other, mem, sums, perm, tables, turns), "send")
     recv = over_strike(sent, SEND)
     box, rank = call(
         route_kernel, (sds((PS, PS)), sds((1, ROWS), jnp.int32)), (), "route", (fe_count,), (dest, row_node, fe_traction)
     )
     sent = call(strike_kernel, sds((PS * BACK, PS)), (recv, box), "strike", args=strike)
     recv = over_strike(sent, BACK)
-    shares = call(dip_kernel, sds((QD, ROWS_DEV, COLS_DEV)), (recv,), "dip", args=(tables, turns))
+    shares = call(dip_kernel, sds((QD, ROWS_DEV, COLS_DEV)), (recv, perm, tables, turns), "dip")
     shares = lax.all_to_all(shares, "dip", 0, 0, tiled=True)
-    traction, spots = call(
+    traction, onehots, spots = call(
         traction_kernel,
-        (sds((ROWS_DEV, COLS_DEV)), sds((2, CAP, PS), jnp.int32)),
+        (sds(slip.shape), sds((CAP // 4, PS, CHUNK), bf16), sds((CAP, PS), jnp.int32)),
         (recv,),
         "traction",
     )
     new_rate, stress, sampled = call(
         owner_kernel,
         (jax.ShapeDtypeStruct(slip.shape, f32), jax.ShapeDtypeStruct(slip.shape, f32), sds((PS, PS))),
-        (shares, traction, spots),
+        (shares, traction, onehots, spots),
         "owner",
         args=(slip, rate, prestress, normal_stress, fric_flag),
         far_outs=2,

time: 97.3 us -> 96.3 us (0.990)
  transfers between devices with their start and end apart: 3 -> 3, of which waited for: 2 -> 2; matrix products, arithmetic and copies ran while one was open for 0% -> 0% of each run, Pallas kernels for 5% -> 6%
where the time goes in v6:
time: 96.3 us; the launch traced here: 95.9 us
  blocking collectives  36.9 us (38%)
  starting transfers between devices  26.5 us (28%)
  waiting for transfers between devices  16.8 us (17%)
  Pallas kernels  13.1 us (14%)
  between operations  1.53 us (2%)
    all_to_all x2, blocking collectives, over_strike(): lax.all_to_all(x.reshape(PS * width // unit, unit, PS), STRIKE, 0, 0, til...  36.9 us
    all_to_all x1, starting transfers between devices, over_strike(): lax.all_to_all(x.reshape(PS * width // unit, unit, PS), STRIKE, 0, 0, til...  18.4 us
    pallas_call x8, Pallas kernels, call(): pl.pallas_call(kernel, out_shape=out_shape, in_specs=in_specs, out_specs=...  13.1 us
    all_to_all x1, waiting for transfers between devices, over_strike(): lax.all_to_all(x.reshape(PS * width // unit, unit, PS), STRIKE, 0, 0, til...  13.1 us
    ppermute x1, starting transfers between devices, body(): other = lax.ppermute(slip_new, 'dip', [(i, i ^ 1) for i in range(QD)])  4.07 us
    all_to_all x1, starting transfers between devices, body(): shares = lax.all_to_all(shares, 'dip', 0, 0, tiled=True)  4.01 us
    all_to_all x1, waiting for transfers between devices, body(): shares = lax.all_to_all(shares, 'dip', 0, 0, tiled=True)  3.78 us
  transfers between devices with their start and end apart: 3, of which 2 were waited for; matrix products, arithmetic and copies ran while one was open for 0% of the time, Pallas kernels for 6%

profile of v6, /device:TPU:1, one launch (start us, length us, event | category | flops | bytes accessed | tf_op | source)
XLA Modules:
  0.0 95.9 jit_solution(2388157342892320122)
XLA Ops:
  0.6 0.9 multiply_add_fusion.own
  1.5 0.0 copy-start.11
  1.5 0.0 copy-start.12
  1.5 0.0 copy-start.13
  1.6 0.0 copy-start.2
  1.6 0.0 copy-start.3
  1.6 0.0 copy-start.4
  1.6 0.0 copy-start.5
  1.6 0.0 copy-start.6
  1.6 0.0 copy-start.7
  1.6 4.1 %collective-permute-start = (f32[32,512]{1,0:T(8,128)S(1)}, f32[32,512]{1,0:T(8,128)S(1)}, u32[]{:S(2)}, u32[]{:S(2)}) collective-permute-start(f32[32,512]{1,0:T(8,128)S(1)} %multiply_add_fusion.own), channel_id=1, source_target_pairs={{0,1},{1,0},{2,3},{3,2},{4,5},{5,4},{6,7},{7,6},{8,9},{9,8},{10,11... | collective-permute-start | bytes 196616 | tf_op jit(solution)/shard_map/ppermute | solution.py:482
  5.7 2.2 %near.1 = (f32[256,128]{1,0:T(8,128)S(1)}, f32[256,512]{1,0:T(8,128)S(1)}, bf16[512,512]{1,0:T(8,128)(2,1)S(1)}, bf16[4,128,512]{2,1,0:T(8,128)(2,1)S(1)}, f32[2,16,512]{2,1,0:T(8,128)S(1)}) custom-call(f32[8,2,32,512]{3,2,1,0:T(8,128)} %history_in.1, bf16[4,128,512]{2,1,0:T(8,128)(2,1)} %constant.18.clone.tables_in, f32[2,16,512]{2,1,0:T(8,128)} %constant.19.clone.turns_in, ...), custom_call_target="tpu_custom_call" | custom-call | tf_op jit(solution)/shard_map/near/pallas_call | solution.py:456
  7.9 0.0 collective-permute-done.other
  7.9 1.4 %send.1 = f32[512,128]{1,0:T(8,128)} custom-call(f32[32,512]{1,0:T(8,128)S(1)} %collective-permute-done.other, f32[256,128]{1,0:T(8,128)S(1)} %get-tuple-element.16.mem, f32[256,512]{1,0:T(8,128)S(1)} %get-tuple-element.17.sums, bf16[512,512]{1,0:T(8,128)(2,1)S(1)} %get-tuple-element.18.perm, bf16[4,128,512]{2,1,0:T(8,128)(2,1)S(1)} %get-tuple-element.19.tables, ...), custom_call_target="tpu_custom_call" | custom-call | tf_op jit(solution)/shard_map/send/pallas_call | solution.py:456
  9.3 18.4 %all-to-all-start = ((f32[128,4,128]{2,1,0:T(4,128)}), f32[128,4,128]{2,1,0:T(4,128)S(1)}, u32[]{:S(2)}, u32[]{:S(2)}) async-start(f32[128,4,128]{2,1,0:T(4,128)} %bitcast), calls=%async_computation | async-start | bytes 524288 | tf_op jit(solution)/shard_map/all_to_all | solution.py:473
  28.4 1.5 %route.1 = (f32[128,128]{1,0:T(8,128)S(1)}, s32[1,4096]{1,0:T(1,128)S(1)}) custom-call(s32[1,1]{1,0:T(1,128)S(6)} %copy.23.count, s32[1,4096]{1,0:T(1,128)S(1)} %bitcast.16, s32[1,4096]{1,0:T(1,128)S(1)} %copy-done.12, f32[1,4096]{1,0:T(1,128)S(1)} %copy-done.13), custom_call_target="tpu_custom_call" | custom-call | tf_op jit(solution)/shard_map/route/pallas_call | solution.py:456
  29.9 13.1 %all-to-all-done = f32[128,4,128]{2,1,0:T(4,128)S(1)} async-done(((f32[128,4,128]{2,1,0:T(4,128)}), f32[128,4,128]{2,1,0:T(4,128)S(1)}, u32[]{:S(2)}, u32[]{:S(2)}) %all-to-all-start) | async-done | bytes 262176 | tf_op jit(solution)/shard_map/all_to_all | solution.py:473
  43.0 0.0 copy-done.2
  43.0 0.0 copy-start
  43.0 0.0 copy-start.1
  43.0 0.0 copy-start.8
  43.0 0.0 copy-start.9
  43.0 0.0 copy-start.10
  43.1 1.2 %strike.1 = f32[384,128]{1,0:T(8,128)S(1)} custom-call(f32[512,128]{1,0:T(8,128)S(1)} %bitcast.13, f32[128,128]{1,0:T(8,128)S(1)} %get-tuple-element.21.outbox, bf16[2,256,128]{2,1,0:T(8,128)(2,1)S(1)} %copy-done.7, bf16[2,128,256]{2,1,0:T(8,128)(2,1)S(1)} %copy-done.6, f32[2,128,128]{2,1,0:T(8,128)S(1)} %copy-done.5, bf16[2,256,256]{2,1,0:T(8,128)(2,1)S(1)} %copy-done.4, ...), custom_call_target="tpu_custom_call" | custom-call | tf_op jit(solution)/shard_map/strike/pallas_call | solution.py:456
  44.3 19.0 %all_to_all.20 = f32[384,1,128]{2,1,0:T(1,128)S(1)} all-to-all(f32[384,1,128]{2,1,0:T(1,128)S(1)} %bitcast.14), channel_id=1, replica_groups=mesh['z'=8,'y'=8,'c'=2,'dip'=4] {'z','y','c'}, dimensions={0} | all-to-all | bytes 393216 | tf_op jit(solution)/shard_map/all_to_all | solution.py:473
  63.2 2.6 %dip.1 = f32[4,32,512]{2,1,0:T(8,128)} custom-call(f32[384,128]{1,0:T(8,128)S(1)} %bitcast.11, bf16[512,512]{1,0:T(8,128)(2,1)S(1)} %get-tuple-element.18.perm, bf16[4,128,512]{2,1,0:T(8,128)(2,1)S(1)} %get-tuple-element.19.tables, f32[2,16,512]{2,1,0:T(8,128)S(1)} %get-tuple-element.20.turns), custom_call_target="tpu_custom_call" | custom-call | tf_op jit(solution)/shard_map/dip/pallas_call | solution.py:456
  65.8 4.0 %all-to-all-start.2 = ((f32[4,32,512]{2,1,0:T(8,128)}), f32[4,32,512]{2,1,0:T(8,128)S(1)}, u32[]{:S(2)}, u32[]{:S(2)}) async-start(f32[4,32,512]{2,1,0:T(8,128)} %dip.1), calls=%async_computation.2 | async-start | bytes 524288 | tf_op jit(solution)/shard_map/all_to_all | solution.py:505
  69.8 2.0 %traction.1 = (f32[32,512]{1,0:T(8,128)S(1)}, bf16[16,128,512]{2,1,0:T(8,128)(2,1)S(1)}, s32[64,128]{1,0:T(8,128)S(1)}) custom-call(f32[384,128]{1,0:T(8,128)S(1)} %bitcast.12), custom_call_target="tpu_custom_call" | custom-call | tf_op jit(solution)/shard_map/traction/pallas_call | solution.py:456
  71.9 3.8 %all-to-all-done.2.shares = f32[4,32,512]{2,1,0:T(8,128)S(1)} async-done(((f32[4,32,512]{2,1,0:T(8,128)}), f32[4,32,512]{2,1,0:T(8,128)S(1)}, u32[]{:S(2)}, u32[]{:S(2)}) %all-to-all-start.2) | async-done | bytes 262176 | tf_op jit(solution)/shard_map/all_to_all | solution.py:505
  75.7 0.9 owner.1
  76.6 18.0 %all_to_all.21 = f32[128,1,128]{2,1,0:T(1,128)S(1)} all-to-all(f32[128,1,128]{2,1,0:T(1,128)S(1)} %bitcast.18), channel_id=1, replica_groups=mesh['z'=8,'y'=8,'c'=2,'dip'=4] {'z','y','c'}, dimensions={0} | all-to-all | bytes 131072 | tf_op jit(solution)/shard_map/all_to_all | solution.py:473
  94.6 1.3 %back.1 = f32[1,4096]{1,0:T(1,128)} custom-call(s32[1,1]{1,0:T(1,128)S(6)} %copy.23.count, f32[128,128]{1,0:T(8,128)S(1)} %bitcast.15, s32[1,4096]{1,0:T(1,128)S(1)} %get-tuple-element.28.rank, s32[1,4096]{1,0:T(1,128)S(1)} %bitcast.17), custom_call_target="tpu_custom_call" | custom-call | tf_op jit(solution)/shard_map/back/pallas_call | solution.py:456
  (13 shorter events, 0.0 us)
Async XLA Ops:
  1.5 26.9 %copy-start.11 = (s32[1,4096,1]{1,2,0:T(1,128)S(1)}, s32[1,4096,1]{1,2,0:T(1,128)}, u32[]{:S(2)}) copy-start(s32[1,4096,1]{1,2,0:T(1,128)} %param.24) | copy-start | bytes 49156
  1.5 26.9 %copy-start.12 = (s32[1,4096]{1,0:T(1,128)S(1)}, s32[1,4096]{1,0:T(1,128)}, u32[]{:S(2)}) copy-start(s32[1,4096]{1,0:T(1,128)} %node.1) | copy-start | bytes 49156
  1.5 26.9 %copy-start.13 = (f32[1,4096]{1,0:T(1,128)S(1)}, f32[1,4096]{1,0:T(1,128)}, u32[]{:S(2)}) copy-start(f32[1,4096]{1,0:T(1,128)} %value.1) | copy-start | bytes 49156
  1.6 41.4 %copy-start.2 = (bf16[4,128,256]{2,1,0:T(8,128)(2,1)S(1)}, bf16[4,128,256]{2,1,0:T(8,128)(2,1)}, u32[]{:S(2)}) copy-start(bf16[4,128,256]{2,1,0:T(8,128)(2,1)} %constant.25.clone.mem_table) | copy-start | bytes 786436
  1.6 41.4 %copy-start.3 = (bf16[2,256,256]{2,1,0:T(8,128)(2,1)S(1)}, bf16[2,256,256]{2,1,0:T(8,128)(2,1)}, u32[]{:S(2)}) copy-start(bf16[2,256,256]{2,1,0:T(8,128)(2,1)} %constant.24.clone.second_inv) | copy-start | bytes 786436
  1.6 41.4 %copy-start.4 = (bf16[2,256,256]{2,1,0:T(8,128)(2,1)S(1)}, bf16[2,256,256]{2,1,0:T(8,128)(2,1)}, u32[]{:S(2)}) copy-start(bf16[2,256,256]{2,1,0:T(8,128)(2,1)} %constant.23.clone.second) | copy-start | bytes 786436
  1.6 41.4 %copy-start.5 = (f32[2,128,128]{2,1,0:T(8,128)S(1)}, f32[2,128,128]{2,1,0:T(8,128)}, u32[]{:S(2)}) copy-start(f32[2,128,128]{2,1,0:T(8,128)} %constant.22.clone.twiddle) | copy-start | bytes 393220
  1.6 41.4 %copy-start.6 = (bf16[2,128,256]{2,1,0:T(8,128)(2,1)S(1)}, bf16[2,128,256]{2,1,0:T(8,128)(2,1)}, u32[]{:S(2)}) copy-start(bf16[2,128,256]{2,1,0:T(8,128)(2,1)} %constant.21.clone.first_t) | copy-start | bytes 393220
  1.6 41.4 %copy-start.7 = (bf16[2,256,128]{2,1,0:T(8,128)(2,1)S(1)}, bf16[2,256,128]{2,1,0:T(8,128)(2,1)}, u32[]{:S(2)}) copy-start(bf16[2,256,128]{2,1,0:T(8,128)(2,1)} %constant.20.clone.first) | copy-start | bytes 393220
  1.6 6.3 %collective-permute-start = (f32[32,512]{1,0:T(8,128)S(1)}, f32[32,512]{1,0:T(8,128)S(1)}, u32[]{:S(2)}, u32[]{:S(2)}) collective-permute-start(f32[32,512]{1,0:T(8,128)S(1)} %multiply_add_fusion.own), channel_id=1, source_target_pairs={{0,1},{1,0},{2,3},{3,2},{4,5},{5,4},{6,7},{7,6},{8,9},{9,8},{10,11... | collective-permute-start | bytes 196616 | tf_op jit(solution)/shard_map/ppermute | solution.py:482
  9.3 33.6 %all-to-all-start = ((f32[128,4,128]{2,1,0:T(4,128)}), f32[128,4,128]{2,1,0:T(4,128)S(1)}, u32[]{:S(2)}, u32[]{:S(2)}) async-start(f32[128,4,128]{2,1,0:T(4,128)} %bitcast), calls=%async_computation | async-start | bytes 524288 | tf_op jit(solution)/shard_map/all_to_all | solution.py:473
  43.0 32.7 %copy-start = (f32[32,512]{1,0:T(8,128)S(1)}, f32[32,512]{1,0:T(8,128)}, u32[]{:S(2)}) copy-start(f32[32,512]{1,0:T(8,128)} %slip.1) | copy-start | bytes 196612
  43.0 32.6 %copy-start.1 = (f32[32,512]{1,0:T(8,128)S(1)}, f32[32,512]{1,0:T(8,128)}, u32[]{:S(2)}) copy-start(f32[32,512]{1,0:T(8,128)} %rate.1) | copy-start | bytes 196612
  43.0 32.6 %copy-start.8 = (f32[32,512]{1,0:T(8,128)S(1)}, f32[32,512]{1,0:T(8,128)}, u32[]{:S(2)}) copy-start(f32[32,512]{1,0:T(8,128)} %prestress.1) | copy-start | bytes 196612
  43.0 32.6 %copy-start.9 = (f32[32,512]{1,0:T(8,128)S(1)}, f32[32,512]{1,0:T(8,128)}, u32[]{:S(2)}) copy-start(f32[32,512]{1,0:T(8,128)} %normal.1) | copy-start | bytes 196612
  43.0 32.6 %copy-start.10 = (s32[32,512]{1,0:T(8,128)S(1)}, s32[32,512]{1,0:T(8,128)}, u32[]{:S(2)}) copy-start(s32[32,512]{1,0:T(8,128)} %flag.1) | copy-start | bytes 196612
  65.8 9.8 %all-to-all-start.2 = ((f32[4,32,512]{2,1,0:T(8,128)}), f32[4,32,512]{2,1,0:T(8,128)S(1)}, u32[]{:S(2)}, u32[]{:S(2)}) async-start(f32[4,32,512]{2,1,0:T(8,128)} %dip.1), calls=%async_computation.2 | async-start | bytes 524288 | tf_op jit(solution)/shard_map/all_to_all | solution.py:505

commit v7 on v6

--- a/solution.py
+++ b/solution.py
@@ -59,8 +59,7 @@
     cb = np.kron(np.eye(4), np.cos(small))
     sb = np.kron(np.eye(4), np.sin(small))
     second = np.block([[cb, -sb], [sb, cb]])
-    second_inv = np.block([[cb, sb], [-sb, cb]])
-    return np_split(first), np_split(first.T), twiddle, np_split(second), np_split(second_inv)
+    return np_split(first), np_split(first.T), twiddle, np_split(second)
 
 
 def memory_tables():
@@ -90,6 +89,11 @@
     return dot(hi, t_hi) + (dot(lo, t_hi) + dot(hi, t_lo))
 
 
+def dot_data_turned(x, t_hi, t_lo):
+    hi, lo = split(x)
+    return dot(hi, t_hi, NT) + (dot(lo, t_hi, NT) + dot(hi, t_lo, NT))
+
+
 def dot_table_data(t_hi, t_lo, x):
     hi, lo = split(x)
     return dot(t_hi, hi) + (dot(t_hi, lo) + dot(t_lo, hi))
@@ -114,9 +118,9 @@
     return [(turns(0, 4 * q + b), turns(1, 4 * q + b)) for b in range(4)]
 
 
-def interleave():
-    pos = iota((COLS_DEV, COLS_DEV), 1)
-    return (iota((COLS_DEV, COLS_DEV), 0) == 4 * (pos & (PS - 1)) + (pos >> 7)).astype(f32).astype(bf16)
+def interleave(dims):
+    pos = iota((COLS_DEV, COLS_DEV), dims)
+    return (iota((COLS_DEV, COLS_DEV), 1 - dims) == 4 * (pos & (PS - 1)) + (pos >> 7)).astype(f32).astype(bf16)
 
 
 def by_class(x):
@@ -202,7 +206,7 @@
     for copy in far_tables + copies:
         copy.start()
     z_re, z_im = memory_weights(p, q)
-    perm[...] = interleave()
+    perm[...] = interleave(1)
     for copy in far_tables:
         copy.wait()
     sums[...] = dip_forward_part(own[...], perm[...], tables, lambda i, row: turns[i, pl.ds(row, 1), :], q)
@@ -225,7 +229,23 @@
         out[pl.ds(2 + h, PS, stride=SEND), :] = mem[PS * h : PS * (h + 1), :]
 
 
-def strike_part(lines, mems, first, first_t, twiddle, second, second_inv, mem_table, p, q):
+def spectral_factor(p, q):
+    n = PS
+    lane = iota((n, n), 1)
+    fs = signed(rev_bits(iota((n, n), 0)) + PS * (lane & 31), NS)
+    fs = fs * fs
+    parity, slot = lane >> 6, (lane >> 5) & 1
+    factor = []
+    for h in range(2):
+        ell = p + PS * (2 * h + parity)
+        kd = jnp.where(outer_modes(ell, q), jnp.where((ell == 0) & (slot == 1), 2 * COLS_DEV, ell), COLS_DEV + ell)
+        fd = kd.astype(f32) * (1.0 / ND)
+        wave = (2.0 * math.pi) * jnp.sqrt(fs + fd * fd)
+        factor.append((-0.5 * SCALE) * wave)
+    return jnp.concatenate(factor, axis=0)
+
+
+def strike_part(lines, mems, factor, first, first_t, twiddle, second, mem_table, p, q):
     n = PS
     w = []
     for h in range(2):
@@ -241,20 +261,8 @@
         a_re, a_im = a[:n, n * h : n * (h + 1)], a[n:, n * h : n * (h + 1)]
         b.append(jnp.concatenate([a_re * tc + a_im * ts, a_im * tc - a_re * ts], axis=1))
     spec = dot_data_table(jnp.concatenate(b, axis=0), second[0], second[1])
-    lane = iota((n, n), 1)
-    fs = signed(rev_bits(iota((n, n), 0)) + PS * (lane & 31), NS)
-    fs = fs * fs
-    parity, slot = lane >> 6, (lane >> 5) & 1
-    factor = []
-    for h in range(2):
-        ell = p + PS * (2 * h + parity)
-        kd = jnp.where(outer_modes(ell, q), jnp.where((ell == 0) & (slot == 1), 2 * COLS_DEV, ell), COLS_DEV + ell)
-        fd = kd.astype(f32) * (1.0 / ND)
-        wave = (2.0 * math.pi) * jnp.sqrt(fs + fd * fd)
-        wave = (-0.5 * SCALE) * wave
-        factor.append(jnp.concatenate([wave, wave], axis=1))
-    g = jnp.concatenate(factor, axis=0) * (SCALE * spec - w)
-    b = dot_data_table(g, second_inv[0], second_inv[1])
+    g = jnp.concatenate([factor, factor], axis=1) * (SCALE * spec - w)
+    b = dot_data_turned(g, second[0], second[1])
     turned = []
     for h in range(2):
         b_re, b_im = b[n * h : n * (h + 1), :n], b[n * h : n * (h + 1), n:]
@@ -262,15 +270,15 @@
     return dot_table_data(first_t[0], first_t[1], jnp.concatenate(turned, axis=1))
 
 
-def strike_kernel(recv, outbox, first, first_t, twiddle, second, second_inv, mem_table, out):
+def strike_kernel(recv, outbox, factor, first, first_t, twiddle, second, mem_table, out):
     t = strike_part(
         [recv[pl.ds(h, PS, stride=SEND), :] for h in range(2)],
         [recv[pl.ds(2 + h, PS, stride=SEND), :] for h in range(2)],
+        factor[...],
         first,
         first_t,
         twiddle,
         second,
-        second_inv,
         lambda i: mem_table[i],
         *position(),
     )
@@ -307,8 +315,12 @@
     return box, jnp.concatenate(ranks, axis=1)
 
 
-def route_kernel(count, dest, node, value, out, rank):
+def route_kernel(count, tables, dest, node, value, out, rank, perm, turned, factor):
     out[...], rank[...] = route_part(dest[...], node[...], value[...], count[0, 0])
+    perm[...] = interleave(0)
+    for i in range(4):
+        turned[i] = tables[i].astype(f32).T.astype(bf16)
+    factor[...] = spectral_factor(*position())
 
 
 def dip_inverse_part(lines, tables, turns, perm, q):
@@ -340,13 +352,13 @@
         hi, lo = [
             jnp.concatenate([x[i] * keep_even, x[i] * keep_odd, x[i] * flip_even, y[i] * sign], axis=0) for i in range(2)
         ]
-        f = f + (dot(hi, tables[k], NT) + (dot(lo, tables[k], NT) + dot(hi, tables[k + 1], NT)))
+        f = f + (dot(hi, tables[k]) + (dot(lo, tables[k]) + dot(hi, tables[k + 1])))
     f = [f[PS * i : PS * (i + 1)] for i in range(4)]
     f = [f[0] + f[1], f[2] + f[3], f[0] - f[1], f[2] - f[3]]
     rows = 32
     f = jnp.concatenate([jnp.concatenate([x[rows * i : rows * (i + 1)] for i in range(4)], axis=1) for x in f], axis=0)
     hi, lo = split(f)
-    f = dot(hi, perm, NT) + dot(lo, perm, NT)
+    f = dot(hi, perm) + dot(lo, perm)
     return [f[rows * qd : rows * (qd + 1)] for qd in range(QD)]
 
 
@@ -496,12 +508,23 @@
     )
     sent = call(send_kernel, sds((PS * SEND, PS)), (other, mem, sums, perm, tables, turns), "send")
     recv = over_strike(sent, SEND)
-    box, rank = call(
-        route_kernel, (sds((PS, PS)), sds((1, ROWS), jnp.int32)), (), "route", (fe_count,), (dest, row_node, fe_traction)
+    box, rank, perm, turned, factor = call(
+        route_kernel,
+        (
+            sds((PS, PS)),
+            sds((1, ROWS), jnp.int32),
+            sds((COLS_DEV, COLS_DEV), bf16),
+            sds((4, COLS_DEV, COLS_DEV // 4), bf16),
+            sds((2 * PS, PS)),
+        ),
+        (tables,),
+        "route",
+        (fe_count,),
+        (dest, row_node, fe_traction),
     )
-    sent = call(strike_kernel, sds((PS * BACK, PS)), (recv, box), "strike", args=strike)
+    sent = call(strike_kernel, sds((PS * BACK, PS)), (recv, box, factor), "strike", args=strike)
     recv = over_strike(sent, BACK)
-    shares = call(dip_kernel, sds((QD, ROWS_DEV, COLS_DEV)), (recv, perm, tables, turns), "dip")
+    shares = call(dip_kernel, sds((QD, ROWS_DEV, COLS_DEV)), (recv, perm, turned, turns), "dip")
     shares = lax.all_to_all(shares, "dip", 0, 0, tiled=True)
     traction, onehots, spots = call(
         traction_kernel,

time: 96.3 us -> 96.1 us (level)
  no operation moved by 1% of the time
where the time goes in v7:
time: 96.1 us; the launch traced here: 95.7 us
  blocking collectives  37.1 us (39%)
  starting transfers between devices  26.5 us (28%)
  waiting for transfers between devices  16.6 us (17%)
  Pallas kernels  13 us (14%)
  between operations  1.51 us (2%)
    all_to_all x2, blocking collectives, over_strike(): lax.all_to_all(x.reshape(PS * width // unit, unit, PS), STRIKE, 0, 0, til...  37.1 us
    all_to_all x1, starting transfers between devices, over_strike(): lax.all_to_all(x.reshape(PS * width // unit, unit, PS), STRIKE, 0, 0, til...  18.4 us
    pallas_call x8, Pallas kernels, call(): pl.pallas_call(kernel, out_shape=out_shape, in_specs=in_specs, out_specs=...  13 us
    all_to_all x1, waiting for transfers between devices, over_strike(): lax.all_to_all(x.reshape(PS * width // unit, unit, PS), STRIKE, 0, 0, til...  12.9 us
    ppermute x1, starting transfers between devices, body(): other = lax.ppermute(slip_new, 'dip', [(i, i ^ 1) for i in range(QD)])  4.07 us
    all_to_all x1, starting transfers between devices, body(): shares = lax.all_to_all(shares, 'dip', 0, 0, tiled=True)  4.02 us
    all_to_all x1, waiting for transfers between devices, body(): shares = lax.all_to_all(shares, 'dip', 0, 0, tiled=True)  3.78 us
  transfers between devices with their start and end apart: 3, of which 2 were waited for; matrix products, arithmetic and copies ran while one was open for 0% of the time, Pallas kernels for 6%

profile of v7, /device:TPU:1, one launch (start us, length us, event | category | flops | bytes accessed | tf_op | source)
XLA Modules:
  0.0 95.7 jit_solution(10642766160943428349)
XLA Ops:
  0.6 0.9 multiply_add_fusion.own
  1.5 0.0 copy-start.10
  1.5 0.0 copy-start.11
  1.5 0.0 copy-start.12
  1.6 0.0 copy-start.2
  1.6 0.0 copy-start.3
  1.6 0.0 copy-start.4
  1.6 0.0 copy-start.5
  1.6 0.0 copy-start.6
  1.6 4.1 %collective-permute-start = (f32[32,512]{1,0:T(8,128)S(1)}, f32[32,512]{1,0:T(8,128)S(1)}, u32[]{:S(2)}, u32[]{:S(2)}) collective-permute-start(f32[32,512]{1,0:T(8,128)S(1)} %multiply_add_fusion.own), channel_id=1, source_target_pairs={{0,1},{1,0},{2,3},{3,2},{4,5},{5,4},{6,7},{7,6},{8,9},{9,8},{10,11... | collective-permute-start | bytes 196616 | tf_op jit(solution)/shard_map/ppermute | solution.py:494
  5.7 2.2 %near.1 = (f32[256,128]{1,0:T(8,128)S(1)}, f32[256,512]{1,0:T(8,128)S(1)}, bf16[512,512]{1,0:T(8,128)(2,1)S(1)}, bf16[4,128,512]{2,1,0:T(8,128)(2,1)S(1)}, f32[2,16,512]{2,1,0:T(8,128)S(1)}) custom-call(f32[8,2,32,512]{3,2,1,0:T(8,128)} %history_in.1, bf16[4,128,512]{2,1,0:T(8,128)(2,1)} %constant.16.clone.tables_in, f32[2,16,512]{2,1,0:T(8,128)} %constant.17.clone.turns_in, ...), custom_call_target="tpu_custom_call" | custom-call | tf_op jit(solution)/shard_map/near/pallas_call | solution.py:468
  7.9 0.0 collective-permute-done.other
  7.9 1.4 %send.1 = f32[512,128]{1,0:T(8,128)} custom-call(f32[32,512]{1,0:T(8,128)S(1)} %collective-permute-done.other, f32[256,128]{1,0:T(8,128)S(1)} %get-tuple-element.19.mem, f32[256,512]{1,0:T(8,128)S(1)} %get-tuple-element.20.sums, bf16[512,512]{1,0:T(8,128)(2,1)S(1)} %get-tuple-element.21.perm, bf16[4,128,512]{2,1,0:T(8,128)(2,1)S(1)} %get-tuple-element.22.tables, ...), custom_call_target="tpu_custom_call" | custom-call | tf_op jit(solution)/shard_map/send/pallas_call | solution.py:468
  9.3 18.4 %all-to-all-start = ((f32[128,4,128]{2,1,0:T(4,128)}), f32[128,4,128]{2,1,0:T(4,128)S(1)}, u32[]{:S(2)}, u32[]{:S(2)}) async-start(f32[128,4,128]{2,1,0:T(4,128)} %bitcast), calls=%async_computation | async-start | bytes 524288 | tf_op jit(solution)/shard_map/all_to_all | solution.py:485
  28.4 0.0 copy-done.10
  28.4 0.0 copy-done.11
  28.4 1.7 %route.1 = (f32[128,128]{1,0:T(8,128)S(1)}, s32[1,4096]{1,0:T(1,128)S(1)}, bf16[512,512]{1,0:T(8,128)(2,1)S(1)}, bf16[4,512,128]{2,1,0:T(8,128)(2,1)S(1)}, f32[256,128]{1,0:T(8,128)S(1)}) custom-call(s32[1,1]{1,0:T(1,128)S(6)} %copy.22.count, bf16[4,128,512]{2,1,0:T(8,128)(2,1)S(1)} %get-tuple-element.22.tables, s32[1,4096]{1,0:T(1,128)S(1)} %bitcast.17, ...), custom_call_target="tpu_custom_call" | custom-call | tf_op jit(solution)/shard_map/route/pallas_call | solution.py:468
  30.1 12.9 %all-to-all-done = f32[128,4,128]{2,1,0:T(4,128)S(1)} async-done(((f32[128,4,128]{2,1,0:T(4,128)}), f32[128,4,128]{2,1,0:T(4,128)S(1)}, u32[]{:S(2)}, u32[]{:S(2)}) %all-to-all-start) | async-done | bytes 262176 | tf_op jit(solution)/shard_map/all_to_all | solution.py:485
  43.0 0.0 copy-start
  43.0 0.0 copy-start.1
  43.0 0.0 copy-start.7
  43.0 0.0 copy-start.8
  43.0 0.0 copy-start.9
  43.0 1.2 %strike.1 = f32[384,128]{1,0:T(8,128)S(1)} custom-call(f32[512,128]{1,0:T(8,128)S(1)} %bitcast.13, f32[128,128]{1,0:T(8,128)S(1)} %get-tuple-element.24.outbox, f32[256,128]{1,0:T(8,128)S(1)} %get-tuple-element.25.factor, bf16[2,256,128]{2,1,0:T(8,128)(2,1)S(1)} %copy-done.6, bf16[2,128,256]{2,1,0:T(8,128)(2,1)S(1)} %copy-done.5, ...), custom_call_target="tpu_custom_call" | custom-call | tf_op jit(solution)/shard_map/strike/pallas_call | solution.py:468
  44.2 19.0 %all_to_all.20 = f32[384,1,128]{2,1,0:T(1,128)S(1)} all-to-all(f32[384,1,128]{2,1,0:T(1,128)S(1)} %bitcast.14), channel_id=1, replica_groups=mesh['z'=8,'y'=8,'c'=2,'dip'=4] {'z','y','c'}, dimensions={0} | all-to-all | bytes 393216 | tf_op jit(solution)/shard_map/all_to_all | solution.py:485
  63.2 2.3 %dip.1 = f32[4,32,512]{2,1,0:T(8,128)} custom-call(f32[384,128]{1,0:T(8,128)S(1)} %bitcast.11, bf16[512,512]{1,0:T(8,128)(2,1)S(1)} %get-tuple-element.26.perm, bf16[4,512,128]{2,1,0:T(8,128)(2,1)S(1)} %get-tuple-element.27.tables, f32[2,16,512]{2,1,0:T(8,128)S(1)} %get-tuple-element.23.turns), custom_call_target="tpu_custom_call" | custom-call | tf_op jit(solution)/shard_map/dip/pallas_call | solution.py:468
  65.5 4.0 %all-to-all-start.2 = ((f32[4,32,512]{2,1,0:T(8,128)}), f32[4,32,512]{2,1,0:T(8,128)S(1)}, u32[]{:S(2)}, u32[]{:S(2)}) async-start(f32[4,32,512]{2,1,0:T(8,128)} %dip.1), calls=%async_computation.2 | async-start | bytes 524288 | tf_op jit(solution)/shard_map/all_to_all | solution.py:528
  69.5 2.0 %traction.1 = (f32[32,512]{1,0:T(8,128)S(1)}, bf16[16,128,512]{2,1,0:T(8,128)(2,1)S(1)}, s32[64,128]{1,0:T(8,128)S(1)}) custom-call(f32[384,128]{1,0:T(8,128)S(1)} %bitcast.12), custom_call_target="tpu_custom_call" | custom-call | tf_op jit(solution)/shard_map/traction/pallas_call | solution.py:468
  71.5 3.8 %all-to-all-done.2.shares = f32[4,32,512]{2,1,0:T(8,128)S(1)} async-done(((f32[4,32,512]{2,1,0:T(8,128)}), f32[4,32,512]{2,1,0:T(8,128)S(1)}, u32[]{:S(2)}, u32[]{:S(2)}) %all-to-all-start.2) | async-done | bytes 262176 | tf_op jit(solution)/shard_map/all_to_all | solution.py:528
  75.3 0.9 owner.1
  76.2 18.1 %all_to_all.21 = f32[128,1,128]{2,1,0:T(1,128)S(1)} all-to-all(f32[128,1,128]{2,1,0:T(1,128)S(1)} %bitcast.16), channel_id=1, replica_groups=mesh['z'=8,'y'=8,'c'=2,'dip'=4] {'z','y','c'}, dimensions={0} | all-to-all | bytes 131072 | tf_op jit(solution)/shard_map/all_to_all | solution.py:485
  94.4 1.3 %back.1 = f32[1,4096]{1,0:T(1,128)} custom-call(s32[1,1]{1,0:T(1,128)S(6)} %copy.22.count, f32[128,128]{1,0:T(8,128)S(1)} %bitcast.15, s32[1,4096]{1,0:T(1,128)S(1)} %get-tuple-element.34.rank, s32[1,4096]{1,0:T(1,128)S(1)} %bitcast.18), custom_call_target="tpu_custom_call" | custom-call | tf_op jit(solution)/shard_map/back/pallas_call | solution.py:468
  (11 shorter events, 0.0 us)
Async XLA Ops:
  1.5 26.8 %copy-start.10 = (s32[1,4096,1]{1,2,0:T(1,128)S(1)}, s32[1,4096,1]{1,2,0:T(1,128)}, u32[]{:S(2)}) copy-start(s32[1,4096,1]{1,2,0:T(1,128)} %param.23) | copy-start | bytes 49156
  1.5 26.8 %copy-start.11 = (s32[1,4096]{1,0:T(1,128)S(1)}, s32[1,4096]{1,0:T(1,128)}, u32[]{:S(2)}) copy-start(s32[1,4096]{1,0:T(1,128)} %node.1) | copy-start | bytes 49156
  1.5 26.8 %copy-start.12 = (f32[1,4096]{1,0:T(1,128)S(1)}, f32[1,4096]{1,0:T(1,128)}, u32[]{:S(2)}) copy-start(f32[1,4096]{1,0:T(1,128)} %value.1) | copy-start | bytes 49156
  1.6 41.4 %copy-start.2 = (bf16[4,128,256]{2,1,0:T(8,128)(2,1)S(1)}, bf16[4,128,256]{2,1,0:T(8,128)(2,1)}, u32[]{:S(2)}) copy-start(bf16[4,128,256]{2,1,0:T(8,128)(2,1)} %constant.22.clone.mem_table) | copy-start | bytes 786436
  1.6 41.4 %copy-start.3 = (bf16[2,256,256]{2,1,0:T(8,128)(2,1)S(1)}, bf16[2,256,256]{2,1,0:T(8,128)(2,1)}, u32[]{:S(2)}) copy-start(bf16[2,256,256]{2,1,0:T(8,128)(2,1)} %constant.21.clone.second) | copy-start | bytes 786436
  1.6 41.4 %copy-start.4 = (f32[2,128,128]{2,1,0:T(8,128)S(1)}, f32[2,128,128]{2,1,0:T(8,128)}, u32[]{:S(2)}) copy-start(f32[2,128,128]{2,1,0:T(8,128)} %constant.20.clone.twiddle) | copy-start | bytes 393220
  1.6 41.4 %copy-start.5 = (bf16[2,128,256]{2,1,0:T(8,128)(2,1)S(1)}, bf16[2,128,256]{2,1,0:T(8,128)(2,1)}, u32[]{:S(2)}) copy-start(bf16[2,128,256]{2,1,0:T(8,128)(2,1)} %constant.19.clone.first_t) | copy-start | bytes 393220
  1.6 41.4 %copy-start.6 = (bf16[2,256,128]{2,1,0:T(8,128)(2,1)S(1)}, bf16[2,256,128]{2,1,0:T(8,128)(2,1)}, u32[]{:S(2)}) copy-start(bf16[2,256,128]{2,1,0:T(8,128)(2,1)} %constant.18.clone.first) | copy-start | bytes 393220
  1.6 6.3 %collective-permute-start = (f32[32,512]{1,0:T(8,128)S(1)}, f32[32,512]{1,0:T(8,128)S(1)}, u32[]{:S(2)}, u32[]{:S(2)}) collective-permute-start(f32[32,512]{1,0:T(8,128)S(1)} %multiply_add_fusion.own), channel_id=1, source_target_pairs={{0,1},{1,0},{2,3},{3,2},{4,5},{5,4},{6,7},{7,6},{8,9},{9,8},{10,11... | collective-permute-start | bytes 196616 | tf_op jit(solution)/shard_map/ppermute | solution.py:494
  9.3 33.6 %all-to-all-start = ((f32[128,4,128]{2,1,0:T(4,128)}), f32[128,4,128]{2,1,0:T(4,128)S(1)}, u32[]{:S(2)}, u32[]{:S(2)}) async-start(f32[128,4,128]{2,1,0:T(4,128)} %bitcast), calls=%async_computation | async-start | bytes 524288 | tf_op jit(solution)/shard_map/all_to_all | solution.py:485
  43.0 32.3 %copy-start = (f32[32,512]{1,0:T(8,128)S(1)}, f32[32,512]{1,0:T(8,128)}, u32[]{:S(2)}) copy-start(f32[32,512]{1,0:T(8,128)} %slip.1) | copy-start | bytes 196612
  43.0 32.3 %copy-start.1 = (f32[32,512]{1,0:T(8,128)S(1)}, f32[32,512]{1,0:T(8,128)}, u32[]{:S(2)}) copy-start(f32[32,512]{1,0:T(8,128)} %rate.1) | copy-start | bytes 196612
  43.0 32.3 %copy-start.7 = (f32[32,512]{1,0:T(8,128)S(1)}, f32[32,512]{1,0:T(8,128)}, u32[]{:S(2)}) copy-start(f32[32,512]{1,0:T(8,128)} %prestress.1) | copy-start | bytes 196612
  43.0 32.3 %copy-start.8 = (f32[32,512]{1,0:T(8,128)S(1)}, f32[32,512]{1,0:T(8,128)}, u32[]{:S(2)}) copy-start(f32[32,512]{1,0:T(8,128)} %normal.1) | copy-start | bytes 196612
  43.0 32.3 %copy-start.9 = (s32[32,512]{1,0:T(8,128)S(1)}, s32[32,512]{1,0:T(8,128)}, u32[]{:S(2)}) copy-start(s32[32,512]{1,0:T(8,128)} %flag.1) | copy-start | bytes 196612
  65.5 9.8 %all-to-all-start.2 = ((f32[4,32,512]{2,1,0:T(8,128)}), f32[4,32,512]{2,1,0:T(8,128)S(1)}, u32[]{:S(2)}, u32[]{:S(2)}) async-start(f32[4,32,512]{2,1,0:T(8,128)} %dip.1), calls=%async_computation.2 | async-start | bytes 524288 | tf_op jit(solution)/shard_map/all_to_all | solution.py:528

commit v8 on v7

--- a/solution.py
+++ b/solution.py
@@ -323,7 +323,7 @@
     factor[...] = spectral_factor(*position())
 
 
-def dip_inverse_part(lines, tables, turns, perm, q):
+def dip_inverse_part(lines, tables, turns, q):
     lines = [x.T for x in lines]
     t0, t1 = [
         jnp.concatenate([lines[i >> 1][64 * (i & 1) + 32 * slot : 64 * (i & 1) + 32 * slot + 32] for i in range(4)], axis=1)
@@ -358,15 +358,23 @@
     rows = 32
     f = jnp.concatenate([jnp.concatenate([x[rows * i : rows * (i + 1)] for i in range(4)], axis=1) for x in f], axis=0)
     hi, lo = split(f)
-    f = dot(hi, perm) + dot(lo, perm)
-    return [f[rows * qd : rows * (qd + 1)] for qd in range(QD)]
-
-
-def dip_kernel(recv, perm, tables, turns, out):
+    return hi, lo
+
+
+def dip_kernel(recv, perm, tables, turns, out, halves, sems):
     lines = [recv[pl.ds(h, PS, stride=BACK), :] for h in range(2)]
-    shares = dip_inverse_part(lines, tables, lambda i, row: turns[i, row : row + 1, :], perm[...], position()[1])
-    for qd, share in enumerate(shares):
-        out[qd] = share
+    hi, lo = dip_inverse_part(lines, tables, lambda i, row: turns[i, row : row + 1, :], position()[1])
+    half = COLS_DEV // 2
+    copies = []
+    for i in range(2):
+        cols = perm[:, half * i : half * (i + 1)]
+        share = dot(hi, cols) + dot(lo, cols)
+        for qd in range(QD):
+            halves[i, qd] = share[ROWS_DEV * qd : ROWS_DEV * (qd + 1)]
+        copies.append(pltpu.make_async_copy(halves.at[i], out.at[:, :, pl.ds(half * i, half)], sems.at[i]))
+        copies[i].start()
+    for copy in copies:
+        copy.wait()
 
 
 def unpack_rows(fe, roll):
@@ -462,7 +470,7 @@
     spec = pl.BlockSpec(memory_space=pltpu.VMEM)
     hbm = pl.BlockSpec(memory_space=pltpu.HBM)
     in_specs = [pl.BlockSpec(memory_space=pltpu.SMEM)] * len(scalars) + [hbm] * len(far) + [spec] * (len(operands) + len(args))
-    outs = tuple(hbm if i < far_outs else spec for i in range(len(out_shape))) if isinstance(out_shape, tuple) else spec
+    outs = tuple(hbm if i < far_outs else spec for i in range(len(out_shape))) if isinstance(out_shape, tuple) else hbm if far_outs else spec
     far = [pltpu.with_memory_space_constraint(x, pltpu.HBM) for x in far]
     operands = [pltpu.with_memory_space_constraint(x, pltpu.VMEM) for x in operands]
     return pl.pallas_call(
@@ -524,7 +532,14 @@
     )
     sent = call(strike_kernel, sds((PS * BACK, PS)), (recv, box, factor), "strike", args=strike)
     recv = over_strike(sent, BACK)
-    shares = call(dip_kernel, sds((QD, ROWS_DEV, COLS_DEV)), (recv, perm, turned, turns), "dip")
+    shares = call(
+        dip_kernel,
+        jax.ShapeDtypeStruct((QD, *slip.shape), f32),
+        (recv, perm, turned, turns),
+        "dip",
+        far_outs=1,
+        scratch=[sds((2, QD, ROWS_DEV, COLS_DEV // 2)), pltpu.SemaphoreType.DMA((2,))],
+    )
     shares = lax.all_to_all(shares, "dip", 0, 0, tiled=True)
     traction, onehots, spots = call(
         traction_kernel,

time: 96.1 us -> 96.1 us (level)
  no operation moved by 1% of the time
where the time goes in v8:
time: 96.1 us; the launch traced here: 95.7 us
  blocking collectives  37.1 us (39%)
  starting transfers between devices  26.5 us (28%)
  waiting for transfers between devices  16.6 us (17%)
  Pallas kernels  13 us (14%)
  between operations  1.52 us (2%)
    all_to_all x2, blocking collectives, over_strike(): lax.all_to_all(x.reshape(PS * width // unit, unit, PS), STRIKE, 0, 0, til...  37.1 us
    all_to_all x1, starting transfers between devices, over_strike(): lax.all_to_all(x.reshape(PS * width // unit, unit, PS), STRIKE, 0, 0, til...  18.4 us
    pallas_call x8, Pallas kernels, call(): pl.pallas_call(kernel, out_shape=out_shape, in_specs=in_specs, out_specs=...  13 us
    all_to_all x1, waiting for transfers between devices, over_strike(): lax.all_to_all(x.reshape(PS * width // unit, unit, PS), STRIKE, 0, 0, til...  12.9 us
    ppermute x1, starting transfers between devices, body(): other = lax.ppermute(slip_new, 'dip', [(i, i ^ 1) for i in range(QD)])  4.07 us
    all_to_all x1, starting transfers between devices, body(): shares = lax.all_to_all(shares, 'dip', 0, 0, tiled=True)  4.02 us
    all_to_all x1, waiting for transfers between devices, body(): shares = lax.all_to_all(shares, 'dip', 0, 0, tiled=True)  3.78 us
  transfers between devices with their start and end apart: 3, of which 2 were waited for; matrix products, arithmetic and copies ran while one was open for 0% of the time, Pallas kernels for 6%

profile of v8, /device:TPU:1, one launch (start us, length us, event | category | flops | bytes accessed | tf_op | source)
XLA Modules:
  0.0 95.7 jit_solution(9217422581310473878)
XLA Ops:
  0.6 0.9 multiply_add_fusion.own
  1.5 0.0 copy-start.10
  1.5 0.0 copy-start.11
  1.5 0.0 copy-start.12
  1.6 0.0 copy-start.2
  1.6 0.0 copy-start.3
  1.6 0.0 copy-start.4
  1.6 0.0 copy-start.5
  1.6 0.0 copy-start.6
  1.6 4.1 %collective-permute-start = (f32[32,512]{1,0:T(8,128)S(1)}, f32[32,512]{1,0:T(8,128)S(1)}, u32[]{:S(2)}, u32[]{:S(2)}) collective-permute-start(f32[32,512]{1,0:T(8,128)S(1)} %multiply_add_fusion.own), channel_id=1, source_target_pairs={{0,1},{1,0},{2,3},{3,2},{4,5},{5,4},{6,7},{7,6},{8,9},{9,8},{10,11... | collective-permute-start | bytes 196616 | tf_op jit(solution)/shard_map/ppermute | solution.py:502
  5.7 2.2 %near.1 = (f32[256,128]{1,0:T(8,128)S(1)}, f32[256,512]{1,0:T(8,128)S(1)}, bf16[512,512]{1,0:T(8,128)(2,1)S(1)}, bf16[4,128,512]{2,1,0:T(8,128)(2,1)S(1)}, f32[2,16,512]{2,1,0:T(8,128)S(1)}) custom-call(f32[8,2,32,512]{3,2,1,0:T(8,128)} %history_in.1, bf16[4,128,512]{2,1,0:T(8,128)(2,1)} %constant.16.clone.tables_in, f32[2,16,512]{2,1,0:T(8,128)} %constant.17.clone.turns_in, ...), custom_call_target="tpu_custom_call" | custom-call | tf_op jit(solution)/shard_map/near/pallas_call | solution.py:476
  7.9 0.0 collective-permute-done.other
  7.9 1.4 %send.1 = f32[512,128]{1,0:T(8,128)} custom-call(f32[32,512]{1,0:T(8,128)S(1)} %collective-permute-done.other, f32[256,128]{1,0:T(8,128)S(1)} %get-tuple-element.19.mem, f32[256,512]{1,0:T(8,128)S(1)} %get-tuple-element.20.sums, bf16[512,512]{1,0:T(8,128)(2,1)S(1)} %get-tuple-element.21.perm, bf16[4,128,512]{2,1,0:T(8,128)(2,1)S(1)} %get-tuple-element.22.tables, ...), custom_call_target="tpu_custom_call" | custom-call | tf_op jit(solution)/shard_map/send/pallas_call | solution.py:476
  9.3 18.4 %all-to-all-start = ((f32[128,4,128]{2,1,0:T(4,128)}), f32[128,4,128]{2,1,0:T(4,128)S(1)}, u32[]{:S(2)}, u32[]{:S(2)}) async-start(f32[128,4,128]{2,1,0:T(4,128)} %bitcast), calls=%async_computation | async-start | bytes 524288 | tf_op jit(solution)/shard_map/all_to_all | solution.py:493
  28.4 0.0 copy-done.10
  28.4 0.0 copy-done.11
  28.4 1.7 %route.1 = (f32[128,128]{1,0:T(8,128)S(1)}, s32[1,4096]{1,0:T(1,128)S(1)}, bf16[512,512]{1,0:T(8,128)(2,1)S(1)}, bf16[4,512,128]{2,1,0:T(8,128)(2,1)S(1)}, f32[256,128]{1,0:T(8,128)S(1)}) custom-call(s32[1,1]{1,0:T(1,128)S(6)} %copy.22.count, bf16[4,128,512]{2,1,0:T(8,128)(2,1)S(1)} %get-tuple-element.22.tables, s32[1,4096]{1,0:T(1,128)S(1)} %bitcast.17, ...), custom_call_target="tpu_custom_call" | custom-call | tf_op jit(solution)/shard_map/route/pallas_call | solution.py:476
  30.1 12.9 %all-to-all-done = f32[128,4,128]{2,1,0:T(4,128)S(1)} async-done(((f32[128,4,128]{2,1,0:T(4,128)}), f32[128,4,128]{2,1,0:T(4,128)S(1)}, u32[]{:S(2)}, u32[]{:S(2)}) %all-to-all-start) | async-done | bytes 262176 | tf_op jit(solution)/shard_map/all_to_all | solution.py:493
  43.0 0.0 copy-start
  43.0 0.0 copy-start.1
  43.0 0.0 copy-start.7
  43.0 0.0 copy-start.8
  43.0 0.0 copy-start.9
  43.0 1.2 %strike.1 = f32[384,128]{1,0:T(8,128)S(1)} custom-call(f32[512,128]{1,0:T(8,128)S(1)} %bitcast.13, f32[128,128]{1,0:T(8,128)S(1)} %get-tuple-element.24.outbox, f32[256,128]{1,0:T(8,128)S(1)} %get-tuple-element.25.factor, bf16[2,256,128]{2,1,0:T(8,128)(2,1)S(1)} %copy-done.6, bf16[2,128,256]{2,1,0:T(8,128)(2,1)S(1)} %copy-done.5, ...), custom_call_target="tpu_custom_call" | custom-call | tf_op jit(solution)/shard_map/strike/pallas_call | solution.py:476
  44.2 19.0 %all_to_all.20 = f32[384,1,128]{2,1,0:T(1,128)S(1)} all-to-all(f32[384,1,128]{2,1,0:T(1,128)S(1)} %bitcast.14), channel_id=1, replica_groups=mesh['z'=8,'y'=8,'c'=2,'dip'=4] {'z','y','c'}, dimensions={0} | all-to-all | bytes 393216 | tf_op jit(solution)/shard_map/all_to_all | solution.py:493
  63.2 2.3 %dip.1 = f32[4,32,512]{2,1,0:T(8,128)} custom-call(f32[384,128]{1,0:T(8,128)S(1)} %bitcast.11, bf16[512,512]{1,0:T(8,128)(2,1)S(1)} %get-tuple-element.26.perm, bf16[4,512,128]{2,1,0:T(8,128)(2,1)S(1)} %get-tuple-element.27.tables, f32[2,16,512]{2,1,0:T(8,128)S(1)} %get-tuple-element.23.turns), custom_call_target="tpu_custom_call" | custom-call | tf_op jit(solution)/shard_map/dip/pallas_call | solution.py:476
  65.5 4.0 %all-to-all-start.2 = ((f32[4,32,512]{2,1,0:T(8,128)}), f32[4,32,512]{2,1,0:T(8,128)S(1)}, u32[]{:S(2)}, u32[]{:S(2)}) async-start(f32[4,32,512]{2,1,0:T(8,128)} %dip.1), calls=%async_computation.2 | async-start | bytes 524288 | tf_op jit(solution)/shard_map/all_to_all | solution.py:543
  69.5 2.0 %traction.1 = (f32[32,512]{1,0:T(8,128)S(1)}, bf16[16,128,512]{2,1,0:T(8,128)(2,1)S(1)}, s32[64,128]{1,0:T(8,128)S(1)}) custom-call(f32[384,128]{1,0:T(8,128)S(1)} %bitcast.12), custom_call_target="tpu_custom_call" | custom-call | tf_op jit(solution)/shard_map/traction/pallas_call | solution.py:476
  71.5 3.8 %all-to-all-done.2.shares = f32[4,32,512]{2,1,0:T(8,128)S(1)} async-done(((f32[4,32,512]{2,1,0:T(8,128)}), f32[4,32,512]{2,1,0:T(8,128)S(1)}, u32[]{:S(2)}, u32[]{:S(2)}) %all-to-all-start.2) | async-done | bytes 262176 | tf_op jit(solution)/shard_map/all_to_all | solution.py:543
  75.3 0.9 owner.1
  76.2 18.1 %all_to_all.21 = f32[128,1,128]{2,1,0:T(1,128)S(1)} all-to-all(f32[128,1,128]{2,1,0:T(1,128)S(1)} %bitcast.16), channel_id=1, replica_groups=mesh['z'=8,'y'=8,'c'=2,'dip'=4] {'z','y','c'}, dimensions={0} | all-to-all | bytes 131072 | tf_op jit(solution)/shard_map/all_to_all | solution.py:493
  94.4 1.3 %back.1 = f32[1,4096]{1,0:T(1,128)} custom-call(s32[1,1]{1,0:T(1,128)S(6)} %copy.22.count, f32[128,128]{1,0:T(8,128)S(1)} %bitcast.15, s32[1,4096]{1,0:T(1,128)S(1)} %get-tuple-element.34.rank, s32[1,4096]{1,0:T(1,128)S(1)} %bitcast.18), custom_call_target="tpu_custom_call" | custom-call | tf_op jit(solution)/shard_map/back/pallas_call | solution.py:476
  (11 shorter events, 0.0 us)
Async XLA Ops:
  1.5 26.8 %copy-start.10 = (s32[1,4096,1]{1,2,0:T(1,128)S(1)}, s32[1,4096,1]{1,2,0:T(1,128)}, u32[]{:S(2)}) copy-start(s32[1,4096,1]{1,2,0:T(1,128)} %param.23) | copy-start | bytes 49156
  1.5 26.8 %copy-start.11 = (s32[1,4096]{1,0:T(1,128)S(1)}, s32[1,4096]{1,0:T(1,128)}, u32[]{:S(2)}) copy-start(s32[1,4096]{1,0:T(1,128)} %node.1) | copy-start | bytes 49156
  1.5 26.8 %copy-start.12 = (f32[1,4096]{1,0:T(1,128)S(1)}, f32[1,4096]{1,0:T(1,128)}, u32[]{:S(2)}) copy-start(f32[1,4096]{1,0:T(1,128)} %value.1) | copy-start | bytes 49156
  1.6 41.4 %copy-start.2 = (bf16[4,128,256]{2,1,0:T(8,128)(2,1)S(1)}, bf16[4,128,256]{2,1,0:T(8,128)(2,1)}, u32[]{:S(2)}) copy-start(bf16[4,128,256]{2,1,0:T(8,128)(2,1)} %constant.22.clone.mem_table) | copy-start | bytes 786436
  1.6 41.4 %copy-start.3 = (bf16[2,256,256]{2,1,0:T(8,128)(2,1)S(1)}, bf16[2,256,256]{2,1,0:T(8,128)(2,1)}, u32[]{:S(2)}) copy-start(bf16[2,256,256]{2,1,0:T(8,128)(2,1)} %constant.21.clone.second) | copy-start | bytes 786436
  1.6 41.4 %copy-start.4 = (f32[2,128,128]{2,1,0:T(8,128)S(1)}, f32[2,128,128]{2,1,0:T(8,128)}, u32[]{:S(2)}) copy-start(f32[2,128,128]{2,1,0:T(8,128)} %constant.20.clone.twiddle) | copy-start | bytes 393220
  1.6 41.4 %copy-start.5 = (bf16[2,128,256]{2,1,0:T(8,128)(2,1)S(1)}, bf16[2,128,256]{2,1,0:T(8,128)(2,1)}, u32[]{:S(2)}) copy-start(bf16[2,128,256]{2,1,0:T(8,128)(2,1)} %constant.19.clone.first_t) | copy-start | bytes 393220
  1.6 41.4 %copy-start.6 = (bf16[2,256,128]{2,1,0:T(8,128)(2,1)S(1)}, bf16[2,256,128]{2,1,0:T(8,128)(2,1)}, u32[]{:S(2)}) copy-start(bf16[2,256,128]{2,1,0:T(8,128)(2,1)} %constant.18.clone.first) | copy-start | bytes 393220
  1.6 6.3 %collective-permute-start = (f32[32,512]{1,0:T(8,128)S(1)}, f32[32,512]{1,0:T(8,128)S(1)}, u32[]{:S(2)}, u32[]{:S(2)}) collective-permute-start(f32[32,512]{1,0:T(8,128)S(1)} %multiply_add_fusion.own), channel_id=1, source_target_pairs={{0,1},{1,0},{2,3},{3,2},{4,5},{5,4},{6,7},{7,6},{8,9},{9,8},{10,11... | collective-permute-start | bytes 196616 | tf_op jit(solution)/shard_map/ppermute | solution.py:502
  9.3 33.6 %all-to-all-start = ((f32[128,4,128]{2,1,0:T(4,128)}), f32[128,4,128]{2,1,0:T(4,128)S(1)}, u32[]{:S(2)}, u32[]{:S(2)}) async-start(f32[128,4,128]{2,1,0:T(4,128)} %bitcast), calls=%async_computation | async-start | bytes 524288 | tf_op jit(solution)/shard_map/all_to_all | solution.py:493
  43.0 32.3 %copy-start = (f32[32,512]{1,0:T(8,128)S(1)}, f32[32,512]{1,0:T(8,128)}, u32[]{:S(2)}) copy-start(f32[32,512]{1,0:T(8,128)} %slip.1) | copy-start | bytes 196612
  43.0 32.3 %copy-start.1 = (f32[32,512]{1,0:T(8,128)S(1)}, f32[32,512]{1,0:T(8,128)}, u32[]{:S(2)}) copy-start(f32[32,512]{1,0:T(8,128)} %rate.1) | copy-start | bytes 196612
  43.0 32.3 %copy-start.7 = (f32[32,512]{1,0:T(8,128)S(1)}, f32[32,512]{1,0:T(8,128)}, u32[]{:S(2)}) copy-start(f32[32,512]{1,0:T(8,128)} %prestress.1) | copy-start | bytes 196612
  43.0 32.3 %copy-start.8 = (f32[32,512]{1,0:T(8,128)S(1)}, f32[32,512]{1,0:T(8,128)}, u32[]{:S(2)}) copy-start(f32[32,512]{1,0:T(8,128)} %normal.1) | copy-start | bytes 196612
  43.0 32.3 %copy-start.9 = (s32[32,512]{1,0:T(8,128)S(1)}, s32[32,512]{1,0:T(8,128)}, u32[]{:S(2)}) copy-start(s32[32,512]{1,0:T(8,128)} %flag.1) | copy-start | bytes 196612
  65.5 9.8 %all-to-all-start.2 = ((f32[4,32,512]{2,1,0:T(8,128)}), f32[4,32,512]{2,1,0:T(8,128)S(1)}, u32[]{:S(2)}, u32[]{:S(2)}) async-start(f32[4,32,512]{2,1,0:T(8,128)} %dip.1), calls=%async_computation.2 | async-start | bytes 524288 | tf_op jit(solution)/shard_map/all_to_all | solution.py:543

commit v9 on v7

--- a/solution.py
+++ b/solution.py
@@ -442,13 +442,13 @@
 
 
 def return_part(got, dest, rank, count):
-    parts = jnp.concatenate(split(got.T[:CAP]), axis=1)
+    parts = jnp.concatenate(split(got[:, :CAP]), axis=1)
     out = []
     for i in range(ROWS // CHUNK):
         cut = slice(CHUNK * i, CHUNK * (i + 1))
-        onehot = (iota((PS, CHUNK), 0) == dest[:, cut]).astype(f32).astype(bf16)
+        onehot = (iota((CAP, CHUNK), 0) == rank[:, cut]).astype(f32).astype(bf16)
         here = dot(parts, jnp.concatenate([onehot, onehot], axis=0))
-        here = jnp.sum(jnp.where(iota((CAP, CHUNK), 0) == rank[:, cut], here, 0.0), axis=0, keepdims=True)
+        here = jnp.sum(jnp.where(iota((PS, CHUNK), 0) == dest[:, cut], here, 0.0), axis=0, keepdims=True)
         live = (CHUNK * i + iota((1, CHUNK), 1)) < count
         out.append(jnp.where(live, here, 0.0))
     return jnp.concatenate(out, axis=1)

time: 96.1 us -> 95.8 us (level)
  no operation moved by 1% of the time
where the time goes in v9:
time: 95.8 us; the launch traced here: 95.4 us
  blocking collectives  36.9 us (39%)
  starting transfers between devices  26.5 us (28%)
  waiting for transfers between devices  16.6 us (17%)
  Pallas kernels  12.9 us (13%)
  between operations  1.51 us (2%)
    all_to_all x2, blocking collectives, over_strike(): lax.all_to_all(x.reshape(PS * width // unit, unit, PS), STRIKE, 0, 0, til...  36.9 us
    all_to_all x1, starting transfers between devices, over_strike(): lax.all_to_all(x.reshape(PS * width // unit, unit, PS), STRIKE, 0, 0, til...  18.4 us
    pallas_call x8, Pallas kernels, call(): pl.pallas_call(kernel, out_shape=out_shape, in_specs=in_specs, out_specs=...  12.9 us
    all_to_all x1, waiting for transfers between devices, over_strike(): lax.all_to_all(x.reshape(PS * width // unit, unit, PS), STRIKE, 0, 0, til...  12.9 us
    ppermute x1, starting transfers between devices, body(): other = lax.ppermute(slip_new, 'dip', [(i, i ^ 1) for i in range(QD)])  4.07 us
    all_to_all x1, starting transfers between devices, body(): shares = lax.all_to_all(shares, 'dip', 0, 0, tiled=True)  4.01 us
    all_to_all x1, waiting for transfers between devices, body(): shares = lax.all_to_all(shares, 'dip', 0, 0, tiled=True)  3.77 us
  transfers between devices with their start and end apart: 3, of which 2 were waited for; matrix products, arithmetic and copies ran while one was open for 0% of the time, Pallas kernels for 6%

profile of v9, /device:TPU:1, one launch (start us, length us, event | category | flops | bytes accessed | tf_op | source)
XLA Modules:
  0.0 95.4 jit_solution(15882090195354863318)
XLA Ops:
  0.6 0.9 multiply_add_fusion.own
  1.5 0.0 copy-start.10
  1.5 0.0 copy-start.11
  1.5 0.0 copy-start.12
  1.6 0.0 copy-start.2
  1.6 0.0 copy-start.3
  1.6 0.0 copy-start.4
  1.6 0.0 copy-start.5
  1.6 0.0 copy-start.6
  1.6 4.1 %collective-permute-start = (f32[32,512]{1,0:T(8,128)S(1)}, f32[32,512]{1,0:T(8,128)S(1)}, u32[]{:S(2)}, u32[]{:S(2)}) collective-permute-start(f32[32,512]{1,0:T(8,128)S(1)} %multiply_add_fusion.own), channel_id=1, source_target_pairs={{0,1},{1,0},{2,3},{3,2},{4,5},{5,4},{6,7},{7,6},{8,9},{9,8},{10,11... | collective-permute-start | bytes 196616 | tf_op jit(solution)/shard_map/ppermute | solution.py:494
  5.7 2.2 %near.1 = (f32[256,128]{1,0:T(8,128)S(1)}, f32[256,512]{1,0:T(8,128)S(1)}, bf16[512,512]{1,0:T(8,128)(2,1)S(1)}, bf16[4,128,512]{2,1,0:T(8,128)(2,1)S(1)}, f32[2,16,512]{2,1,0:T(8,128)S(1)}) custom-call(f32[8,2,32,512]{3,2,1,0:T(8,128)} %history_in.1, bf16[4,128,512]{2,1,0:T(8,128)(2,1)} %constant.16.clone.tables_in, f32[2,16,512]{2,1,0:T(8,128)} %constant.17.clone.turns_in, ...), custom_call_target="tpu_custom_call" | custom-call | tf_op jit(solution)/shard_map/near/pallas_call | solution.py:468
  7.9 0.0 collective-permute-done.other
  7.9 1.4 %send.1 = f32[512,128]{1,0:T(8,128)} custom-call(f32[32,512]{1,0:T(8,128)S(1)} %collective-permute-done.other, f32[256,128]{1,0:T(8,128)S(1)} %get-tuple-element.19.mem, f32[256,512]{1,0:T(8,128)S(1)} %get-tuple-element.20.sums, bf16[512,512]{1,0:T(8,128)(2,1)S(1)} %get-tuple-element.21.perm, bf16[4,128,512]{2,1,0:T(8,128)(2,1)S(1)} %get-tuple-element.22.tables, ...), custom_call_target="tpu_custom_call" | custom-call | tf_op jit(solution)/shard_map/send/pallas_call | solution.py:468
  9.3 18.4 %all-to-all-start = ((f32[128,4,128]{2,1,0:T(4,128)}), f32[128,4,128]{2,1,0:T(4,128)S(1)}, u32[]{:S(2)}, u32[]{:S(2)}) async-start(f32[128,4,128]{2,1,0:T(4,128)} %bitcast), calls=%async_computation | async-start | bytes 524288 | tf_op jit(solution)/shard_map/all_to_all | solution.py:485
  28.4 0.0 copy-done.10
  28.4 1.7 %route.1 = (f32[128,128]{1,0:T(8,128)S(1)}, s32[1,4096]{1,0:T(1,128)S(1)}, bf16[512,512]{1,0:T(8,128)(2,1)S(1)}, bf16[4,512,128]{2,1,0:T(8,128)(2,1)S(1)}, f32[256,128]{1,0:T(8,128)S(1)}) custom-call(s32[1,1]{1,0:T(1,128)S(6)} %copy.22.count, bf16[4,128,512]{2,1,0:T(8,128)(2,1)S(1)} %get-tuple-element.22.tables, s32[1,4096]{1,0:T(1,128)S(1)} %bitcast.17, ...), custom_call_target="tpu_custom_call" | custom-call | tf_op jit(solution)/shard_map/route/pallas_call | solution.py:468
  30.1 12.9 %all-to-all-done = f32[128,4,128]{2,1,0:T(4,128)S(1)} async-done(((f32[128,4,128]{2,1,0:T(4,128)}), f32[128,4,128]{2,1,0:T(4,128)S(1)}, u32[]{:S(2)}, u32[]{:S(2)}) %all-to-all-start) | async-done | bytes 262176 | tf_op jit(solution)/shard_map/all_to_all | solution.py:485
  43.0 0.0 copy-start
  43.0 0.0 copy-start.1
  43.0 0.0 copy-start.7
  43.0 0.0 copy-start.8
  43.0 0.0 copy-start.9
  43.0 1.2 %strike.1 = f32[384,128]{1,0:T(8,128)S(1)} custom-call(f32[512,128]{1,0:T(8,128)S(1)} %bitcast.13, f32[128,128]{1,0:T(8,128)S(1)} %get-tuple-element.24.outbox, f32[256,128]{1,0:T(8,128)S(1)} %get-tuple-element.25.factor, bf16[2,256,128]{2,1,0:T(8,128)(2,1)S(1)} %copy-done.6, bf16[2,128,256]{2,1,0:T(8,128)(2,1)S(1)} %copy-done.5, ...), custom_call_target="tpu_custom_call" | custom-call | tf_op jit(solution)/shard_map/strike/pallas_call | solution.py:468
  44.2 19.0 %all_to_all.20 = f32[384,1,128]{2,1,0:T(1,128)S(1)} all-to-all(f32[384,1,128]{2,1,0:T(1,128)S(1)} %bitcast.14), channel_id=1, replica_groups=mesh['z'=8,'y'=8,'c'=2,'dip'=4] {'z','y','c'}, dimensions={0} | all-to-all | bytes 393216 | tf_op jit(solution)/shard_map/all_to_all | solution.py:485
  63.2 2.3 %dip.1 = f32[4,32,512]{2,1,0:T(8,128)} custom-call(f32[384,128]{1,0:T(8,128)S(1)} %bitcast.11, bf16[512,512]{1,0:T(8,128)(2,1)S(1)} %get-tuple-element.26.perm, bf16[4,512,128]{2,1,0:T(8,128)(2,1)S(1)} %get-tuple-element.27.tables, f32[2,16,512]{2,1,0:T(8,128)S(1)} %get-tuple-element.23.turns), custom_call_target="tpu_custom_call" | custom-call | tf_op jit(solution)/shard_map/dip/pallas_call | solution.py:468
  65.5 4.0 %all-to-all-start.2 = ((f32[4,32,512]{2,1,0:T(8,128)}), f32[4,32,512]{2,1,0:T(8,128)S(1)}, u32[]{:S(2)}, u32[]{:S(2)}) async-start(f32[4,32,512]{2,1,0:T(8,128)} %dip.1), calls=%async_computation.2 | async-start | bytes 524288 | tf_op jit(solution)/shard_map/all_to_all | solution.py:528
  69.5 2.0 %traction.1 = (f32[32,512]{1,0:T(8,128)S(1)}, bf16[16,128,512]{2,1,0:T(8,128)(2,1)S(1)}, s32[64,128]{1,0:T(8,128)S(1)}) custom-call(f32[384,128]{1,0:T(8,128)S(1)} %bitcast.12), custom_call_target="tpu_custom_call" | custom-call | tf_op jit(solution)/shard_map/traction/pallas_call | solution.py:468
  71.5 3.8 %all-to-all-done.2.shares = f32[4,32,512]{2,1,0:T(8,128)S(1)} async-done(((f32[4,32,512]{2,1,0:T(8,128)}), f32[4,32,512]{2,1,0:T(8,128)S(1)}, u32[]{:S(2)}, u32[]{:S(2)}) %all-to-all-start.2) | async-done | bytes 262176 | tf_op jit(solution)/shard_map/all_to_all | solution.py:528
  75.3 0.0 copy-done.1
  75.3 0.9 owner.1
  76.2 18.0 %all_to_all.21 = f32[128,1,128]{2,1,0:T(1,128)S(1)} all-to-all(f32[128,1,128]{2,1,0:T(1,128)S(1)} %bitcast.16), channel_id=1, replica_groups=mesh['z'=8,'y'=8,'c'=2,'dip'=4] {'z','y','c'}, dimensions={0} | all-to-all | bytes 131072 | tf_op jit(solution)/shard_map/all_to_all | solution.py:485
  94.2 1.2 %back.1 = f32[1,4096]{1,0:T(1,128)} custom-call(s32[1,1]{1,0:T(1,128)S(6)} %copy.22.count, f32[128,128]{1,0:T(8,128)S(1)} %bitcast.15, s32[1,4096]{1,0:T(1,128)S(1)} %get-tuple-element.34.rank, s32[1,4096]{1,0:T(1,128)S(1)} %bitcast.18), custom_call_target="tpu_custom_call" | custom-call | tf_op jit(solution)/shard_map/back/pallas_call | solution.py:468
  (11 shorter events, 0.0 us)
Async XLA Ops:
  1.5 26.8 %copy-start.10 = (s32[1,4096,1]{1,2,0:T(1,128)S(1)}, s32[1,4096,1]{1,2,0:T(1,128)}, u32[]{:S(2)}) copy-start(s32[1,4096,1]{1,2,0:T(1,128)} %param.23) | copy-start | bytes 49156
  1.5 26.8 %copy-start.11 = (s32[1,4096]{1,0:T(1,128)S(1)}, s32[1,4096]{1,0:T(1,128)}, u32[]{:S(2)}) copy-start(s32[1,4096]{1,0:T(1,128)} %node.1) | copy-start | bytes 49156
  1.5 26.8 %copy-start.12 = (f32[1,4096]{1,0:T(1,128)S(1)}, f32[1,4096]{1,0:T(1,128)}, u32[]{:S(2)}) copy-start(f32[1,4096]{1,0:T(1,128)} %value.1) | copy-start | bytes 49156
  1.6 41.4 %copy-start.2 = (bf16[4,128,256]{2,1,0:T(8,128)(2,1)S(1)}, bf16[4,128,256]{2,1,0:T(8,128)(2,1)}, u32[]{:S(2)}) copy-start(bf16[4,128,256]{2,1,0:T(8,128)(2,1)} %constant.22.clone.mem_table) | copy-start | bytes 786436
  1.6 41.4 %copy-start.3 = (bf16[2,256,256]{2,1,0:T(8,128)(2,1)S(1)}, bf16[2,256,256]{2,1,0:T(8,128)(2,1)}, u32[]{:S(2)}) copy-start(bf16[2,256,256]{2,1,0:T(8,128)(2,1)} %constant.21.clone.second) | copy-start | bytes 786436
  1.6 41.4 %copy-start.4 = (f32[2,128,128]{2,1,0:T(8,128)S(1)}, f32[2,128,128]{2,1,0:T(8,128)}, u32[]{:S(2)}) copy-start(f32[2,128,128]{2,1,0:T(8,128)} %constant.20.clone.twiddle) | copy-start | bytes 393220
  1.6 41.4 %copy-start.5 = (bf16[2,128,256]{2,1,0:T(8,128)(2,1)S(1)}, bf16[2,128,256]{2,1,0:T(8,128)(2,1)}, u32[]{:S(2)}) copy-start(bf16[2,128,256]{2,1,0:T(8,128)(2,1)} %constant.19.clone.first_t) | copy-start | bytes 393220
  1.6 41.4 %copy-start.6 = (bf16[2,256,128]{2,1,0:T(8,128)(2,1)S(1)}, bf16[2,256,128]{2,1,0:T(8,128)(2,1)}, u32[]{:S(2)}) copy-start(bf16[2,256,128]{2,1,0:T(8,128)(2,1)} %constant.18.clone.first) | copy-start | bytes 393220
  1.6 6.3 %collective-permute-start = (f32[32,512]{1,0:T(8,128)S(1)}, f32[32,512]{1,0:T(8,128)S(1)}, u32[]{:S(2)}, u32[]{:S(2)}) collective-permute-start(f32[32,512]{1,0:T(8,128)S(1)} %multiply_add_fusion.own), channel_id=1, source_target_pairs={{0,1},{1,0},{2,3},{3,2},{4,5},{5,4},{6,7},{7,6},{8,9},{9,8},{10,11... | collective-permute-start | bytes 196616 | tf_op jit(solution)/shard_map/ppermute | solution.py:494
  9.3 33.6 %all-to-all-start = ((f32[128,4,128]{2,1,0:T(4,128)}), f32[128,4,128]{2,1,0:T(4,128)S(1)}, u32[]{:S(2)}, u32[]{:S(2)}) async-start(f32[128,4,128]{2,1,0:T(4,128)} %bitcast), calls=%async_computation | async-start | bytes 524288 | tf_op jit(solution)/shard_map/all_to_all | solution.py:485
  43.0 32.3 %copy-start = (f32[32,512]{1,0:T(8,128)S(1)}, f32[32,512]{1,0:T(8,128)}, u32[]{:S(2)}) copy-start(f32[32,512]{1,0:T(8,128)} %slip.1) | copy-start | bytes 196612
  43.0 32.3 %copy-start.1 = (f32[32,512]{1,0:T(8,128)S(1)}, f32[32,512]{1,0:T(8,128)}, u32[]{:S(2)}) copy-start(f32[32,512]{1,0:T(8,128)} %rate.1) | copy-start | bytes 196612
  43.0 32.3 %copy-start.7 = (f32[32,512]{1,0:T(8,128)S(1)}, f32[32,512]{1,0:T(8,128)}, u32[]{:S(2)}) copy-start(f32[32,512]{1,0:T(8,128)} %prestress.1) | copy-start | bytes 196612
  43.0 32.3 %copy-start.8 = (f32[32,512]{1,0:T(8,128)S(1)}, f32[32,512]{1,0:T(8,128)}, u32[]{:S(2)}) copy-start(f32[32,512]{1,0:T(8,128)} %normal.1) | copy-start | bytes 196612
  43.0 32.3 %copy-start.9 = (s32[32,512]{1,0:T(8,128)S(1)}, s32[32,512]{1,0:T(8,128)}, u32[]{:S(2)}) copy-start(s32[32,512]{1,0:T(8,128)} %flag.1) | copy-start | bytes 196612
  65.5 9.8 %all-to-all-start.2 = ((f32[4,32,512]{2,1,0:T(8,128)}), f32[4,32,512]{2,1,0:T(8,128)S(1)}, u32[]{:S(2)}, u32[]{:S(2)}) async-start(f32[4,32,512]{2,1,0:T(8,128)} %dip.1), calls=%async_computation.2 | async-start | bytes 524288 | tf_op jit(solution)/shard_map/all_to_all | solution.py:528
